TPU v7x, 128 devices: a whole 4x4x4 slice. The times are simulated.
128 devices in a mesh: seq: 8 (over x, core), head: 16 (over z, y).
Axes of the slice: x: 4, y: 4, z: 4, core: 2. Of those that a mesh axis runs over, the one named last changes fastest.
Arguments:
- moe_input: bfloat16 [16384, 1536], P(('seq', 'head')), may hold values from -6 to 6
- out_grad: bfloat16 [16384, 1536], P(('seq', 'head')), may hold values from -6 to 6
- route_ids: int32 [16384, 6], P(('seq', 'head')), may hold values from 0 to 63, all different within a row; in each aligned block of 128 rows (0 to 127, 128 to 255, ...) at most 16 rows name the same one
- route_gates: float32 [16384, 6], P(('seq', 'head')), may hold values from 0.05 to 0.35
- gate_halves: bfloat16 [128, 1536, 256], P(('seq', 'head')), may hold values from -0.15625 to 0.15625
- up_halves: bfloat16 [128, 1536, 256], P(('seq', 'head')), may hold values from -0.15625 to 0.15625
- down_halves: bfloat16 [128, 256, 1536], P(('seq', 'head')), may hold values from -0.25 to 0.25
- out_proj: bfloat16 [3072, 1536], P('head'), may hold values from -0.109375 to 0.109375
- ssd_x: float32 [16384, 3072], P('seq', 'head'), may hold values from -0.125 to 0.125
- b_proj: float32 [16384, 128], P('seq'), may hold values from -0.5 to 0.5
- c_proj: float32 [16384, 128], P('seq'), may hold values from -0.5 to 0.5
- log_decay: float32 [48, 16384], P('head', 'seq'), may hold values from -2.3 to 0, as said below
- skip_gain: float32 [48], P('head'), may hold values from 0.5 to 1.5
Outputs:
- resid_grad: bfloat16 [16384, 1536], P(('seq', 'head'))
- ssd_x_grad: float32 [16384, 3072], P('seq', 'head')
- b_grad: float32 [16384, 128], P(('seq', 'head'))
Inputs may be any that keep to these rules, and one draw needn't show every extreme that they name: `route_ids`: each row names 6 different experts; the 128 rows of one device name any one expert at most 16 times, a bound that some block reaches. `log_decay`: negative.
All inputs are finite; a program needn't handle non-finite values.
Results may differ from a plain program's by a relative error of at most 0.0039.
Values may be sent and summed in bfloat16 or wider, within the bound.
No kernel may reach another device: no remote copies, remote signals or barrier semaphores. Data moves between devices by JAX's collectives and lax.ppermute only.
A program may use at most 128 MiB of HBM per device.

v0:
```python
import functools

import jax
import jax.numpy as jnp
from jax import lax
from jax.experimental import pallas as pl
from jax.experimental.pallas import tpu as pltpu
from jax.sharding import PartitionSpec as P


BLOCK = 256
SLOTS = 8
F32 = jnp.float32
BF16 = jnp.bfloat16
HIGHEST = lax.Precision.HIGHEST
NT = (((1,), (1,)), ((), ()))
NN = (((1,), (0,)), ((), ()))


def params(limit=67043328):
    return pltpu.CompilerParams(vmem_limit_bytes=limit)


def cost(flops, bytes_accessed):
    return pl.CostEstimate(flops=int(flops), bytes_accessed=int(bytes_accessed), transcendentals=0)


def split(a):
    hi = a.astype(BF16)
    return hi, (a - hi.astype(F32)).astype(BF16)


def dot(a, b, dims):
    return lax.dot_general(a, b, dims, preferred_element_type=F32)


def dot_high(a, b, dims):
    return lax.dot_general(a, b, dims, precision=HIGHEST, preferred_element_type=F32)


def slot_experts(rows, toks):
    row = lax.broadcasted_iota(jnp.int32, (rows, toks), 0)
    dev, slot = row >> 3, row & 7
    x, core, z, y = dev >> 5, (dev >> 4) & 1, (dev >> 2) & 3, dev & 3
    expert = (2 * x + (y & 1)) * 8 + 2 * z + (y >> 1)
    return expert, 2 * slot + core


def select_kernel(ids_ref, rows_ref, sel_ref, out_ref):
    slots, toks = sel_ref.shape
    expert, rank = slot_experts(slots, toks)
    named = ids_ref[0:1, :] == expert
    for k in range(1, ids_ref.shape[0]):
        named = jnp.logical_or(named, ids_ref[k : k + 1, :] == expert)
    named = jnp.where(named, 1.0, 0.0)
    earlier = jnp.where(
        lax.broadcasted_iota(jnp.int32, (toks, toks), 0)
        < lax.broadcasted_iota(jnp.int32, (toks, toks), 1),
        1.0,
        0.0,
    )
    before = dot(named.astype(BF16), earlier.astype(BF16), NN)
    sel = jnp.where(before == rank.astype(F32), named, 0.0).astype(BF16)
    sel_ref[...] = sel
    out_ref[...] = dot(sel, rows_ref[...], NN).astype(BF16)


def second_kernel(ids_ref, gates_ref, sel_ref, rows_ref, out_ref, hi_ref, lo_ref):
    slots, toks = sel_ref.shape
    out_ref[...] = dot(sel_ref[...], rows_ref[...], NN).astype(BF16)
    expert, _ = slot_experts(slots, toks)
    gate = jnp.zeros((slots, toks), F32)
    for k in range(ids_ref.shape[0]):
        gate = jnp.where(ids_ref[k : k + 1, :] == expert, gates_ref[k : k + 1, :], gate)
    mix = (gate * sel_ref[...].astype(F32)).T
    hi, lo = split(mix)
    hi_ref[...] = hi
    lo_ref[...] = lo


def weights_kernel(home_ref, *refs):
    own, far, (cat_ref, cat_t_ref, down_t_ref), bufs, sem = refs[:6], refs[6:12], refs[12:15], refs[15:17], refs[17]
    half = bufs[0].shape[0]

    def copies(sources):
        targets = [cat_ref.at[:, pl.ds(k * half, half)] for k in range(4)] + list(bufs)
        return [
            pltpu.make_async_copy(s.at[0], t, sem.at[k]) for k, (s, t) in enumerate(zip(sources, targets))
        ]

    @pl.when(home_ref[0] == 1)
    def _():
        for c in copies(own):
            c.start()

    @pl.when(home_ref[0] == 0)
    def _():
        for c in copies(far):
            c.start()

    for k, c in enumerate(copies(own)):
        c.wait()
        if k < 4:
            cat_t_ref[k * half : (k + 1) * half, :] = cat_ref[:, k * half : (k + 1) * half].T
        else:
            down_t_ref[:, (k - 4) * half : (k - 3) * half] = bufs[k - 4][...].T


def acts_kernel(x_ref, w_ref, out_ref):
    act = dot(x_ref[...], w_ref[...], NN)
    hidden = act.shape[1] // 2
    gate, up = act[:, :hidden], act[:, hidden:]
    sig = jax.nn.sigmoid(gate)
    out_ref[:, :hidden] = up * sig * (1.0 + gate * (1.0 - sig))
    out_ref[:, hidden:] = gate * sig


def back_kernel(g_ref, act_ref, down_ref, cat_ref, out_ref, down_buf, cat_buf, sem):
    first = pl.program_id(0) == 0
    down_copy = pltpu.make_async_copy(down_ref, down_buf, sem.at[0])
    cat_copy = pltpu.make_async_copy(cat_ref, cat_buf, sem.at[1])

    @pl.when(first)
    def _():
        down_copy.start()
        cat_copy.start()
        down_copy.wait()

    grad = dot(g_ref[...], down_buf[...], NN)
    hidden = grad.shape[1]
    both = jnp.concatenate(
        [(grad * act_ref[:, :hidden]).astype(BF16), (grad * act_ref[:, hidden:]).astype(BF16)], axis=1
    )

    @pl.when(first)
    def _():
        cat_copy.wait()

    out_ref[...] = dot(both, cat_buf[...], NN).astype(BF16)


def combine_kernel(hi_ref, lo_ref, rows_ref, grad_ref, out_ref):
    rows = rows_ref[...]
    total = dot(hi_ref[...], rows, NN) + dot(lo_ref[...], rows, NN)
    out_ref[...] = (grad_ref[...].astype(F32) + total).astype(BF16)


def project_kernel(place_ref, own_ref, other_ref, near_ref, up_ref, far_a_ref, far_b_ref, dn_ref, out_ref, toks_ref, buf_ref, sem):
    core, z, y = place_ref[0], place_ref[1], place_ref[2]
    rows = near_ref.shape[0]
    copies = []
    at = 0
    for k, source in enumerate((near_ref, up_ref, far_a_ref, far_b_ref, dn_ref)):
        n = source.shape[0]
        copies.append(pltpu.make_async_copy(source, buf_ref.at[pl.ds(at, n)], sem.at[k]))
        at += n
    for c in copies:
        c.start()
    toks = own_ref.shape[0]
    toks_ref[pl.ds(pl.multiple_of(core * toks, toks), toks), :] = own_ref[...]
    toks_ref[pl.ds(pl.multiple_of((1 - core) * toks, toks), toks), :] = other_ref[...]
    both = toks_ref[...]
    part = out_ref.shape[2]
    waits = ((0,), (1,), (2, 3), (4,))
    for k, dz in enumerate((0, 3, 2, 1)):
        for w in waits[k]:
            copies[w].wait()
        g = dot(buf_ref[k * rows : (k + 1) * rows, :], both, NT).astype(BF16)
        for q, dy in enumerate((0, 3, 2, 1)):
            head = ((z + dz) & 3) * 4 + ((y + dy) & 3)
            for c in range(2):
                out_ref[c, head] = g[q * part : (q + 1) * part, c * toks : (c + 1) * toks]


def block_grads(g_ref, k):
    pieces = []
    for j in (2 * k, 2 * k + 1):
        pieces.append(jnp.concatenate([g_ref[0, j], g_ref[1, j]], axis=0))
    return jnp.concatenate(pieces, axis=1)


def head_rows(rows, heads, dim):
    n = rows.shape[1]
    return jnp.concatenate([jnp.broadcast_to(rows[h : h + 1, :], (dim, n)) for h in range(heads)], axis=0)


def prepare_kernel(
    d_ref, b_ref, c_ref, x_ref, wh_ref, wl_ref, ts_ref, te_ref, tt_ref, xh_ref, xl_ref, eh_ref, el_ref, th_ref, tl_ref,
    bs_ref, tot_ref,
):
    heads, n = d_ref.shape
    dim = x_ref.shape[0] // heads
    row = lax.broadcasted_iota(jnp.int32, (n, n), 0)
    col = lax.broadcasted_iota(jnp.int32, (n, n), 1)
    tri = jnp.where(col <= row, 1.0, 0.0)
    d = jnp.concatenate([d_ref[...], jnp.zeros((8 - heads, n), F32)], axis=0)
    across = dot_high(d, tri, NT)
    down = dot_high(tri, d, NT)
    scores = dot_high(b_ref[...], c_ref[...], NT)
    later = col >= row
    for h in range(heads):
        gap = across[h : h + 1, :] - down[:, h : h + 1]
        w = jnp.where(later, jnp.exp(jnp.where(later, gap, 0.0)), 0.0) * scores
        wh_ref[0, h], wl_ref[0, h] = split(w)

    @pl.when(pl.program_id(0) == 0)
    def _():
        tot_ref[...] = jnp.zeros_like(tot_ref)

    last = across[:, n - 1 : n]
    te = jnp.exp(last - across)
    tt = jnp.exp(last - across + tot_ref[:, 0:1])
    ts_ref[...] = jnp.exp(across)
    te_ref[...] = te
    tt_ref[...] = tt
    x = x_ref[...]
    xh_ref[...], xl_ref[...] = split(x.T)
    eh_ref[...], el_ref[...] = split((x * head_rows(te, heads, dim)).T)
    th_ref[...], tl_ref[...] = split((x * head_rows(tt, heads, dim)).T)
    block_sum = jnp.broadcast_to(last, tot_ref.shape)
    bs_ref[0] = block_sum
    tot_ref[...] = tot_ref[...] + block_sum


def state_kernel(heads, g_ref, c_ref, ts_ref, bs_ref, tot_ref, fut_ref, pay_ref):
    blocks, rows, lanes = fut_ref.shape
    dim = rows // heads
    n = c_ref.shape[0] // blocks
    states = []
    for k in range(blocks):
        at = slice(k * n, (k + 1) * n)
        g = block_grads(g_ref, k).astype(F32)
        ghi, glo = split(g * head_rows(ts_ref[:, at], heads, dim))
        chi, clo = split(c_ref[at, :])
        states.append(dot(ghi, chi, NN) + dot(ghi, clo, NN) + dot(glo, chi, NN))
    carry = jnp.zeros((rows, lanes), F32)
    for k in reversed(range(blocks)):
        fut_ref[k] = carry
        carry = head_rows(jnp.exp(bs_ref[k]), heads, dim) * carry + states[k]
    first = tot_ref[...]
    hi, _ = split(first)
    mid, low = split(first - hi.astype(F32))
    sent = jnp.concatenate([carry.astype(BF16), hi, mid, low, low], axis=0)
    for j in range(pay_ref.shape[0]):
        pay_ref[j] = sent


def intra_kernel(
    heads, skip_ref, wh_ref, wl_ref, g_ref, xh_ref, xl_ref, eh_ref, el_ref, te_ref, b_ref, c_ref, fut_ref, gx_ref, pb_ref
):
    n = wh_ref.shape[2]
    rows = gx_ref.shape[0]
    dim = rows // heads
    for k in range(wh_ref.shape[0]):
        at = slice(k * n, (k + 1) * n)
        fhi, flo = split(fut_ref[k])
        bhi, blo = split(b_ref[at, :])
        cross = dot(fhi, bhi, NT) + dot(flo, bhi, NT) + dot(fhi, blo, NT)
        cross = cross * head_rows(te_ref[:, at], heads, dim)
        acc = None
        grads = block_grads(g_ref, k)
        for h in range(heads):
            w = wh_ref[k, h]
            cols = slice(h * dim, (h + 1) * dim)
            g = grads[cols]
            gx_ref[cols, at] = dot(g, w, NT) + cross[cols] + skip_ref[h] * g.astype(F32)
            inner = dot(xh_ref[at, cols], g, NN) + dot(xl_ref[at, cols], g, NN)
            term = (w.astype(F32) + wl_ref[k, h].astype(F32)) * inner
            acc = term if acc is None else acc + term
        ahi, alo = split(acc)
        chi, clo = split(c_ref[at, :])
        eh = eh_ref[at, :]
        pb_ref[at, :] = (
            dot(ahi, chi, NN)
            + dot(alo, chi, NN)
            + dot(ahi, clo, NN)
            + dot(eh, fhi, NN)
            + dot(eh, flo, NN)
            + dot(el_ref[at, :], fhi, NN)
        )


def finish_b_kernel(heads, seq_ref, pay_ref, th_ref, tl_ref, pb_ref, out_ref, hi_ref, lo_ref):
    rows, lanes = hi_ref.shape
    dim = rows // heads

    @pl.when(pl.program_id(0) == 0)
    def _():
        place = seq_ref[0]
        acc = jnp.zeros((rows, lanes), F32)
        log = jnp.zeros((8, lanes), F32)
        for j in range(pay_ref.shape[0]):
            ahead = j > place
            factor = jnp.where(ahead, jnp.exp(log), 0.0)
            acc = acc + head_rows(factor, heads, dim) * pay_ref[j, 0:rows, :].astype(F32)
            tots = pay_ref[j, rows : rows + 32, :].astype(F32)
            log = log + jnp.where(ahead, tots[0:8] + tots[8:16] + tots[16:24], 0.0)
        hi_ref[...], lo_ref[...] = split(acc)

    hi = hi_ref[...]
    th = th_ref[...]
    total = pb_ref[...] + dot(th, hi, NN) + dot(th, lo_ref[...], NN) + dot(tl_ref[...], hi, NN)
    out_ref[...] = total.astype(out_ref.dtype)


def finish_x_kernel(heads, hi_ref, lo_ref, tt_ref, b_ref, gx_ref, out_ref):
    bhi, blo = split(b_ref[...])
    hi = hi_ref[...]
    tt = head_rows(tt_ref[...], heads, out_ref.shape[0] // heads)
    out_ref[...] = gx_ref[...] + tt * (dot(hi, bhi, NT) + dot(lo_ref[...], bhi, NT) + dot(hi, blo, NT))


def whole(shape):
    zeros = (0,) * len(shape)
    return pl.BlockSpec(shape, lambda *_: zeros)


def shards(
    moe_input,
    out_grad,
    route_ids,
    route_gates,
    gate_halves,
    up_halves,
    down_halves,
    out_proj,
    ssd_x,
    b_proj,
    c_proj,
    log_decay,
    skip_gain,
):
    sds = jax.ShapeDtypeStruct
    toks, width = moe_input.shape
    seq_axes = ("x", "core")
    n_seq, n_head = lax.axis_size(seq_axes), lax.axis_size("head")
    devices = n_seq * n_head
    slots = devices * SLOTS
    both = ("x", "core", "head")
    smem_spec = pl.BlockSpec(memory_space=pltpu.SMEM)
    any_spec = pl.BlockSpec(memory_space=pl.ANY)
    heads = skip_gain.shape[0]
    inner = out_proj.shape[0]
    seq_rows, state = b_proj.shape
    blocks = seq_rows // BLOCK
    seq, head = lax.axis_index(seq_axes), lax.axis_index("head")
    core = lax.axis_index("core")

    home = core == (head & 1)
    over_y, over_core = [], []
    for s in range(n_seq):
        for h in range(n_head):
            if (s & 1) != (h & 1):
                over_y.append((s * n_head + h, s * n_head + (h ^ 1)))
            else:
                over_core.append((s * n_head + h, (s ^ 1) * n_head + h))
    halves = (gate_halves, up_halves, down_halves)
    y_halves, far_own = [], []
    for a in halves:
        y_halves.append(lax.ppermute(a, both, over_y))
    for a in halves:
        far_own.append(lax.ppermute(a, both, over_core))
    far_y = [lax.ppermute(a, both, over_core) for a in y_halves]
    own = [a for o, y in zip(halves, y_halves) for a in (o, y)]
    far = [a for o, y in zip(far_own, far_y) for a in (o, y)]
    _, width, half = gate_halves.shape
    hidden = 2 * half
    expert_cat, expert_cat_t, expert_down_t = pl.pallas_call(
        weights_kernel,
        in_specs=[smem_spec] + [any_spec] * 12,
        out_shape=(sds((width, 2 * hidden), BF16), sds((2 * hidden, width), BF16), sds((width, hidden), BF16)),
        scratch_shapes=[pltpu.VMEM((half, width), BF16)] * 2 + [pltpu.SemaphoreType.DMA((6,))],
        compiler_params=params(),
        cost_estimate=cost(1e9, 12 << 20),
        name="expert_weights",
    )(home.astype(jnp.int32).reshape(1), *own, *far)

    ids_t, gates_t = route_ids.T, route_gates.T
    sel, send_input = pl.pallas_call(
        select_kernel,
        out_shape=(sds((slots, toks), BF16), sds((slots, width), BF16)),
        compiler_params=params(),
        cost_estimate=cost(2 * slots * toks * width, 4 << 20),
        name="select_rows",
    )(ids_t, moe_input)
    send_grad, mix_hi, mix_lo = pl.pallas_call(
        second_kernel,
        out_shape=(sds((slots, width), BF16), sds((toks, slots), BF16), sds((toks, slots), BF16)),
        compiler_params=params(),
        cost_estimate=cost(2 * slots * toks * width, 4 << 20),
        name="select_grads",
    )(ids_t, gates_t, sel, out_grad)

    def exchange(rows):
        shaped = rows.reshape(devices, SLOTS, width)
        return lax.all_to_all(shaped, both, split_axis=0, concat_axis=0, tiled=True).reshape(slots, width)

    recv_input = exchange(send_input)
    recv_grad = exchange(send_grad)

    part = inner // 2

    def shift(rows, dz, dy):
        pairs = [(z * 4 + y, (z + dz) % 4 * 4 + (y + dy) % 4) for z in range(4) for y in range(4)]
        return lax.ppermute(rows, "head", pairs)

    near = lax.dynamic_slice(out_proj, (core * part, 0), (part, width))
    up, dn = shift(near, 0, 1), shift(near, 0, -1)
    far_up = shift(up[: part // 2], 0, 1)
    far_dn = shift(dn[part // 2 :], 0, -1)
    line = jnp.concatenate([near, up, far_up, far_dn, dn], axis=0)
    z_up, z_dn = shift(line, 1, 0), shift(line, -1, 0)
    z_far_up = shift(z_up[: 2 * part], 1, 0)
    z_far_dn = shift(z_dn[2 * part :], -1, 0)

    flip = lambda i: blocks - 1 - i
    row_in = pl.BlockSpec((inner, BLOCK), lambda i: (0, flip(i)))
    tok_in = pl.BlockSpec((BLOCK, inner), lambda i: (flip(i), 0))
    tok_st = pl.BlockSpec((BLOCK, state), lambda i: (flip(i), 0))
    row_8 = pl.BlockSpec((8, BLOCK), lambda i: (0, flip(i)))
    blk_st = pl.BlockSpec((1, inner, state), lambda i: (flip(i), 0, 0))
    blk_8 = pl.BlockSpec((1, 8, state), lambda i: (flip(i), 0, 0))
    blk_w = pl.BlockSpec((1, heads, BLOCK, BLOCK), lambda i: (flip(i), 0, 0, 0))
    x_shape = sds((seq_rows, inner), BF16)
    w_shape = sds((blocks, heads, BLOCK, BLOCK), BF16)
    r_shape = sds((8, seq_rows), F32)
    w_hi, w_lo, to_start, to_end, to_last, x_hi, x_lo, e_hi, e_lo, t_hi, t_lo, block_sum, total = pl.pallas_call(
        prepare_kernel,
        grid=(blocks,),
        in_specs=[pl.BlockSpec((heads, BLOCK), lambda i: (0, flip(i))), tok_st, tok_st, row_in],
        out_specs=(blk_w,) * 2 + (row_8,) * 3 + (tok_in,) * 6 + (blk_8, whole((8, state))),
        out_shape=(w_shape,) * 2
        + (r_shape,) * 3
        + (x_shape,) * 6
        + (sds((blocks, 8, state), F32), sds((8, state), F32)),
        compiler_params=params(),
        cost_estimate=cost(4e9, 20 << 20),
        name="scan_prepare",
    )(log_decay, b_proj, c_proj, ssd_x.T)

    tile = 256
    row_spec = pl.BlockSpec((tile, width), lambda i: (i, 0))
    act_spec = pl.BlockSpec((tile, 2 * hidden), lambda i: (i, 0))
    factors = pl.pallas_call(
        acts_kernel,
        grid=(slots // tile,),
        in_specs=[row_spec, whole((width, 2 * hidden))],
        out_specs=act_spec,
        out_shape=sds((slots, 2 * hidden), F32),
        compiler_params=params(),
        cost_estimate=cost(4 * slots * width * hidden, 10 << 20),
        name="expert_acts",
    )(recv_input, expert_cat)
    expert_rows = pl.pallas_call(
        back_kernel,
        grid=(slots // tile,),
        in_specs=[row_spec, act_spec, any_spec, any_spec],
        out_specs=row_spec,
        out_shape=sds((slots, width), BF16),
        scratch_shapes=[
            pltpu.VMEM((width, hidden), BF16),
            pltpu.VMEM((2 * hidden, width), BF16),
            pltpu.SemaphoreType.DMA((2,)),
        ],
        compiler_params=params(),
        cost_estimate=cost(6 * slots * width * hidden, 14 << 20),
        name="expert_back",
    )(recv_grad, factors, expert_down_t, expert_cat_t)
    returned = exchange(expert_rows)

    resid_grad = pl.pallas_call(
        combine_kernel,
        out_shape=sds((toks, width), BF16),
        compiler_params=params(),
        cost_estimate=cost(4 * slots * toks * width, 4 << 20),
        name="combine_rows",
    )(mix_hi, mix_lo, returned, out_grad)
    resid_other = lax.ppermute(resid_grad, "core", [(0, 1), (1, 0)])
    grad_all = pl.pallas_call(
        project_kernel,
        grid=(1,),
        in_specs=[smem_spec] + [whole((toks, width))] * 2 + [any_spec] * 5,
        out_specs=whole((2, n_head, part, toks)),
        out_shape=sds((2, n_head, part, toks), BF16),
        scratch_shapes=[
            pltpu.VMEM((2 * toks, width), BF16),
            pltpu.VMEM((n_head * part, width), BF16),
            pltpu.SemaphoreType.DMA((5,)),
        ],
        compiler_params=params(),
        cost_estimate=cost(4 * n_head * part * toks * width, 7 << 20),
        name="project_rows",
    )(jnp.stack([core, head >> 2, head & 3]), resid_grad, resid_other, line, z_up, z_far_up, z_far_dn, z_dn)
    grads = lax.all_to_all(
        grad_all.reshape(2 * n_head, part, toks), ("core", "head"), split_axis=0, concat_axis=0, tiled=True
    ).reshape(2, n_head, part, toks)

    pay_rows = inner + 32
    future, payload = pl.pallas_call(
        functools.partial(state_kernel, heads),
        out_shape=(sds((blocks, inner, state), F32), sds((n_seq, pay_rows, state), BF16)),
        grid=(1,),
        in_specs=[
            whole((2, n_head, part, toks)),
            whole((seq_rows, state)),
            whole((8, seq_rows)),
            whole((blocks, 8, state)),
            whole((8, state)),
        ],
        out_specs=(whole((blocks, inner, state)), whole((n_seq, pay_rows, state))),
        compiler_params=params(),
        cost_estimate=cost(1e9, 4 << 20),
        name="scan_state",
    )(grads, c_proj, to_start, block_sum, total)
    pays = lax.all_to_all(payload, seq_axes, split_axis=0, concat_axis=0, tiled=True)
    pair = 2
    spec = lambda *shape: pl.BlockSpec(shape, lambda i: (i,) + (0,) * (len(shape) - 1))
    cols = lambda *shape: pl.BlockSpec(shape, lambda i: (0, i))
    tok_in2, tok_st2 = spec(pair * BLOCK, inner), spec(pair * BLOCK, state)
    row_in2, row_82 = cols(inner, pair * BLOCK), cols(8, pair * BLOCK)
    w_spec = spec(pair, heads, BLOCK, BLOCK)
    part_x, part_b = pl.pallas_call(
        functools.partial(intra_kernel, heads),
        grid=(blocks // pair,),
        in_specs=[smem_spec, w_spec, w_spec, pl.BlockSpec((2, pair * BLOCK // toks, part, toks), lambda i: (0, i, 0, 0))]
        + [tok_in2] * 4
        + [row_82, tok_st2, tok_st2, spec(pair, inner, state)],
        out_specs=(row_in2, tok_st2),
        out_shape=(sds((inner, seq_rows), F32), sds((seq_rows, state), F32)),
        compiler_params=params(),
        cost_estimate=cost(4e9, 16 << 20),
        name="scan_intra",
    )(skip_gain, w_hi, w_lo, grads, x_hi, x_lo, e_hi, e_lo, to_end, b_proj, c_proj, future)
    partial_b, in_hi, in_lo = pl.pallas_call(
        functools.partial(finish_b_kernel, heads),
        grid=(blocks // pair,),
        in_specs=[smem_spec, whole((n_seq, pay_rows, state)), tok_in2, tok_in2, tok_st2],
        out_specs=(tok_st2, whole((inner, state)), whole((inner, state))),
        out_shape=(sds((seq_rows, state), BF16), sds((inner, state), BF16), sds((inner, state), BF16)),
        compiler_params=params(),
        cost_estimate=cost(4e8, 6 << 20),
        name="scan_finish_b",
    )(seq.reshape(1), pays, t_hi, t_lo, part_b)
    shares = lax.all_to_all(
        partial_b.reshape(n_head, seq_rows // n_head, state), "head", split_axis=0, concat_axis=0, tiled=True
    )
    grad_x = pl.pallas_call(
        functools.partial(finish_x_kernel, heads),
        grid=(blocks // pair,),
        in_specs=[whole((inner, state)), whole((inner, state)), row_82, tok_st2, row_in2],
        out_specs=row_in2,
        out_shape=sds((inner, seq_rows), F32),
        compiler_params=params(),
        cost_estimate=cost(4e8, 6 << 20),
        name="scan_finish_x",
    )(in_hi, in_lo, to_last, b_proj, part_x)
    b_grad = jnp.sum(shares.astype(F32), axis=0)
    return (resid_grad, grad_x.T, b_grad)


def solution(mesh):
    n_seq, n_head = mesh.shape["seq"], mesh.shape["head"]
    fine = jax.sharding.Mesh(mesh.devices.reshape(n_seq // 2, 2, n_head), ("x", "core", "head"))

    seq, every = ("x", "core"), ("x", "core", "head")
    return jax.shard_map(
        shards,
        mesh=fine,
        in_specs=(
            P(every, None),
            P(every, None),
            P(every, None),
            P(every, None),
            P(every, None, None),
            P(every, None, None),
            P(every, None, None),
            P("head", None),
            P(seq, "head"),
            P(seq, None),
            P(seq, None),
            P("head", seq),
            P("head"),
        ),
        out_specs=(P(every, None), P(seq, "head"), P(every, None)),
        check_vma=False,
    )
```

profile of v0, /device:TPU:0, one launch (start us, length us, event | category | flops | bytes accessed | tf_op | source)
XLA Modules:
  0.0 325.4 jit_solution(16426607329838942212)
XLA Ops:
  0.6 4.1 %select_rows.1 = (bf16[1024,128]{1,0:T(8,128)(2,1)}, bf16[1024,1536]{1,0:T(8,128)(2,1)}) custom-call(s32[6,128]{1,0:T(8,128)} %bitcast.25, bf16[128,1536]{1,0:T(8,128)(2,1)} %rows_ref.2), custom_call_target="tpu_custom_call" | custom-call | flops 402653184 | bytes 4194304 | tf_op jit(solution)/shard_map/select_rows/pallas_call | solution.py:379
  4.8 11.6 %all-to-all-start.1 = ((bf16[128,8,1536]{2,1,0:T(8,128)(2,1)}), bf16[128,8,1536]{2,1,0:T(8,128)(2,1)}, u32[]{:S(2)}, u32[]{:S(2)}) async-start(bf16[128,8,1536]{2,1,0:T(8,128)(2,1)} %bitcast.21), calls=%async_computation.1 | async-start | bytes 6291456 | tf_op jit(solution)/shard_map/all_to_all | solution.py:396
  16.4 4.1 %select_grads.1 = (bf16[1024,1536]{1,0:T(8,128)(2,1)}, bf16[128,1024]{1,0:T(8,128)(2,1)}, bf16[128,1024]{1,0:T(8,128)(2,1)}) custom-call(s32[6,128]{1,0:T(8,128)} %bitcast.26, f32[6,128]{1,0:T(8,128)} %bitcast.27, bf16[1024,128]{1,0:T(8,128)(2,1)} %get-tuple-element.31.sel_ref, bf16[128,1536]{1,0:T(8,128)(2,1)} %grad_ref.1), custom_call_target="tpu_custom_call" | custom-call | flops 402653184 | bytes 4194304 | tf_op jit(solution)/shard_map/select_grads/pallas_call | solution.py:386
  20.5 35.9 %all-to-all-done.1 = bf16[128,8,1536]{2,1,0:T(8,128)(2,1)} async-done(((bf16[128,8,1536]{2,1,0:T(8,128)(2,1)}), bf16[128,8,1536]{2,1,0:T(8,128)(2,1)}, u32[]{:S(2)}, u32[]{:S(2)}) %all-to-all-start.1) | async-done | bytes 3145760 | tf_op jit(solution)/shard_map/all_to_all | solution.py:396
  56.4 5.9 %all-to-all-start = ((bf16[128,8,1536]{2,1,0:T(8,128)(2,1)}), bf16[128,8,1536]{2,1,0:T(8,128)(2,1)}, u32[]{:S(2)}, u32[]{:S(2)}) async-start(bf16[128,8,1536]{2,1,0:T(8,128)(2,1)} %bitcast.19), calls=%async_computation | async-start | bytes 6291456 | tf_op jit(solution)/shard_map/all_to_all | solution.py:396
  63.6 3.3 %collective-permute-start.3 = (bf16[1,1536,256]{2,1,0:T(8,128)(2,1)S(1)}, bf16[1,1536,256]{2,1,0:T(8,128)(2,1)S(1)}, u32[]{:S(2)}, u32[]{:S(2)}) collective-permute-start(bf16[1,1536,256]{2,1,0:T(8,128)(2,1)S(1)} %copy-done.3), channel_id=1, source_target_pairs={{0,16},{2,18},{4,20},{6,22},{8,24},{10,26},{12,28},{14,30},{17,1},... | collective-permute-start | bytes 2359304 | tf_op jit(solution)/shard_map/ppermute | solution.py:362
  69.5 6.8 %collective-permute-start.5 = (bf16[1,1536,256]{2,1,0:T(8,128)(2,1)S(1)}, bf16[1,1536,256]{2,1,0:T(8,128)(2,1)}, u32[]{:S(2)}, u32[]{:S(2)}) collective-permute-start(bf16[1,1536,256]{2,1,0:T(8,128)(2,1)S(1)} %copy-done.4), channel_id=1, source_target_pairs={{0,16},{2,18},{4,20},{6,22},{8,24},{10,26},{12,28},{14,30},{17,1},... | collective-permute-start | bytes 2359304 | tf_op jit(solution)/shard_map/ppermute | solution.py:362
  76.3 28.9 %collective-permute-done.refs_1_ = bf16[1,1536,256]{2,1,0:T(8,128)(2,1)S(1)} collective-permute-done((bf16[1,1536,256]{2,1,0:T(8,128)(2,1)S(1)}, bf16[1,1536,256]{2,1,0:T(8,128)(2,1)S(1)}, u32[]{:S(2)}, u32[]{:S(2)}) %collective-permute-start) | collective-permute-done | bytes 786464 | tf_op jit(solution)/shard_map/ppermute | solution.py:360
  108.8 5.0 %collective-permute-done.1.refs_3_ = bf16[1,1536,256]{2,1,0:T(8,128)(2,1)} collective-permute-done((bf16[1,1536,256]{2,1,0:T(8,128)(2,1)S(1)}, bf16[1,1536,256]{2,1,0:T(8,128)(2,1)}, u32[]{:S(2)}, u32[]{:S(2)}) %collective-permute-start.1) | collective-permute-done | bytes 786464 | tf_op jit(solution)/shard_map/ppermute | solution.py:360
  115.9 6.3 %collective-permute-done.2.refs_5_ = bf16[1,256,1536]{2,1,0:T(8,128)(2,1)} collective-permute-done((bf16[1,256,1536]{2,1,0:T(8,128)(2,1)S(1)}, bf16[1,256,1536]{2,1,0:T(8,128)(2,1)}, u32[]{:S(2)}, u32[]{:S(2)}) %collective-permute-start.2) | collective-permute-done | bytes 786464 | tf_op jit(solution)/shard_map/ppermute | solution.py:360
  125.7 5.7 %expert_weights.1 = (bf16[1536,1024]{1,0:T(8,128)(2,1)}, bf16[1024,1536]{1,0:T(8,128)(2,1)}, bf16[1536,512]{1,0:T(8,128)(2,1)}) custom-call(s32[1]{0:T(128)} %bitcast.6.home_ref, bf16[1,1536,256]{2,1,0:T(8,128)(2,1)} %refs_0_.1, bf16[1,1536,256]{2,1,0:T(8,128)(2,1)} %copy-done.6, bf16[1,1536,256]{2,1,0:T(8,128)(2,1)} %refs_2_.1, ...), custom_call_target="tpu_custom_call" | custom-call | flops 1000000000 | bytes 12582912 | tf_op jit(solution)/shard_map/expert_weights/pallas_call | solution.py:368
  131.4 7.8 %expert_acts.1.act_ref = f32[1024,1024]{1,0:T(8,128)} custom-call(bf16[1024,1536]{1,0:T(8,128)(2,1)} %bitcast.5.x_ref, bf16[1536,1024]{1,0:T(8,128)(2,1)} %get-tuple-element.36.w_ref), custom_call_target="tpu_custom_call" | custom-call | flops 3221225472 | bytes 10485760 | tf_op jit(solution)/shard_map/expert_acts/pallas_call | solution.py:444
  139.2 10.8 %expert_back.1 = bf16[1024,1536]{1,0:T(8,128)(2,1)} custom-call(bf16[1024,1536]{1,0:T(8,128)(2,1)} %bitcast.3.g_ref, f32[1024,1024]{1,0:T(8,128)} %expert_acts.1.act_ref, bf16[1536,512]{1,0:T(8,128)(2,1)} %get-tuple-element.37.down_ref, bf16[1024,1536]{1,0:T(8,128)(2,1)} %get-tuple-element.38.cat_ref), custom_call_target="tpu_custom_call" | custom-call | flops 4831838208 | bytes 14680064 | tf_op jit(solution)/shard_map/expert_back/pallas_call | solution.py:454
  150.0 10.5 %all-to-all-start.2 = ((bf16[128,8,1536]{2,1,0:T(8,128)(2,1)}), bf16[128,8,1536]{2,1,0:T(8,128)(2,1)}, u32[]{:S(2)}, u32[]{:S(2)}) async-start(bf16[128,8,1536]{2,1,0:T(8,128)(2,1)} %bitcast.20), calls=%async_computation.2 | async-start | bytes 6291456 | tf_op jit(solution)/shard_map/all_to_all | solution.py:396
  162.9 38.7 %collective-permute-done.12 = bf16[96,1536]{1,0:T(8,128)(2,1)S(1)} collective-permute-done((bf16[96,1536]{1,0:T(8,128)(2,1)S(1)}, bf16[96,1536]{1,0:T(8,128)(2,1)S(1)}, u32[]{:S(2)}, u32[]{:S(2)}) %collective-permute-start.12) | collective-permute-done | bytes 294944 | tf_op jit(solution)/shard_map/ppermute | solution.py:405
  203.8 5.7 %collective-permute-done.11 = bf16[48,1536]{1,0:T(8,128)(2,1)S(1)} collective-permute-done((bf16[48,1536]{1,0:T(8,128)(2,1)S(1)}, bf16[48,1536]{1,0:T(8,128)(2,1)S(1)}, u32[]{:S(2)}, u32[]{:S(2)}) %collective-permute-start.11) | collective-permute-done | bytes 147488 | tf_op jit(solution)/shard_map/ppermute | solution.py:405
  209.6 3.7 %collective-permute-start.16 = (bf16[384,1536]{1,0:T(8,128)(2,1)S(1)}, bf16[384,1536]{1,0:T(8,128)(2,1)S(1)}, u32[]{:S(2)}, u32[]{:S(2)}) collective-permute-start(bf16[384,1536]{1,0:T(8,128)(2,1)S(1)} %constant_dynamic-update-slice_fusion.near_ref), channel_id=1, source_target_pairs={{0,12},{1,13},{2,14},{3,15},{4,0},{5,1},{6,2},{7,3},{8,4},{9,5},{1... | collective-permute-start | bytes 3538952 | tf_op jit(solution)/shard_map/ppermute | solution.py:405
  213.3 24.1 %collective-permute-done.16.dn_ref = bf16[384,1536]{1,0:T(8,128)(2,1)S(1)} collective-permute-done((bf16[384,1536]{1,0:T(8,128)(2,1)S(1)}, bf16[384,1536]{1,0:T(8,128)(2,1)S(1)}, u32[]{:S(2)}, u32[]{:S(2)}) %collective-permute-start.16) | collective-permute-done | bytes 1179680 | tf_op jit(solution)/shard_map/ppermute | solution.py:405
  238.3 3.7 %collective-permute-start.17 = (bf16[192,1536]{1,0:T(8,128)(2,1)}, bf16[192,1536]{1,0:T(8,128)(2,1)}, u32[]{:S(2)}, u32[]{:S(2)}) collective-permute-start(bf16[192,1536]{1,0:T(8,128)(2,1)} %slice.19), channel_id=1, source_target_pairs={{0,12},{1,13},{2,14},{3,15},{4,0},{5,1},{6,2},{7,3},{8,4},{9,5},{1... | collective-permute-start | bytes 1769480 | tf_op jit(solution)/shard_map/ppermute | solution.py:405
  244.0 3.8 %combine_rows.1.own_ref = bf16[128,1536]{1,0:T(8,128)(2,1)} custom-call(bf16[128,1024]{1,0:T(8,128)(2,1)} %get-tuple-element.32.hi_ref, bf16[128,1024]{1,0:T(8,128)(2,1)} %get-tuple-element.33.lo_ref, bf16[1024,1536]{1,0:T(8,128)(2,1)} %bitcast.8.rows_ref, bf16[128,1536]{1,0:T(8,128)(2,1)} %grad_ref.1), custom_call_target="tpu_custom_call" | custom-call | flops 805306368 | bytes 4194304 | tf_op jit(solution)/shard_map/combine_rows/pallas_call | solution.py:471
  248.4 4.5 %collective-permute-done.17.far_b_ref = bf16[192,1536]{1,0:T(8,128)(2,1)} collective-permute-done((bf16[192,1536]{1,0:T(8,128)(2,1)}, bf16[192,1536]{1,0:T(8,128)(2,1)}, u32[]{:S(2)}, u32[]{:S(2)}) %collective-permute-start.17) | collective-permute-done | bytes 589856 | tf_op jit(solution)/shard_map/ppermute | solution.py:405
  252.9 5.3 %collective-permute-done.15.far_a_ref = bf16[192,1536]{1,0:T(8,128)(2,1)} collective-permute-done((bf16[192,1536]{1,0:T(8,128)(2,1)}, bf16[192,1536]{1,0:T(8,128)(2,1)}, u32[]{:S(2)}, u32[]{:S(2)}) %collective-permute-start.15) | collective-permute-done | bytes 589856 | tf_op jit(solution)/shard_map/ppermute | solution.py:405
  258.3 6.5 %project_rows.1 = bf16[2,16,96,128]{3,2,1,0:T(8,128)(2,1)} custom-call(s32[3]{0:T(128)} %pad_add_fusion.place_ref, bf16[128,1536]{1,0:T(8,128)(2,1)} %combine_rows.1.own_ref, bf16[128,1536]{1,0:T(8,128)(2,1)} %collective-permute-done.9.other_ref, bf16[384,1536]{1,0:T(8,128)(2,1)} %copy-done.2, bf16[384,1536]{1,0:T(8,128)(2,1)} %copy-done.1, ...), custom_call_target="tpu_custom_call" | custom-call | flops 1207959552 | bytes 7340032 | tf_op jit(solution)/shard_map/project_rows/pallas_call | solution.py:479
  264.8 4.6 %all-to-all-start.3 = ((bf16[32,96,128]{2,1,0:T(8,128)(2,1)}), bf16[32,96,128]{2,1,0:T(8,128)(2,1)}, u32[]{:S(2)}, u32[]{:S(2)}) async-start(bf16[32,96,128]{2,1,0:T(8,128)(2,1)} %bitcast.18), calls=%async_computation.3 | async-start | bytes 1572864 | tf_op jit(solution)/shard_map/all_to_all | solution.py:494
  269.4 13.1 %scan_prepare.1 = (bf16[8,3,256,256]{3,2,1,0:T(8,128)(2,1)}, bf16[8,3,256,256]{3,2,1,0:T(8,128)(2,1)}, f32[8,2048]{1,0:T(8,128)}, f32[8,2048]{1,0:T(8,128)}, f32...) custom-call(f32[3,2048]{1,0:T(4,128)} %d_ref.1, ...), custom_call_target="tpu_custom_call" | custom-call | flops 4000000000 | bytes 20971520 | tf_op jit(solution)/shard_map/scan_prepare/pallas_call | solution.py:427
  284.2 3.3 %scan_state.1 = (f32[8,192,128]{2,1,0:T(8,128)}, bf16[8,224,128]{2,1,0:T(8,128)(2,1)}) custom-call(bf16[2,16,96,128]{3,2,1,0:T(8,128)(2,1)} %bitcast.14.g_ref, f32[2048,128]{1,0:T(8,128)} %c_ref.5, f32[8,2048]{1,0:T(8,128)} %get-tuple-element.39.ts_ref, f32[8,8,128]{2,1,0:T(8,128)} %get-tuple-element.40.bs_ref, f32[8,128]{1,0:T(8,128)} %get-tuple-element.41.tot_ref), custom_call_target="tpu_custom_call" | custom-call | flops 1000000000 | bytes 4194304 | tf_op jit(solution)/shard_map/scan_state/pallas_call | solution.py:499
  287.5 4.4 %all-to-all-start.4 = ((bf16[8,224,128]{2,1,0:T(8,128)(2,1)}), bf16[8,224,128]{2,1,0:T(8,128)(2,1)}, u32[]{:S(2)}, u32[]{:S(2)}) async-start(bf16[8,224,128]{2,1,0:T(8,128)(2,1)} %get-tuple-element.42), calls=%async_computation.4 | async-start | bytes 917504 | tf_op jit(solution)/shard_map/all_to_all | solution.py:515
  291.8 9.5 %scan_intra.1 = (f32[192,2048]{1,0:T(8,128)}, f32[2048,128]{1,0:T(8,128)}) custom-call(f32[3]{0:T(128)} %skip_ref.1, bf16[8,3,256,256]{3,2,1,0:T(8,128)(2,1)} %get-tuple-element.45.wh_ref, bf16[8,3,256,256]{3,2,1,0:T(8,128)(2,1)} %get-tuple-element.46.wl_ref, bf16[2,16,96,128]{3,2,1,0:T(8,128)(2,1)} %bitcast.14.g_ref, ...), custom_call_target="tpu_custom_call" | custom-call | flops 4000000000 | bytes 16777216 | tf_op jit(solution)/shard_map/scan_intra/pallas_call | solution.py:522
  301.5 4.6 %scan_finish_b.1 = (bf16[2048,128]{1,0:T(8,128)(2,1)}, bf16[192,128]{1,0:T(8,128)(2,1)}, bf16[192,128]{1,0:T(8,128)(2,1)}) custom-call(s32[1]{0:T(128)} %bitcast.9.seq_ref, bf16[8,224,128]{2,1,0:T(8,128)(2,1)} %all-to-all-done.4.pay_ref, bf16[2048,192]{1,0:T(8,128)(2,1)} %get-tuple-element.43.th_ref, bf16[2048,192]{1,0:T(8,128)(2,1)} %get-tuple-element.44.tl_ref, ...), custom_call_target="tpu_custom_call" | custom-call | flops 400000000 | bytes 6291456 | tf_op jit(solution)/shard_map/scan_finish_b/pallas_call | solution.py:534
  306.2 5.5 %all-to-all-start.5 = ((bf16[16,128,128]{2,1,0:T(8,128)(2,1)}), bf16[16,128,128]{2,1,0:T(8,128)(2,1)}, u32[]{:S(2)}, u32[]{:S(2)}) async-start(bf16[16,128,128]{2,1,0:T(8,128)(2,1)} %bitcast.23), calls=%async_computation.5 | async-start | bytes 1048576 | tf_op jit(solution)/shard_map/all_to_all | solution.py:544
  311.7 4.4 %scan_finish_x.1 = f32[192,2048]{1,0:T(8,128)} custom-call(bf16[192,128]{1,0:T(8,128)(2,1)} %get-tuple-element.54.hi_ref, bf16[192,128]{1,0:T(8,128)(2,1)} %get-tuple-element.55.lo_ref, f32[8,2048]{1,0:T(8,128)} %get-tuple-element.56.tt_ref, f32[2048,128]{1,0:T(8,128)} %b_ref.5, f32[192,2048]{1,0:T(8,128)} %get-tuple-element.57.gx_ref), custom_call_target="tpu_custom_call" | custom-call | flops 400000000 | bytes 6291456 | tf_op jit(solution)/shard_map/scan_finish_x/pallas_call | solution.py:547
  316.0 7.7 %all-to-all-done.5 = bf16[16,128,128]{2,1,0:T(8,128)(2,1)} async-done(((bf16[16,128,128]{2,1,0:T(8,128)(2,1)}), bf16[16,128,128]{2,1,0:T(8,128)(2,1)}, u32[]{:S(2)}, u32[]{:S(2)}) %all-to-all-start.5) | async-done | bytes 524320 | tf_op jit(solution)/shard_map/all_to_all | solution.py:544
  (59 shorter events, 24.7 us)
Async XLA Ops:
  4.8 51.7 %all-to-all-start.1 = ((bf16[128,8,1536]{2,1,0:T(8,128)(2,1)}), bf16[128,8,1536]{2,1,0:T(8,128)(2,1)}, u32[]{:S(2)}, u32[]{:S(2)}) async-start(bf16[128,8,1536]{2,1,0:T(8,128)(2,1)} %bitcast.21), calls=%async_computation.1 | async-start | bytes 6291456 | tf_op jit(solution)/shard_map/all_to_all | solution.py:396
  56.4 5.9 %copy-start.3 = (bf16[1,1536,256]{2,1,0:T(8,128)(2,1)S(1)}, bf16[1,1536,256]{2,1,0:T(8,128)(2,1)}, u32[]{:S(2)}) copy-start(bf16[1,1536,256]{2,1,0:T(8,128)(2,1)} %refs_0_.1) | copy-start | bytes 2359300
  56.4 10.5 %copy-start.4 = (bf16[1,1536,256]{2,1,0:T(8,128)(2,1)S(1)}, bf16[1,1536,256]{2,1,0:T(8,128)(2,1)}, u32[]{:S(2)}) copy-start(bf16[1,1536,256]{2,1,0:T(8,128)(2,1)} %refs_2_.1) | copy-start | bytes 2359300
  56.4 11.8 %copy-start.5 = (bf16[1,256,1536]{2,1,0:T(8,128)(2,1)S(1)}, bf16[1,256,1536]{2,1,0:T(8,128)(2,1)}, u32[]{:S(2)}) copy-start(bf16[1,256,1536]{2,1,0:T(8,128)(2,1)} %refs_4_.1) | copy-start | bytes 2359300
  56.4 82.8 %all-to-all-start = ((bf16[128,8,1536]{2,1,0:T(8,128)(2,1)}), bf16[128,8,1536]{2,1,0:T(8,128)(2,1)}, u32[]{:S(2)}, u32[]{:S(2)}) async-start(bf16[128,8,1536]{2,1,0:T(8,128)(2,1)} %bitcast.19), calls=%async_computation | async-start | bytes 6291456 | tf_op jit(solution)/shard_map/all_to_all | solution.py:396
  62.3 42.9 %collective-permute-start = (bf16[1,1536,256]{2,1,0:T(8,128)(2,1)S(1)}, bf16[1,1536,256]{2,1,0:T(8,128)(2,1)S(1)}, u32[]{:S(2)}, u32[]{:S(2)}) collective-permute-start(bf16[1,1536,256]{2,1,0:T(8,128)(2,1)S(1)} %copy-done.3), channel_id=1, source_target_pairs={{1,0},{3,2},{5,4},{7,6},{9,8},{11,10},{13,12},{15,14},{16,17},{18,... | collective-permute-start | bytes 2359304 | tf_op jit(solution)/shard_map/ppermute | solution.py:360
  63.6 43.8 %collective-permute-start.3 = (bf16[1,1536,256]{2,1,0:T(8,128)(2,1)S(1)}, bf16[1,1536,256]{2,1,0:T(8,128)(2,1)S(1)}, u32[]{:S(2)}, u32[]{:S(2)}) collective-permute-start(bf16[1,1536,256]{2,1,0:T(8,128)(2,1)S(1)} %copy-done.3), channel_id=1, source_target_pairs={{0,16},{2,18},{4,20},{6,22},{8,24},{10,26},{12,28},{14,30},{17,1},... | collective-permute-start | bytes 2359304 | tf_op jit(solution)/shard_map/ppermute | solution.py:362
  66.9 46.8 %collective-permute-start.1 = (bf16[1,1536,256]{2,1,0:T(8,128)(2,1)S(1)}, bf16[1,1536,256]{2,1,0:T(8,128)(2,1)}, u32[]{:S(2)}, u32[]{:S(2)}) collective-permute-start(bf16[1,1536,256]{2,1,0:T(8,128)(2,1)S(1)} %copy-done.4), channel_id=1, source_target_pairs={{1,0},{3,2},{5,4},{7,6},{9,8},{11,10},{13,12},{15,14},{16,17},{18,... | collective-permute-start | bytes 2359304 | tf_op jit(solution)/shard_map/ppermute | solution.py:360
  68.2 53.9 %collective-permute-start.2 = (bf16[1,256,1536]{2,1,0:T(8,128)(2,1)S(1)}, bf16[1,256,1536]{2,1,0:T(8,128)(2,1)}, u32[]{:S(2)}, u32[]{:S(2)}) collective-permute-start(bf16[1,256,1536]{2,1,0:T(8,128)(2,1)S(1)} %copy-done.5), channel_id=1, source_target_pairs={{1,0},{3,2},{5,4},{7,6},{9,8},{11,10},{13,12},{15,14},{16,17},{18,... | collective-permute-start | bytes 2359304 | tf_op jit(solution)/shard_map/ppermute | solution.py:360
  69.5 54.8 %collective-permute-start.5 = (bf16[1,1536,256]{2,1,0:T(8,128)(2,1)S(1)}, bf16[1,1536,256]{2,1,0:T(8,128)(2,1)}, u32[]{:S(2)}, u32[]{:S(2)}) collective-permute-start(bf16[1,1536,256]{2,1,0:T(8,128)(2,1)S(1)} %copy-done.4), channel_id=1, source_target_pairs={{0,16},{2,18},{4,20},{6,22},{8,24},{10,26},{12,28},{14,30},{17,1},... | collective-permute-start | bytes 2359304 | tf_op jit(solution)/shard_map/ppermute | solution.py:362
  105.2 19.1 %copy-start.6 = (bf16[1,1536,256]{2,1,0:T(8,128)(2,1)}, bf16[1,1536,256]{2,1,0:T(8,128)(2,1)S(1)}, u32[]{:S(2)}) copy-start(bf16[1,1536,256]{2,1,0:T(8,128)(2,1)S(1)} %collective-permute-done.refs_1_) | copy-start | bytes 2359300
  105.2 19.1 %collective-permute-start.7 = (bf16[1,256,1536]{2,1,0:T(8,128)(2,1)S(1)}, bf16[1,256,1536]{2,1,0:T(8,128)(2,1)}, u32[]{:S(2)}, u32[]{:S(2)}) collective-permute-start(bf16[1,256,1536]{2,1,0:T(8,128)(2,1)S(1)} %copy-done.5), channel_id=1, source_target_pairs={{0,16},{2,18},{4,20},{6,22},{8,24},{10,26},{12,28},{14,30},{17,1},... | collective-permute-start | bytes 2359304 | tf_op jit(solution)/shard_map/ppermute | solution.py:362
  107.4 14.8 %copy-start.7 = (bf16[1,1536,256]{2,1,0:T(8,128)(2,1)}, bf16[1,1536,256]{2,1,0:T(8,128)(2,1)S(1)}, u32[]{:S(2)}) copy-start(bf16[1,1536,256]{2,1,0:T(8,128)(2,1)S(1)} %collective-permute-done.3.refs_6_) | copy-start | bytes 2359300
  107.4 16.9 %collective-permute-start.4 = (bf16[1,1536,256]{2,1,0:T(8,128)(2,1)S(1)}, bf16[1,1536,256]{2,1,0:T(8,128)(2,1)S(1)}, u32[]{:S(2)}, u32[]{:S(2)}) collective-permute-start(bf16[1,1536,256]{2,1,0:T(8,128)(2,1)S(1)} %collective-permute-done.refs_1_), channel_id=1, source_target_pairs={{0,16},{2,18},{4,20},{6,22},{8,24},{10,26},{12,28},{14,30},{17,1},... | collective-permute-start | bytes 2359304 | tf_op jit(solution)/shard_map/ppermute | solution.py:363
  113.7 11.5 %collective-permute-start.6 = (bf16[1,1536,256]{2,1,0:T(8,128)(2,1)}, bf16[1,1536,256]{2,1,0:T(8,128)(2,1)}, u32[]{:S(2)}, u32[]{:S(2)}) collective-permute-start(bf16[1,1536,256]{2,1,0:T(8,128)(2,1)} %collective-permute-done.1.refs_3_), channel_id=1, source_target_pairs={{0,16},{2,18},{4,20},{6,22},{8,24},{10,26},{12,28},{14,30},{17,1},... | collective-permute-start | bytes 2359304 | tf_op jit(solution)/shard_map/ppermute | solution.py:363
  122.2 3.5 %collective-permute-start.8 = (bf16[1,256,1536]{2,1,0:T(8,128)(2,1)}, bf16[1,256,1536]{2,1,0:T(8,128)(2,1)}, u32[]{:S(2)}, u32[]{:S(2)}) collective-permute-start(bf16[1,256,1536]{2,1,0:T(8,128)(2,1)} %collective-permute-done.2.refs_5_), channel_id=1, source_target_pairs={{0,16},{2,18},{4,20},{6,22},{8,24},{10,26},{12,28},{14,30},{17,1},... | collective-permute-start | bytes 2359304 | tf_op jit(solution)/shard_map/ppermute | solution.py:363
  150.0 10.6 %copy-start.9 = (bf16[192,1536]{1,0:T(8,128)(2,1)S(1)}, bf16[192,1536]{1,0:T(8,128)(2,1)}, u32[]{:S(2)}) copy-start(bf16[192,1536]{1,0:T(8,128)(2,1)} %param.20) | copy-start | bytes 1769476
  150.0 93.9 %all-to-all-start.2 = ((bf16[128,8,1536]{2,1,0:T(8,128)(2,1)}), bf16[128,8,1536]{2,1,0:T(8,128)(2,1)}, u32[]{:S(2)}, u32[]{:S(2)}) async-start(bf16[128,8,1536]{2,1,0:T(8,128)(2,1)} %bitcast.20), calls=%async_computation.2 | async-start | bytes 6291456 | tf_op jit(solution)/shard_map/all_to_all | solution.py:396
  160.6 40.9 %collective-permute-start.12 = (bf16[96,1536]{1,0:T(8,128)(2,1)S(1)}, bf16[96,1536]{1,0:T(8,128)(2,1)S(1)}, u32[]{:S(2)}, u32[]{:S(2)}) collective-permute-start(bf16[96,1536]{1,0:T(8,128)(2,1)S(1)} %get-tuple-element.60), channel_id=1, source_target_pairs={{0,3},{1,0},{2,1},{3,2},{4,7},{5,4},{6,5},{7,6},{8,11},{9,8},{10,9... | collective-permute-start | bytes 884744 | tf_op jit(solution)/shard_map/ppermute | solution.py:405
  162.9 40.2 %collective-permute-start.10 = (bf16[96,1536]{1,0:T(8,128)(2,1)S(1)}, bf16[96,1536]{1,0:T(8,128)(2,1)S(1)}, u32[]{:S(2)}, u32[]{:S(2)}) collective-permute-start(bf16[96,1536]{1,0:T(8,128)(2,1)S(1)} %get-tuple-element.60), channel_id=1, source_target_pairs={{0,1},{1,2},{2,3},{3,0},{4,5},{5,6},{6,7},{7,4},{8,9},{9,10},{10,1... | collective-permute-start | bytes 884744 | tf_op jit(solution)/shard_map/ppermute | solution.py:405
  201.6 8.0 %collective-permute-start.13 = (bf16[48,1536]{1,0:T(8,128)(2,1)S(1)}, bf16[48,1536]{1,0:T(8,128)(2,1)S(1)}, u32[]{:S(2)}, u32[]{:S(2)}) collective-permute-start(bf16[48,1536]{1,0:T(8,128)(2,1)S(1)} %slice.17), channel_id=1, source_target_pairs={{0,3},{1,0},{2,1},{3,2},{4,7},{5,4},{6,5},{7,6},{8,11},{9,8},{10,9... | collective-permute-start | bytes 442376 | tf_op jit(solution)/shard_map/ppermute | solution.py:405
  203.1 6.4 %collective-permute-start.11 = (bf16[48,1536]{1,0:T(8,128)(2,1)S(1)}, bf16[48,1536]{1,0:T(8,128)(2,1)S(1)}, u32[]{:S(2)}, u32[]{:S(2)}) collective-permute-start(bf16[48,1536]{1,0:T(8,128)(2,1)S(1)} %slice.16), channel_id=1, source_target_pairs={{0,1},{1,2},{2,3},{3,0},{4,5},{5,6},{6,7},{7,4},{8,9},{9,10},{10,1... | collective-permute-start | bytes 442376 | tf_op jit(solution)/shard_map/ppermute | solution.py:405
  209.6 34.4 %copy-start.2 = (bf16[384,1536]{1,0:T(8,128)(2,1)}, bf16[384,1536]{1,0:T(8,128)(2,1)S(1)}, u32[]{:S(2)}) copy-start(bf16[384,1536]{1,0:T(8,128)(2,1)S(1)} %constant_dynamic-update-slice_fusion.near_ref) | copy-start | bytes 3538948
  209.6 27.8 %collective-permute-start.16 = (bf16[384,1536]{1,0:T(8,128)(2,1)S(1)}, bf16[384,1536]{1,0:T(8,128)(2,1)S(1)}, u32[]{:S(2)}, u32[]{:S(2)}) collective-permute-start(bf16[384,1536]{1,0:T(8,128)(2,1)S(1)} %constant_dynamic-update-slice_fusion.near_ref), channel_id=1, source_target_pairs={{0,12},{1,13},{2,14},{3,15},{4,0},{5,1},{6,2},{7,3},{8,4},{9,5},{1... | collective-permute-start | bytes 3538952 | tf_op jit(solution)/shard_map/ppermute | solution.py:405
  213.3 28.7 %collective-permute-start.14 = (bf16[384,1536]{1,0:T(8,128)(2,1)S(1)}, bf16[384,1536]{1,0:T(8,128)(2,1)S(1)}, u32[]{:S(2)}, u32[]{:S(2)}) collective-permute-start(bf16[384,1536]{1,0:T(8,128)(2,1)S(1)} %constant_dynamic-update-slice_fusion.near_ref), channel_id=1, source_target_pairs={{0,4},{1,5},{2,6},{3,7},{4,8},{5,9},{6,10},{7,11},{8,12},{9,13},{1... | collective-permute-start | bytes 3538952 | tf_op jit(solution)/shard_map/ppermute | solution.py:405
  237.4 6.5 %copy-start = (bf16[384,1536]{1,0:T(8,128)(2,1)}, bf16[384,1536]{1,0:T(8,128)(2,1)S(1)}, u32[]{:S(2)}) copy-start(bf16[384,1536]{1,0:T(8,128)(2,1)S(1)} %collective-permute-done.16.dn_ref) | copy-start | bytes 3538948
  238.3 14.6 %collective-permute-start.17 = (bf16[192,1536]{1,0:T(8,128)(2,1)}, bf16[192,1536]{1,0:T(8,128)(2,1)}, u32[]{:S(2)}, u32[]{:S(2)}) collective-permute-start(bf16[192,1536]{1,0:T(8,128)(2,1)} %slice.19), channel_id=1, source_target_pairs={{0,12},{1,13},{2,14},{3,15},{4,0},{5,1},{6,2},{7,3},{8,4},{9,5},{1... | collective-permute-start | bytes 1769480 | tf_op jit(solution)/shard_map/ppermute | solution.py:405
  243.9 14.3 %collective-permute-start.15 = (bf16[192,1536]{1,0:T(8,128)(2,1)}, bf16[192,1536]{1,0:T(8,128)(2,1)}, u32[]{:S(2)}, u32[]{:S(2)}) collective-permute-start(bf16[192,1536]{1,0:T(8,128)(2,1)} %slice.18), channel_id=1, source_target_pairs={{0,4},{1,5},{2,6},{3,7},{4,8},{5,9},{6,10},{7,11},{8,12},{9,13},{1... | collective-permute-start | bytes 1769480 | tf_op jit(solution)/shard_map/ppermute | solution.py:405
  247.8 10.5 %collective-permute-start.9 = (bf16[128,1536]{1,0:T(8,128)(2,1)}, bf16[128,1536]{1,0:T(8,128)(2,1)}, u32[]{:S(2)}, u32[]{:S(2)}) collective-permute-start(bf16[128,1536]{1,0:T(8,128)(2,1)} %combine_rows.1.own_ref), channel_id=1, source_target_pairs={{0,16},{16,0},{1,17},{17,1},{2,18},{18,2},{3,19},{19,3},{4,20},{20... | collective-permute-start | bytes 1179656 | tf_op jit(solution)/shard_map/ppermute | solution.py:478
  264.8 19.4 %all-to-all-start.3 = ((bf16[32,96,128]{2,1,0:T(8,128)(2,1)}), bf16[32,96,128]{2,1,0:T(8,128)(2,1)}, u32[]{:S(2)}, u32[]{:S(2)}) async-start(bf16[32,96,128]{2,1,0:T(8,128)(2,1)} %bitcast.18), calls=%async_computation.3 | async-start | bytes 1572864 | tf_op jit(solution)/shard_map/all_to_all | solution.py:494
  287.5 14.1 %all-to-all-start.4 = ((bf16[8,224,128]{2,1,0:T(8,128)(2,1)}), bf16[8,224,128]{2,1,0:T(8,128)(2,1)}, u32[]{:S(2)}, u32[]{:S(2)}) async-start(bf16[8,224,128]{2,1,0:T(8,128)(2,1)} %get-tuple-element.42), calls=%async_computation.4 | async-start | bytes 917504 | tf_op jit(solution)/shard_map/all_to_all | solution.py:515
  306.2 17.5 %all-to-all-start.5 = ((bf16[16,128,128]{2,1,0:T(8,128)(2,1)}), bf16[16,128,128]{2,1,0:T(8,128)(2,1)}, u32[]{:S(2)}, u32[]{:S(2)}) async-start(bf16[16,128,128]{2,1,0:T(8,128)(2,1)} %bitcast.23), calls=%async_computation.5 | async-start | bytes 1048576 | tf_op jit(solution)/shard_map/all_to_all | solution.py:544
  (2 other events, 1.9 us)
where the time goes:
time: 327 us; the launch traced here: 325 us
  waiting for transfers between devices  164 us (50%)
  Pallas kernels  77.9 us (24%)
  starting transfers between devices  76.2 us (23%)
  local copies, waits for them, and re-layouts  3.88 us (1%)
    ppermute x8, waiting for transfers between devices, shift(): return lax.ppermute(rows, 'head', pairs)  78.4 us
    ppermute x3, waiting for transfers between devices, shards(): y_halves.append(lax.ppermute(a, both, over_y))  40.1 us
    all_to_all x3, waiting for transfers between devices, exchange(): lax.all_to_all(shaped, both, split_axis=0, concat_axis=0, tiled=True)  35.9 us
    all_to_all x3, starting transfers between devices, exchange(): lax.all_to_all(shaped, both, split_axis=0, concat_axis=0, tiled=True)  28 us
    pallas_call x1, Pallas kernels, shards(): pl.pallas_call(prepare_kernel, grid=(blocks,), in_specs=[pl.BlockSpec((he...  13.1 us
    ppermute x3, starting transfers between devices, shards(): far_own.append(lax.ppermute(a, both, over_core))  12.3 us
    ppermute x8, starting transfers between devices, shift(): return lax.ppermute(rows, 'head', pairs)  11.8 us
    pallas_call x1, Pallas kernels, shards(): pl.pallas_call(back_kernel, grid=(slots // tile,), in_specs=[row_spec, ac...  10.8 us
  transfers between devices with their start and end apart: 24, of which 13 were waited for; matrix products, arithmetic and copies ran while one was open for 1% of the time, Pallas kernels for 15%

commit v1 on v0

--- a/solution.py
+++ b/solution.py
@@ -47,22 +47,24 @@
 
 
 def select_kernel(ids_ref, rows_ref, sel_ref, out_ref):
-    slots, toks = sel_ref.shape
-    expert, rank = slot_experts(slots, toks)
-    named = ids_ref[0:1, :] == expert
-    for k in range(1, ids_ref.shape[0]):
-        named = jnp.logical_or(named, ids_ref[k : k + 1, :] == expert)
-    named = jnp.where(named, 1.0, 0.0)
-    earlier = jnp.where(
-        lax.broadcasted_iota(jnp.int32, (toks, toks), 0)
-        < lax.broadcasted_iota(jnp.int32, (toks, toks), 1),
-        1.0,
-        0.0,
-    )
-    before = dot(named.astype(BF16), earlier.astype(BF16), NN)
-    sel = jnp.where(before == rank.astype(F32), named, 0.0).astype(BF16)
-    sel_ref[...] = sel
-    out_ref[...] = dot(sel, rows_ref[...], NN).astype(BF16)
+    @pl.when(pl.program_id(0) == 0)
+    def _():
+        slots, toks = sel_ref.shape
+        expert, rank = slot_experts(slots, toks)
+        named = ids_ref[0:1, :] == expert
+        for k in range(1, ids_ref.shape[0]):
+            named = jnp.logical_or(named, ids_ref[k : k + 1, :] == expert)
+        named = jnp.where(named, 1.0, 0.0)
+        earlier = jnp.where(
+            lax.broadcasted_iota(jnp.int32, (toks, toks), 0)
+            < lax.broadcasted_iota(jnp.int32, (toks, toks), 1),
+            1.0,
+            0.0,
+        )
+        before = dot(named.astype(BF16), earlier.astype(BF16), NN)
+        sel_ref[...] = jnp.where(before == rank.astype(F32), named, 0.0).astype(BF16)
+
+    out_ref[...] = dot(sel_ref[...], rows_ref[...], NN).astype(BF16)
 
 
 def second_kernel(ids_ref, gates_ref, sel_ref, rows_ref, out_ref, hi_ref, lo_ref):
@@ -139,44 +141,43 @@
     out_ref[...] = dot(both, cat_buf[...], NN).astype(BF16)
 
 
-def combine_kernel(hi_ref, lo_ref, rows_ref, grad_ref, out_ref):
+def combine_kernel(hi_ref, lo_ref, rows_ref, grad_ref, out_ref, first_ref, second_ref):
     rows = rows_ref[...]
     total = dot(hi_ref[...], rows, NN) + dot(lo_ref[...], rows, NN)
-    out_ref[...] = (grad_ref[...].astype(F32) + total).astype(BF16)
-
-
-def project_kernel(place_ref, own_ref, other_ref, near_ref, up_ref, far_a_ref, far_b_ref, dn_ref, out_ref, toks_ref, buf_ref, sem):
-    core, z, y = place_ref[0], place_ref[1], place_ref[2]
-    rows = near_ref.shape[0]
+    resid = (grad_ref[...].astype(F32) + total).astype(BF16)
+    out_ref[...] = resid
+    half = first_ref.shape[0]
+    first_ref[...] = resid[:half]
+    second_ref[...] = resid[half:]
+
+
+def project_kernel(y_ref, *refs):
+    resids, projs, outs, toks_ref, buf_ref, sem = refs[:8], refs[8:13], refs[13:17], refs[17], refs[18], refs[19]
     copies = []
     at = 0
-    for k, source in enumerate((near_ref, up_ref, far_a_ref, far_b_ref, dn_ref)):
+    for k, source in enumerate(projs):
         n = source.shape[0]
         copies.append(pltpu.make_async_copy(source, buf_ref.at[pl.ds(at, n)], sem.at[k]))
         at += n
     for c in copies:
         c.start()
-    toks = own_ref.shape[0]
-    toks_ref[pl.ds(pl.multiple_of(core * toks, toks), toks), :] = own_ref[...]
-    toks_ref[pl.ds(pl.multiple_of((1 - core) * toks, toks), toks), :] = other_ref[...]
-    both = toks_ref[...]
-    part = out_ref.shape[2]
-    waits = ((0,), (1,), (2, 3), (4,))
-    for k, dz in enumerate((0, 3, 2, 1)):
-        for w in waits[k]:
+    half = resids[0].shape[0]
+    toks = 2 * half
+    for k, source in enumerate(resids):
+        place = ((y_ref[0] + (0, 3, 1, 2)[k // 2]) & 3) * toks + k % 2 * half
+        toks_ref[pl.ds(pl.multiple_of(place, half), half), :] = source[...]
+    line = toks_ref[...]
+    rows = outs[0].shape[1]
+    for k, waits in enumerate(((0,), (1,), (2, 3), (4,))):
+        for w in waits:
             copies[w].wait()
-        g = dot(buf_ref[k * rows : (k + 1) * rows, :], both, NT).astype(BF16)
-        for q, dy in enumerate((0, 3, 2, 1)):
-            head = ((z + dz) & 3) * 4 + ((y + dy) & 3)
-            for c in range(2):
-                out_ref[c, head] = g[q * part : (q + 1) * part, c * toks : (c + 1) * toks]
+        g = dot(buf_ref[k * rows : (k + 1) * rows, :], line, NT).astype(BF16)
+        for q in range(4):
+            outs[k][q] = g[:, q * toks : (q + 1) * toks]
 
 
 def block_grads(g_ref, k):
-    pieces = []
-    for j in (2 * k, 2 * k + 1):
-        pieces.append(jnp.concatenate([g_ref[0, j], g_ref[1, j]], axis=0))
-    return jnp.concatenate(pieces, axis=1)
+    return jnp.concatenate([g_ref[2 * k], g_ref[2 * k + 1]], axis=1)
 
 
 def head_rows(rows, heads, dim):
@@ -222,10 +223,12 @@
     tot_ref[...] = tot_ref[...] + block_sum
 
 
-def state_kernel(heads, g_ref, c_ref, ts_ref, bs_ref, tot_ref, fut_ref, pay_ref):
+def state_kernel(heads, z_ref, g0_ref, g1_ref, g2_ref, g3_ref, c_ref, ts_ref, bs_ref, tot_ref, fut_ref, pay_ref, g_ref):
     blocks, rows, lanes = fut_ref.shape
     dim = rows // heads
     n = c_ref.shape[0] // blocks
+    for dz, source in enumerate((g0_ref, g1_ref, g2_ref, g3_ref)):
+        g_ref[pl.ds(((z_ref[0] + dz) & 3) * 4, 4)] = source[...]
     states = []
     for k in range(blocks):
         at = slice(k * n, (k + 1) * n)
@@ -245,27 +248,19 @@
         pay_ref[j] = sent
 
 
-def intra_kernel(
-    heads, skip_ref, wh_ref, wl_ref, g_ref, xh_ref, xl_ref, eh_ref, el_ref, te_ref, b_ref, c_ref, fut_ref, gx_ref, pb_ref
-):
+def intra_kernel(heads, wh_ref, wl_ref, g_ref, xh_ref, xl_ref, eh_ref, el_ref, c_ref, fut_ref, pb_ref):
     n = wh_ref.shape[2]
-    rows = gx_ref.shape[0]
-    dim = rows // heads
+    dim = fut_ref.shape[1] // heads
     for k in range(wh_ref.shape[0]):
         at = slice(k * n, (k + 1) * n)
         fhi, flo = split(fut_ref[k])
-        bhi, blo = split(b_ref[at, :])
-        cross = dot(fhi, bhi, NT) + dot(flo, bhi, NT) + dot(fhi, blo, NT)
-        cross = cross * head_rows(te_ref[:, at], heads, dim)
         acc = None
         grads = block_grads(g_ref, k)
         for h in range(heads):
-            w = wh_ref[k, h]
             cols = slice(h * dim, (h + 1) * dim)
             g = grads[cols]
-            gx_ref[cols, at] = dot(g, w, NT) + cross[cols] + skip_ref[h] * g.astype(F32)
             inner = dot(xh_ref[at, cols], g, NN) + dot(xl_ref[at, cols], g, NN)
-            term = (w.astype(F32) + wl_ref[k, h].astype(F32)) * inner
+            term = (wh_ref[k, h].astype(F32) + wl_ref[k, h].astype(F32)) * inner
             acc = term if acc is None else acc + term
         ahi, alo = split(acc)
         chi, clo = split(c_ref[at, :])
@@ -280,34 +275,56 @@
         )
 
 
-def finish_b_kernel(heads, seq_ref, pay_ref, th_ref, tl_ref, pb_ref, out_ref, hi_ref, lo_ref):
-    rows, lanes = hi_ref.shape
+def finish_b_kernel(heads, seq_ref, pay_ref, th_ref, tl_ref, pb_ref, out_ref, in_ref, th_buf, tl_buf, pb_buf, sem):
+    steps, n = th_buf.shape[0], th_buf.shape[1]
+    copies = [
+        [
+            pltpu.make_async_copy(source.at[pl.ds(i * n, n)], buf.at[i], sem.at[k, i])
+            for k, (source, buf) in enumerate(((th_ref, th_buf), (tl_ref, tl_buf), (pb_ref, pb_buf)))
+        ]
+        for i in range(steps)
+    ]
+    for step in copies:
+        for c in step:
+            c.start()
+    rows, lanes = in_ref.shape
     dim = rows // heads
-
-    @pl.when(pl.program_id(0) == 0)
-    def _():
-        place = seq_ref[0]
-        acc = jnp.zeros((rows, lanes), F32)
-        log = jnp.zeros((8, lanes), F32)
-        for j in range(pay_ref.shape[0]):
-            ahead = j > place
-            factor = jnp.where(ahead, jnp.exp(log), 0.0)
-            acc = acc + head_rows(factor, heads, dim) * pay_ref[j, 0:rows, :].astype(F32)
-            tots = pay_ref[j, rows : rows + 32, :].astype(F32)
-            log = log + jnp.where(ahead, tots[0:8] + tots[8:16] + tots[16:24], 0.0)
-        hi_ref[...], lo_ref[...] = split(acc)
-
-    hi = hi_ref[...]
-    th = th_ref[...]
-    total = pb_ref[...] + dot(th, hi, NN) + dot(th, lo_ref[...], NN) + dot(tl_ref[...], hi, NN)
-    out_ref[...] = total.astype(out_ref.dtype)
-
-
-def finish_x_kernel(heads, hi_ref, lo_ref, tt_ref, b_ref, gx_ref, out_ref):
-    bhi, blo = split(b_ref[...])
-    hi = hi_ref[...]
-    tt = head_rows(tt_ref[...], heads, out_ref.shape[0] // heads)
-    out_ref[...] = gx_ref[...] + tt * (dot(hi, bhi, NT) + dot(lo_ref[...], bhi, NT) + dot(hi, blo, NT))
+    place = seq_ref[0]
+    acc = jnp.zeros((rows, lanes), F32)
+    log = jnp.zeros((8, lanes), F32)
+    for j in range(pay_ref.shape[0]):
+        ahead = j > place
+        factor = jnp.where(ahead, jnp.exp(log), 0.0)
+        acc = acc + head_rows(factor, heads, dim) * pay_ref[j, 0:rows, :].astype(F32)
+        tots = pay_ref[j, rows : rows + 32, :].astype(F32)
+        log = log + jnp.where(ahead, tots[0:8] + tots[8:16] + tots[16:24], 0.0)
+    in_ref[...] = acc
+    hi, lo = split(acc)
+    for i in range(steps):
+        for c in copies[i]:
+            c.wait()
+        th = th_buf[i]
+        total = pb_buf[i] + dot(th, hi, NN) + dot(th, lo, NN) + dot(tl_buf[i], hi, NN)
+        out_ref[i * n : (i + 1) * n, :] = total.astype(out_ref.dtype)
+
+
+def finish_x_kernel(heads, skip_ref, wh_ref, g_ref, te_ref, tt_ref, b_ref, fut_ref, in_ref, out_ref):
+    n = wh_ref.shape[2]
+    rows = out_ref.shape[0]
+    dim = rows // heads
+    ihi, ilo = split(in_ref[...])
+    for k in range(wh_ref.shape[0]):
+        at = slice(k * n, (k + 1) * n)
+        fhi, flo = split(fut_ref[k])
+        bhi, blo = split(b_ref[at, :])
+        local = dot(fhi, bhi, NT) + dot(flo, bhi, NT) + dot(fhi, blo, NT)
+        far = dot(ihi, bhi, NT) + dot(ilo, bhi, NT) + dot(ihi, blo, NT)
+        cross = local * head_rows(te_ref[:, at], heads, dim) + far * head_rows(tt_ref[:, at], heads, dim)
+        grads = block_grads(g_ref, k)
+        for h in range(heads):
+            cols = slice(h * dim, (h + 1) * dim)
+            g = grads[cols]
+            out_ref[cols, at] = dot(g, wh_ref[k, h], NT) + cross[cols] + skip_ref[h] * g.astype(F32)
 
 
 def whole(shape):
@@ -375,9 +392,13 @@
         name="expert_weights",
     )(home.astype(jnp.int32).reshape(1), *own, *far)
 
+    strip = lambda rows: pl.BlockSpec((rows, width // 4), lambda i: (0, i))
     ids_t, gates_t = route_ids.T, route_gates.T
     sel, send_input = pl.pallas_call(
         select_kernel,
+        grid=(4,),
+        in_specs=[whole(ids_t.shape), strip(toks)],
+        out_specs=(whole((slots, toks)), strip(slots)),
         out_shape=(sds((slots, toks), BF16), sds((slots, width), BF16)),
         compiler_params=params(),
         cost_estimate=cost(2 * slots * toks * width, 4 << 20),
@@ -398,20 +419,13 @@
     recv_input = exchange(send_input)
     recv_grad = exchange(send_grad)
 
-    part = inner // 2
-
     def shift(rows, dz, dy):
         pairs = [(z * 4 + y, (z + dz) % 4 * 4 + (y + dy) % 4) for z in range(4) for y in range(4)]
         return lax.ppermute(rows, "head", pairs)
 
-    near = lax.dynamic_slice(out_proj, (core * part, 0), (part, width))
-    up, dn = shift(near, 0, 1), shift(near, 0, -1)
-    far_up = shift(up[: part // 2], 0, 1)
-    far_dn = shift(dn[part // 2 :], 0, -1)
-    line = jnp.concatenate([near, up, far_up, far_dn, dn], axis=0)
-    z_up, z_dn = shift(line, 1, 0), shift(line, -1, 0)
-    z_far_up = shift(z_up[: 2 * part], 1, 0)
-    z_far_dn = shift(z_dn[2 * part :], -1, 0)
+    proj_up, proj_dn = shift(out_proj, 1, 0), shift(out_proj, -1, 0)
+    proj_far_up = shift(proj_up[: inner // 2], 1, 0)
+    proj_far_dn = shift(proj_dn[inner // 2 :], -1, 0)
 
     flip = lambda i: blocks - 1 - i
     row_in = pl.BlockSpec((inner, BLOCK), lambda i: (0, flip(i)))
@@ -468,50 +482,85 @@
     )(recv_grad, factors, expert_down_t, expert_cat_t)
     returned = exchange(expert_rows)
 
-    resid_grad = pl.pallas_call(
+    resid_grad, first, second = pl.pallas_call(
         combine_kernel,
-        out_shape=sds((toks, width), BF16),
+        grid=(4,),
+        in_specs=[whole((toks, slots))] * 2 + [strip(slots), strip(toks)],
+        out_specs=(strip(toks), strip(toks // 2), strip(toks // 2)),
+        out_shape=(sds((toks, width), BF16),) + (sds((toks // 2, width), BF16),) * 2,
         compiler_params=params(),
         cost_estimate=cost(4 * slots * toks * width, 4 << 20),
         name="combine_rows",
     )(mix_hi, mix_lo, returned, out_grad)
-    resid_other = lax.ppermute(resid_grad, "core", [(0, 1), (1, 0)])
-    grad_all = pl.pallas_call(
+    up_first = shift(first, 0, 1)
+    dn_second = shift(second, 0, -1)
+    up_second = shift(second, 0, 1)
+    dn_first = shift(first, 0, -1)
+    far_first = shift(up_first, 0, 1)
+    far_second = shift(dn_second, 0, -1)
+    part_spec = whole((n_head // 4, inner, toks))
+    part_shape = sds((n_head // 4, inner, toks), BF16)
+    halves_spec = whole((toks // 2, width))
+    to_0, to_3, to_2, to_1 = pl.pallas_call(
         project_kernel,
         grid=(1,),
-        in_specs=[smem_spec] + [whole((toks, width))] * 2 + [any_spec] * 5,
-        out_specs=whole((2, n_head, part, toks)),
-        out_shape=sds((2, n_head, part, toks), BF16),
+        in_specs=[smem_spec] + [halves_spec] * 8 + [any_spec] * 5,
+        out_specs=(part_spec,) * 4,
+        out_shape=(part_shape,) * 4,
         scratch_shapes=[
-            pltpu.VMEM((2 * toks, width), BF16),
-            pltpu.VMEM((n_head * part, width), BF16),
+            pltpu.VMEM((4 * toks, width), BF16),
+            pltpu.VMEM((4 * inner, width), BF16),
             pltpu.SemaphoreType.DMA((5,)),
         ],
-        compiler_params=params(),
-        cost_estimate=cost(4 * n_head * part * toks * width, 7 << 20),
+        compiler_params=params(24 << 20),
+        cost_estimate=cost(32 * inner * toks * width, 7 << 20),
         name="project_rows",
-    )(jnp.stack([core, head >> 2, head & 3]), resid_grad, resid_other, line, z_up, z_far_up, z_far_dn, z_dn)
-    grads = lax.all_to_all(
-        grad_all.reshape(2 * n_head, part, toks), ("core", "head"), split_axis=0, concat_axis=0, tiled=True
-    ).reshape(2, n_head, part, toks)
+    )(
+        (head & 3).reshape(1),
+        first,
+        second,
+        up_first,
+        up_second,
+        dn_first,
+        dn_second,
+        far_first,
+        far_second,
+        out_proj,
+        proj_up,
+        proj_far_up,
+        proj_far_dn,
+        proj_dn,
+    )
+    from_2 = shift(to_2, 2, 0)
+    from_3 = shift(to_1, 1, 0)
+    from_1 = shift(to_3, -1, 0)
 
     pay_rows = inner + 32
-    future, payload = pl.pallas_call(
+    future, payload, grads = pl.pallas_call(
         functools.partial(state_kernel, heads),
-        out_shape=(sds((blocks, inner, state), F32), sds((n_seq, pay_rows, state), BF16)),
+        out_shape=(
+            sds((blocks, inner, state), F32),
+            sds((n_seq, pay_rows, state), BF16),
+            sds((n_head, inner, toks), BF16),
+        ),
         grid=(1,),
-        in_specs=[
-            whole((2, n_head, part, toks)),
+        in_specs=[smem_spec]
+        + [part_spec] * 4
+        + [
             whole((seq_rows, state)),
             whole((8, seq_rows)),
             whole((blocks, 8, state)),
             whole((8, state)),
         ],
-        out_specs=(whole((blocks, inner, state)), whole((n_seq, pay_rows, state))),
+        out_specs=(
+            whole((blocks, inner, state)),
+            whole((n_seq, pay_rows, state)),
+            whole((n_head, inner, toks)),
+        ),
         compiler_params=params(),
         cost_estimate=cost(1e9, 4 << 20),
         name="scan_state",
-    )(grads, c_proj, to_start, block_sum, total)
+    )((head >> 2).reshape(1), to_0, from_1, from_2, from_3, c_proj, to_start, block_sum, total)
     pays = lax.all_to_all(payload, seq_axes, split_axis=0, concat_axis=0, tiled=True)
     pair = 2
     spec = lambda *shape: pl.BlockSpec(shape, lambda i: (i,) + (0,) * (len(shape) - 1))
@@ -519,24 +568,27 @@
     tok_in2, tok_st2 = spec(pair * BLOCK, inner), spec(pair * BLOCK, state)
     row_in2, row_82 = cols(inner, pair * BLOCK), cols(8, pair * BLOCK)
     w_spec = spec(pair, heads, BLOCK, BLOCK)
-    part_x, part_b = pl.pallas_call(
+    g_spec = spec(pair * BLOCK // toks, inner, toks)
+    f_spec = spec(pair, inner, state)
+    part_b = pl.pallas_call(
         functools.partial(intra_kernel, heads),
         grid=(blocks // pair,),
-        in_specs=[smem_spec, w_spec, w_spec, pl.BlockSpec((2, pair * BLOCK // toks, part, toks), lambda i: (0, i, 0, 0))]
-        + [tok_in2] * 4
-        + [row_82, tok_st2, tok_st2, spec(pair, inner, state)],
-        out_specs=(row_in2, tok_st2),
-        out_shape=(sds((inner, seq_rows), F32), sds((seq_rows, state), F32)),
+        in_specs=[w_spec, w_spec, g_spec] + [tok_in2] * 4 + [tok_st2, f_spec],
+        out_specs=tok_st2,
+        out_shape=sds((seq_rows, state), F32),
         compiler_params=params(),
         cost_estimate=cost(4e9, 16 << 20),
         name="scan_intra",
-    )(skip_gain, w_hi, w_lo, grads, x_hi, x_lo, e_hi, e_lo, to_end, b_proj, c_proj, future)
-    partial_b, in_hi, in_lo = pl.pallas_call(
+    )(w_hi, w_lo, grads, x_hi, x_lo, e_hi, e_lo, c_proj, future)
+    steps = 4
+    partial_b, incoming = pl.pallas_call(
         functools.partial(finish_b_kernel, heads),
-        grid=(blocks // pair,),
-        in_specs=[smem_spec, whole((n_seq, pay_rows, state)), tok_in2, tok_in2, tok_st2],
-        out_specs=(tok_st2, whole((inner, state)), whole((inner, state))),
-        out_shape=(sds((seq_rows, state), BF16), sds((inner, state), BF16), sds((inner, state), BF16)),
+        grid=(1,),
+        in_specs=[smem_spec, whole((n_seq, pay_rows, state))] + [any_spec] * 3,
+        out_specs=(whole((seq_rows, state)), whole((inner, state))),
+        out_shape=(sds((seq_rows, state), BF16), sds((inner, state), F32)),
+        scratch_shapes=[pltpu.VMEM((steps, seq_rows // steps, inner), BF16)] * 2
+        + [pltpu.VMEM((steps, seq_rows // steps, state), F32), pltpu.SemaphoreType.DMA((3, steps))],
         compiler_params=params(),
         cost_estimate=cost(4e8, 6 << 20),
         name="scan_finish_b",
@@ -547,13 +599,13 @@
     grad_x = pl.pallas_call(
         functools.partial(finish_x_kernel, heads),
         grid=(blocks // pair,),
-        in_specs=[whole((inner, state)), whole((inner, state)), row_82, tok_st2, row_in2],
+        in_specs=[smem_spec, w_spec, g_spec, row_82, row_82, tok_st2, f_spec, whole((inner, state))],
         out_specs=row_in2,
         out_shape=sds((inner, seq_rows), F32),
         compiler_params=params(),
         cost_estimate=cost(4e8, 6 << 20),
         name="scan_finish_x",
-    )(in_hi, in_lo, to_last, b_proj, part_x)
+    )(skip_gain, w_hi, grads, to_end, to_last, b_proj, future, incoming)
     b_grad = jnp.sum(shares.astype(F32), axis=0)
     return (resid_grad, grad_x.T, b_grad)
 

time: 327 us -> 308 us (0.942)
  waiting for transfers between devices: 164 us -> 139 us
    ppermute x8 -> x13, waiting for transfers between devices: 78.4 us -> 50.9 us  [shift(): return lax.ppermute(rows, 'head', pairs)]
    ppermute x8 -> x13, starting transfers between devices: 11.8 us -> 18.3 us  [shift(): return lax.ppermute(rows, 'head', pairs)]
    all_to_all x1 -> x0, starting transfers between devices: 4.64 us -> none  [shards(): lax.all_to_all(grad_all.reshape(2 * n_head, part, toks), ('core', 'head')...]
    ppermute x3, waiting for transfers between devices: 40.1 us -> 44.3 us  [shards(): y_halves.append(lax.ppermute(a, both, over_y))]
    unnamed x24 -> x20, local copies, waits for them, and re-layouts: 2.04 us -> 5.31 us
  transfers between devices with their start and end apart: 24 -> 27, of which waited for: 13 -> 10; matrix products, arithmetic and copies ran while one was open for 1% -> 1% of each run, Pallas kernels for 15% -> 16%
where the time goes in v1:
time: 308 us; the launch traced here: 307 us
  waiting for transfers between devices  139 us (45%)
  Pallas kernels  79.5 us (26%)
  starting transfers between devices  78.7 us (26%)
  local copies, waits for them, and re-layouts  7.04 us (2%)
    ppermute x13, waiting for transfers between devices, shift(): return lax.ppermute(rows, 'head', pairs)  50.9 us
    ppermute x3, waiting for transfers between devices, shards(): y_halves.append(lax.ppermute(a, both, over_y))  44.3 us
    all_to_all x3, waiting for transfers between devices, exchange(): lax.all_to_all(shaped, both, split_axis=0, concat_axis=0, tiled=True)  35.9 us
    all_to_all x3, starting transfers between devices, exchange(): lax.all_to_all(shaped, both, split_axis=0, concat_axis=0, tiled=True)  28 us
    ppermute x13, starting transfers between devices, shift(): return lax.ppermute(rows, 'head', pairs)  18.3 us
    pallas_call x1, Pallas kernels, shards(): pl.pallas_call(prepare_kernel, grid=(blocks,), in_specs=[pl.BlockSpec((he...  13.1 us
    pallas_call x1, Pallas kernels, shards(): pl.pallas_call(back_kernel, grid=(slots // tile,), in_specs=[row_spec, ac...  10.8 us
    ppermute x3, starting transfers between devices, shards(): far_own.append(lax.ppermute(a, both, over_core))  9.39 us
  transfers between devices with their start and end apart: 27, of which 10 were waited for; matrix products, arithmetic and copies ran while one was open for 1% of the time, Pallas kernels for 16%

profile of v1, /device:TPU:0, one launch (start us, length us, event | category | flops | bytes accessed | tf_op | source)
XLA Modules:
  0.0 306.6 jit_solution(14251154455363574831)
XLA Ops:
  0.6 5.0 %select_rows.1 = (bf16[1024,128]{1,0:T(8,128)(2,1)}, bf16[1024,1536]{1,0:T(8,128)(2,1)}) custom-call(s32[6,128]{1,0:T(8,128)} %bitcast.21, bf16[128,1536]{1,0:T(8,128)(2,1)} %rows_ref.2), custom_call_target="tpu_custom_call" | custom-call | flops 402653184 | bytes 4194304 | tf_op jit(solution)/shard_map/select_rows/pallas_call | solution.py:397
  5.6 11.6 %all-to-all-start.1 = ((bf16[128,8,1536]{2,1,0:T(8,128)(2,1)}), bf16[128,8,1536]{2,1,0:T(8,128)(2,1)}, u32[]{:S(2)}, u32[]{:S(2)}) async-start(bf16[128,8,1536]{2,1,0:T(8,128)(2,1)} %bitcast.17), calls=%async_computation.1 | async-start | bytes 6291456 | tf_op jit(solution)/shard_map/all_to_all | solution.py:417
  17.2 4.1 %select_grads.1 = (bf16[1024,1536]{1,0:T(8,128)(2,1)}, bf16[128,1024]{1,0:T(8,128)(2,1)}, bf16[128,1024]{1,0:T(8,128)(2,1)}) custom-call(s32[6,128]{1,0:T(8,128)} %bitcast.22, f32[6,128]{1,0:T(8,128)} %bitcast.23, bf16[1024,128]{1,0:T(8,128)(2,1)} %get-tuple-element.36.sel_ref, bf16[128,1536]{1,0:T(8,128)(2,1)} %grad_ref.1), custom_call_target="tpu_custom_call" | custom-call | flops 402653184 | bytes 4194304 | tf_op jit(solution)/shard_map/select_grads/pallas_call | solution.py:407
  21.3 35.9 %all-to-all-done.1 = bf16[128,8,1536]{2,1,0:T(8,128)(2,1)} async-done(((bf16[128,8,1536]{2,1,0:T(8,128)(2,1)}), bf16[128,8,1536]{2,1,0:T(8,128)(2,1)}, u32[]{:S(2)}, u32[]{:S(2)}) %all-to-all-start.1) | async-done | bytes 3145760 | tf_op jit(solution)/shard_map/all_to_all | solution.py:417
  57.3 5.9 %all-to-all-start = ((bf16[128,8,1536]{2,1,0:T(8,128)(2,1)}), bf16[128,8,1536]{2,1,0:T(8,128)(2,1)}, u32[]{:S(2)}, u32[]{:S(2)}) async-start(bf16[128,8,1536]{2,1,0:T(8,128)(2,1)} %bitcast.15), calls=%async_computation | async-start | bytes 6291456 | tf_op jit(solution)/shard_map/all_to_all | solution.py:417
  67.1 5.0 %collective-permute-start.3 = (bf16[1,1536,256]{2,1,0:T(8,128)(2,1)S(1)}, bf16[1,1536,256]{2,1,0:T(8,128)(2,1)S(1)}, u32[]{:S(2)}, u32[]{:S(2)}) collective-permute-start(bf16[1,1536,256]{2,1,0:T(8,128)(2,1)S(1)} %copy-done.5), channel_id=1, source_target_pairs={{0,16},{2,18},{4,20},{6,22},{8,24},{10,26},{12,28},{14,30},{17,1},... | collective-permute-start | bytes 2359304 | tf_op jit(solution)/shard_map/ppermute | solution.py:379
  74.3 31.7 %collective-permute-done.refs_1_ = bf16[1,1536,256]{2,1,0:T(8,128)(2,1)S(1)} collective-permute-done((bf16[1,1536,256]{2,1,0:T(8,128)(2,1)S(1)}, bf16[1,1536,256]{2,1,0:T(8,128)(2,1)S(1)}, u32[]{:S(2)}, u32[]{:S(2)}) %collective-permute-start) | collective-permute-done | bytes 786464 | tf_op jit(solution)/shard_map/ppermute | solution.py:377
  108.2 6.4 %collective-permute-done.1.refs_3_ = bf16[1,1536,256]{2,1,0:T(8,128)(2,1)} collective-permute-done((bf16[1,1536,256]{2,1,0:T(8,128)(2,1)S(1)}, bf16[1,1536,256]{2,1,0:T(8,128)(2,1)}, u32[]{:S(2)}, u32[]{:S(2)}) %collective-permute-start.1) | collective-permute-done | bytes 786464 | tf_op jit(solution)/shard_map/ppermute | solution.py:377
  114.6 2.2 collective-permute-start.4
  116.7 6.2 %collective-permute-done.2.refs_5_ = bf16[1,256,1536]{2,1,0:T(8,128)(2,1)} collective-permute-done((bf16[1,256,1536]{2,1,0:T(8,128)(2,1)S(1)}, bf16[1,256,1536]{2,1,0:T(8,128)(2,1)}, u32[]{:S(2)}, u32[]{:S(2)}) %collective-permute-start.2) | collective-permute-done | bytes 786464 | tf_op jit(solution)/shard_map/ppermute | solution.py:377
  123.0 2.2 collective-permute-start.6
  126.1 2.2 collective-permute-start.8
  129.6 5.7 %expert_weights.1 = (bf16[1536,1024]{1,0:T(8,128)(2,1)}, bf16[1024,1536]{1,0:T(8,128)(2,1)}, bf16[1536,512]{1,0:T(8,128)(2,1)}) custom-call(s32[1]{0:T(128)} %bitcast.6.home_ref, bf16[1,1536,256]{2,1,0:T(8,128)(2,1)} %refs_0_.1, bf16[1,1536,256]{2,1,0:T(8,128)(2,1)} %copy-done.8, bf16[1,1536,256]{2,1,0:T(8,128)(2,1)} %refs_2_.1, ...), custom_call_target="tpu_custom_call" | custom-call | flops 1000000000 | bytes 12582912 | tf_op jit(solution)/shard_map/expert_weights/pallas_call | solution.py:385
  135.3 7.8 %expert_acts.1.act_ref = f32[1024,1024]{1,0:T(8,128)} custom-call(bf16[1024,1536]{1,0:T(8,128)(2,1)} %bitcast.5.x_ref, bf16[1536,1024]{1,0:T(8,128)(2,1)} %get-tuple-element.41.w_ref), custom_call_target="tpu_custom_call" | custom-call | flops 3221225472 | bytes 10485760 | tf_op jit(solution)/shard_map/expert_acts/pallas_call | solution.py:458
  143.1 10.8 %expert_back.1 = bf16[1024,1536]{1,0:T(8,128)(2,1)} custom-call(bf16[1024,1536]{1,0:T(8,128)(2,1)} %bitcast.3.g_ref, f32[1024,1024]{1,0:T(8,128)} %expert_acts.1.act_ref, bf16[1536,512]{1,0:T(8,128)(2,1)} %get-tuple-element.42.down_ref, bf16[1024,1536]{1,0:T(8,128)(2,1)} %get-tuple-element.43.cat_ref), custom_call_target="tpu_custom_call" | custom-call | flops 4831838208 | bytes 14680064 | tf_op jit(solution)/shard_map/expert_back/pallas_call | solution.py:468
  153.9 10.5 %all-to-all-start.2 = ((bf16[128,8,1536]{2,1,0:T(8,128)(2,1)}), bf16[128,8,1536]{2,1,0:T(8,128)(2,1)}, u32[]{:S(2)}, u32[]{:S(2)}) async-start(bf16[128,8,1536]{2,1,0:T(8,128)(2,1)} %bitcast.16), calls=%async_computation.2 | async-start | bytes 6291456 | tf_op jit(solution)/shard_map/all_to_all | solution.py:417
  165.6 2.2 collective-permute-start.17
  167.8 46.0 %collective-permute-done.15.refs_9_ = bf16[192,1536]{1,0:T(8,128)(2,1)S(1)} collective-permute-done((bf16[192,1536]{1,0:T(8,128)(2,1)}, bf16[192,1536]{1,0:T(8,128)(2,1)S(1)}, u32[]{:S(2)}, u32[]{:S(2)}) %collective-permute-start.15) | collective-permute-done | bytes 589856 | tf_op jit(solution)/shard_map/ppermute | solution.py:424
  215.4 4.7 %combine_rows.1 = (bf16[128,1536]{1,0:T(8,128)(2,1)}, bf16[64,1536]{1,0:T(8,128)(2,1)}, bf16[64,1536]{1,0:T(8,128)(2,1)}) custom-call(bf16[128,1024]{1,0:T(8,128)(2,1)} %get-tuple-element.37.hi_ref, bf16[128,1024]{1,0:T(8,128)(2,1)} %get-tuple-element.38.lo_ref, bf16[1024,1536]{1,0:T(8,128)(2,1)} %bitcast.8.rows_ref, bf16[128,1536]{1,0:T(8,128)(2,1)} %grad_ref.1), custom_call_target="tpu_custom_call" | custom-call | flops 805306368 | bytes 4194304 | tf_op jit(solution)/shard_map/combine_rows/pallas_call | solution.py:485
  224.3 3.3 %collective-permute-start.18 = (bf16[96,1536]{1,0:T(8,128)(2,1)S(1)}, bf16[96,1536]{1,0:T(8,128)(2,1)S(1)}, u32[]{:S(2)}, u32[]{:S(2)}) collective-permute-start(bf16[96,1536]{1,0:T(8,128)(2,1)S(1)} %slice.9), channel_id=1, source_target_pairs={{0,12},{1,13},{2,14},{3,15},{4,0},{5,1},{6,2},{7,3},{8,4},{9,5},{1... | collective-permute-start | bytes 884744 | tf_op jit(solution)/shard_map/ppermute | solution.py:424
  228.0 2.9 collective-permute-start.11
  230.9 3.2 %collective-permute-start.14 = (bf16[64,1536]{1,0:T(8,128)(2,1)S(1)}, bf16[64,1536]{1,0:T(8,128)(2,1)S(1)}, u32[]{:S(2)}, u32[]{:S(2)}) collective-permute-start(bf16[64,1536]{1,0:T(8,128)(2,1)S(1)} %collective-permute-done.12.refs_5_), channel_id=1, source_target_pairs={{0,3},{1,0},{2,1},{3,2},{4,7},{5,4},{6,5},{7,6},{8,11},{9,8},{10,9... | collective-permute-start | bytes 589832 | tf_op jit(solution)/shard_map/ppermute | solution.py:424
  234.1 2.6 collective-permute-done.10.refs_3_
  241.9 4.4 %project_rows.1 = (bf16[4,192,128]{2,1,0:T(8,128)(2,1)S(1)}, bf16[4,192,128]{2,1,0:T(8,128)(2,1)}, bf16[4,192,128]{2,1,0:T(8,128)(2,1)}, bf16[4,192,128]{2,1,0:T(8,128)(2,1)}) custom-call(s32[1]{0:T(128)} %bitcast.11.y_ref, bf16[64,1536]{1,0:T(8,128)(2,1)S(1)} %copy-done.2, bf16[64,1536]{1,0:T(8,128)(2,1)S(1)} %copy-done.3, ...), custom_call_target="tpu_custom_call" | custom-call | flops 1207959552 | bytes 7340032 | tf_op jit(solution)/shard_map/project_rows/pallas_call | solution.py:504
  249.0 13.1 %scan_prepare.1 = (bf16[8,3,256,256]{3,2,1,0:T(8,128)(2,1)}, bf16[8,3,256,256]{3,2,1,0:T(8,128)(2,1)}, f32[8,2048]{1,0:T(8,128)}, f32[8,2048]{1,0:T(8,128)}, f32...) custom-call(f32[3,2048]{1,0:T(4,128)} %d_ref.1, ...), custom_call_target="tpu_custom_call" | custom-call | flops 4000000000 | bytes 20971520 | tf_op jit(solution)/shard_map/scan_prepare/pallas_call | solution.py:441
  262.2 3.9 %scan_state.1 = (f32[8,192,128]{2,1,0:T(8,128)}, bf16[8,224,128]{2,1,0:T(8,128)(2,1)}, bf16[16,192,128]{2,1,0:T(8,128)(2,1)}) custom-call(s32[1]{0:T(128)} %bitcast.10.z_ref, bf16[4,192,128]{2,1,0:T(8,128)(2,1)} %copy-done.4, bf16[4,192,128]{2,1,0:T(8,128)(2,1)} %collective-permute-done.19.g1_ref, bf16[4,192,128]{2,1,0:T(8,128)(2,1)} %collective-permute-done.20.g2_ref, ...), custom_call_target="tpu_custom_call" | custom-call | flops 1000000000 | bytes 4194304 | tf_op jit(solution)/shard_map/scan_state/pallas_call | solution.py:539
  266.1 4.3 %all-to-all-start.3 = ((bf16[8,224,128]{2,1,0:T(8,128)(2,1)}), bf16[8,224,128]{2,1,0:T(8,128)(2,1)}, u32[]{:S(2)}, u32[]{:S(2)}) async-start(bf16[8,224,128]{2,1,0:T(8,128)(2,1)} %get-tuple-element.59), calls=%async_computation.3 | async-start | bytes 917504 | tf_op jit(solution)/shard_map/all_to_all | solution.py:564
  270.4 8.8 %scan_intra.1.pb_ref = f32[2048,128]{1,0:T(8,128)} custom-call(bf16[8,3,256,256]{3,2,1,0:T(8,128)(2,1)} %get-tuple-element.45.wh_ref, bf16[8,3,256,256]{3,2,1,0:T(8,128)(2,1)} %get-tuple-element.62.wl_ref, bf16[16,192,128]{2,1,0:T(8,128)(2,1)} %get-tuple-element.55.g_ref, bf16[2048,192]{1,0:T(8,128)(2,1)} %get-tuple-element.63.xh_ref, ...), custom_call_target="tpu_custom_call" | custom-call | flops 4000000000 | bytes 16777216 | tf_op jit(solution)/shard_map/scan_intra/pallas_call | solution.py:573
  280.1 5.2 %scan_finish_b.1 = (bf16[2048,128]{1,0:T(8,128)(2,1)}, f32[192,128]{1,0:T(8,128)}) custom-call(s32[1]{0:T(128)} %bitcast.12.seq_ref, bf16[8,224,128]{2,1,0:T(8,128)(2,1)} %all-to-all-done.3.pay_ref, bf16[2048,192]{1,0:T(8,128)(2,1)} %get-tuple-element.60.th_ref, bf16[2048,192]{1,0:T(8,128)(2,1)} %get-tuple-element.61.tl_ref, f32[2048,128]{1,0:T(8,128)} %scan_intra.1.pb_ref), custom_call_target="tpu_custom_call" | custom-call | flops 400000000 | bytes 6291456 | tf_op jit(solution)/shard_map/scan_finish_b/pallas_call | solution.py:584
  285.3 8.2 %all-to-all-start.4 = ((bf16[16,128,128]{2,1,0:T(8,128)(2,1)}), bf16[16,128,128]{2,1,0:T(8,128)(2,1)}, u32[]{:S(2)}, u32[]{:S(2)}) async-start(bf16[16,128,128]{2,1,0:T(8,128)(2,1)} %bitcast.19), calls=%async_computation.4 | async-start | bytes 1048576 | tf_op jit(solution)/shard_map/all_to_all | solution.py:596
  293.5 5.9 %scan_finish_x.1 = f32[192,2048]{1,0:T(8,128)} custom-call(f32[3]{0:T(128)} %skip_ref.1, bf16[8,3,256,256]{3,2,1,0:T(8,128)(2,1)} %get-tuple-element.45.wh_ref, bf16[16,192,128]{2,1,0:T(8,128)(2,1)} %get-tuple-element.55.g_ref, f32[8,2048]{1,0:T(8,128)} %get-tuple-element.56.te_ref, f32[8,2048]{1,0:T(8,128)} %get-tuple-element.57.tt_ref, f32[2048,128]{1,0:T(8,128)} %b_ref.3, ...), custom_call_target="tpu_custom_call" | custom-call | flops 400000000 | bytes 6291456 | tf_op jit(solution)/shard_map/scan_finish_x/pallas_call | solution.py:599
  299.5 5.4 %all-to-all-done.4 = bf16[16,128,128]{2,1,0:T(8,128)(2,1)} async-done(((bf16[16,128,128]{2,1,0:T(8,128)(2,1)}), bf16[16,128,128]{2,1,0:T(8,128)(2,1)}, u32[]{:S(2)}, u32[]{:S(2)}) %all-to-all-start.4) | async-done | bytes 524320 | tf_op jit(solution)/shard_map/all_to_all | solution.py:596
  (57 shorter events, 28.1 us)
Async XLA Ops:
  5.6 51.7 %all-to-all-start.1 = ((bf16[128,8,1536]{2,1,0:T(8,128)(2,1)}), bf16[128,8,1536]{2,1,0:T(8,128)(2,1)}, u32[]{:S(2)}, u32[]{:S(2)}) async-start(bf16[128,8,1536]{2,1,0:T(8,128)(2,1)} %bitcast.17), calls=%async_computation.1 | async-start | bytes 6291456 | tf_op jit(solution)/shard_map/all_to_all | solution.py:417
  57.3 5.9 %copy-start.5 = (bf16[1,1536,256]{2,1,0:T(8,128)(2,1)S(1)}, bf16[1,1536,256]{2,1,0:T(8,128)(2,1)}, u32[]{:S(2)}) copy-start(bf16[1,1536,256]{2,1,0:T(8,128)(2,1)} %refs_0_.1) | copy-start | bytes 2359300
  57.3 7.2 %copy-start.6 = (bf16[1,1536,256]{2,1,0:T(8,128)(2,1)S(1)}, bf16[1,1536,256]{2,1,0:T(8,128)(2,1)}, u32[]{:S(2)}) copy-start(bf16[1,1536,256]{2,1,0:T(8,128)(2,1)} %refs_2_.1) | copy-start | bytes 2359300
  57.3 8.5 %copy-start.7 = (bf16[1,256,1536]{2,1,0:T(8,128)(2,1)S(1)}, bf16[1,256,1536]{2,1,0:T(8,128)(2,1)}, u32[]{:S(2)}) copy-start(bf16[1,256,1536]{2,1,0:T(8,128)(2,1)} %refs_4_.1) | copy-start | bytes 2359300
  57.3 85.9 %all-to-all-start = ((bf16[128,8,1536]{2,1,0:T(8,128)(2,1)}), bf16[128,8,1536]{2,1,0:T(8,128)(2,1)}, u32[]{:S(2)}, u32[]{:S(2)}) async-start(bf16[128,8,1536]{2,1,0:T(8,128)(2,1)} %bitcast.15), calls=%async_computation | async-start | bytes 6291456 | tf_op jit(solution)/shard_map/all_to_all | solution.py:417
  63.2 42.9 %collective-permute-start = (bf16[1,1536,256]{2,1,0:T(8,128)(2,1)S(1)}, bf16[1,1536,256]{2,1,0:T(8,128)(2,1)S(1)}, u32[]{:S(2)}, u32[]{:S(2)}) collective-permute-start(bf16[1,1536,256]{2,1,0:T(8,128)(2,1)S(1)} %copy-done.5), channel_id=1, source_target_pairs={{1,0},{3,2},{5,4},{7,6},{9,8},{11,10},{13,12},{15,14},{16,17},{18,... | collective-permute-start | bytes 2359304 | tf_op jit(solution)/shard_map/ppermute | solution.py:377
  64.5 50.1 %collective-permute-start.1 = (bf16[1,1536,256]{2,1,0:T(8,128)(2,1)S(1)}, bf16[1,1536,256]{2,1,0:T(8,128)(2,1)}, u32[]{:S(2)}, u32[]{:S(2)}) collective-permute-start(bf16[1,1536,256]{2,1,0:T(8,128)(2,1)S(1)} %copy-done.6), channel_id=1, source_target_pairs={{1,0},{3,2},{5,4},{7,6},{9,8},{11,10},{13,12},{15,14},{16,17},{18,... | collective-permute-start | bytes 2359304 | tf_op jit(solution)/shard_map/ppermute | solution.py:377
  65.8 57.2 %collective-permute-start.2 = (bf16[1,256,1536]{2,1,0:T(8,128)(2,1)S(1)}, bf16[1,256,1536]{2,1,0:T(8,128)(2,1)}, u32[]{:S(2)}, u32[]{:S(2)}) collective-permute-start(bf16[1,256,1536]{2,1,0:T(8,128)(2,1)S(1)} %copy-done.7), channel_id=1, source_target_pairs={{1,0},{3,2},{5,4},{7,6},{9,8},{11,10},{13,12},{15,14},{16,17},{18,... | collective-permute-start | bytes 2359304 | tf_op jit(solution)/shard_map/ppermute | solution.py:377
  67.1 58.1 %collective-permute-start.3 = (bf16[1,1536,256]{2,1,0:T(8,128)(2,1)S(1)}, bf16[1,1536,256]{2,1,0:T(8,128)(2,1)S(1)}, u32[]{:S(2)}, u32[]{:S(2)}) collective-permute-start(bf16[1,1536,256]{2,1,0:T(8,128)(2,1)S(1)} %copy-done.5), channel_id=1, source_target_pairs={{0,16},{2,18},{4,20},{6,22},{8,24},{10,26},{12,28},{14,30},{17,1},... | collective-permute-start | bytes 2359304 | tf_op jit(solution)/shard_map/ppermute | solution.py:379
  72.1 56.1 %collective-permute-start.5 = (bf16[1,1536,256]{2,1,0:T(8,128)(2,1)S(1)}, bf16[1,1536,256]{2,1,0:T(8,128)(2,1)}, u32[]{:S(2)}, u32[]{:S(2)}) collective-permute-start(bf16[1,1536,256]{2,1,0:T(8,128)(2,1)S(1)} %copy-done.6), channel_id=1, source_target_pairs={{0,16},{2,18},{4,20},{6,22},{8,24},{10,26},{12,28},{14,30},{17,1},... | collective-permute-start | bytes 2359304 | tf_op jit(solution)/shard_map/ppermute | solution.py:379
  106.0 22.3 %copy-start.8 = (bf16[1,1536,256]{2,1,0:T(8,128)(2,1)}, bf16[1,1536,256]{2,1,0:T(8,128)(2,1)S(1)}, u32[]{:S(2)}) copy-start(bf16[1,1536,256]{2,1,0:T(8,128)(2,1)S(1)} %collective-permute-done.refs_1_) | copy-start | bytes 2359300
  106.0 22.2 %collective-permute-start.7 = (bf16[1,256,1536]{2,1,0:T(8,128)(2,1)S(1)}, bf16[1,256,1536]{2,1,0:T(8,128)(2,1)}, u32[]{:S(2)}, u32[]{:S(2)}) collective-permute-start(bf16[1,256,1536]{2,1,0:T(8,128)(2,1)S(1)} %copy-done.7), channel_id=1, source_target_pairs={{0,16},{2,18},{4,20},{6,22},{8,24},{10,26},{12,28},{14,30},{17,1},... | collective-permute-start | bytes 2359304 | tf_op jit(solution)/shard_map/ppermute | solution.py:379
  114.6 13.7 %collective-permute-start.4 = (bf16[1,1536,256]{2,1,0:T(8,128)(2,1)S(1)}, bf16[1,1536,256]{2,1,0:T(8,128)(2,1)}, u32[]{:S(2)}, u32[]{:S(2)}) collective-permute-start(bf16[1,1536,256]{2,1,0:T(8,128)(2,1)S(1)} %collective-permute-done.refs_1_), channel_id=1, source_target_pairs={{0,16},{2,18},{4,20},{6,22},{8,24},{10,26},{12,28},{14,30},{17,1},... | collective-permute-start | bytes 2359304 | tf_op jit(solution)/shard_map/ppermute | solution.py:380
  123.0 5.3 %collective-permute-start.6 = (bf16[1,1536,256]{2,1,0:T(8,128)(2,1)}, bf16[1,1536,256]{2,1,0:T(8,128)(2,1)}, u32[]{:S(2)}, u32[]{:S(2)}) collective-permute-start(bf16[1,1536,256]{2,1,0:T(8,128)(2,1)} %collective-permute-done.1.refs_3_), channel_id=1, source_target_pairs={{0,16},{2,18},{4,20},{6,22},{8,24},{10,26},{12,28},{14,30},{17,1},... | collective-permute-start | bytes 2359304 | tf_op jit(solution)/shard_map/ppermute | solution.py:380
  126.1 3.5 %collective-permute-start.8 = (bf16[1,256,1536]{2,1,0:T(8,128)(2,1)}, bf16[1,256,1536]{2,1,0:T(8,128)(2,1)}, u32[]{:S(2)}, u32[]{:S(2)}) collective-permute-start(bf16[1,256,1536]{2,1,0:T(8,128)(2,1)} %collective-permute-done.2.refs_5_), channel_id=1, source_target_pairs={{0,16},{2,18},{4,20},{6,22},{8,24},{10,26},{12,28},{14,30},{17,1},... | collective-permute-start | bytes 2359304 | tf_op jit(solution)/shard_map/ppermute | solution.py:380
  153.9 61.5 %all-to-all-start.2 = ((bf16[128,8,1536]{2,1,0:T(8,128)(2,1)}), bf16[128,8,1536]{2,1,0:T(8,128)(2,1)}, u32[]{:S(2)}, u32[]{:S(2)}) async-start(bf16[128,8,1536]{2,1,0:T(8,128)(2,1)} %bitcast.16), calls=%async_computation.2 | async-start | bytes 6291456 | tf_op jit(solution)/shard_map/all_to_all | solution.py:417
  164.5 49.4 %collective-permute-start.15 = (bf16[192,1536]{1,0:T(8,128)(2,1)}, bf16[192,1536]{1,0:T(8,128)(2,1)S(1)}, u32[]{:S(2)}, u32[]{:S(2)}) collective-permute-start(bf16[192,1536]{1,0:T(8,128)(2,1)} %refs_8_.1), channel_id=1, source_target_pairs={{0,4},{1,5},{2,6},{3,7},{4,8},{5,9},{6,10},{7,11},{8,12},{9,13},{1... | collective-permute-start | bytes 1769480 | tf_op jit(solution)/shard_map/ppermute | solution.py:424
  165.6 57.8 %collective-permute-start.17 = (bf16[192,1536]{1,0:T(8,128)(2,1)}, bf16[192,1536]{1,0:T(8,128)(2,1)}, u32[]{:S(2)}, u32[]{:S(2)}) collective-permute-start(bf16[192,1536]{1,0:T(8,128)(2,1)} %refs_8_.1), channel_id=1, source_target_pairs={{0,12},{1,13},{2,14},{3,15},{4,0},{5,1},{6,2},{7,3},{8,4},{9,5},{1... | collective-permute-start | bytes 1769480 | tf_op jit(solution)/shard_map/ppermute | solution.py:424
  215.4 12.6 %collective-permute-start.16 = (bf16[96,1536]{1,0:T(8,128)(2,1)}, bf16[96,1536]{1,0:T(8,128)(2,1)}, u32[]{:S(2)}, u32[]{:S(2)}) collective-permute-start(bf16[96,1536]{1,0:T(8,128)(2,1)} %slice.8), channel_id=1, source_target_pairs={{0,4},{1,5},{2,6},{3,7},{4,8},{5,9},{6,10},{7,11},{8,12},{9,13},{1... | collective-permute-start | bytes 884744 | tf_op jit(solution)/shard_map/ppermute | solution.py:424
  220.1 10.8 %collective-permute-start.9 = (bf16[64,1536]{1,0:T(8,128)(2,1)}, bf16[64,1536]{1,0:T(8,128)(2,1)S(1)}, u32[]{:S(2)}, u32[]{:S(2)}) collective-permute-start(bf16[64,1536]{1,0:T(8,128)(2,1)} %get-tuple-element.46.refs_0_), channel_id=1, source_target_pairs={{0,1},{1,2},{2,3},{3,0},{4,5},{5,6},{6,7},{7,4},{8,9},{9,10},{10,1... | collective-permute-start | bytes 589832 | tf_op jit(solution)/shard_map/ppermute | solution.py:424
  221.7 9.2 %collective-permute-start.12 = (bf16[64,1536]{1,0:T(8,128)(2,1)}, bf16[64,1536]{1,0:T(8,128)(2,1)S(1)}, u32[]{:S(2)}, u32[]{:S(2)}) collective-permute-start(bf16[64,1536]{1,0:T(8,128)(2,1)} %get-tuple-element.47.refs_1_), channel_id=1, source_target_pairs={{0,3},{1,0},{2,1},{3,2},{4,7},{5,4},{6,5},{7,6},{8,11},{9,8},{10,9... | collective-permute-start | bytes 589832 | tf_op jit(solution)/shard_map/ppermute | solution.py:424
  224.3 9.8 %collective-permute-start.18 = (bf16[96,1536]{1,0:T(8,128)(2,1)S(1)}, bf16[96,1536]{1,0:T(8,128)(2,1)S(1)}, u32[]{:S(2)}, u32[]{:S(2)}) collective-permute-start(bf16[96,1536]{1,0:T(8,128)(2,1)S(1)} %slice.9), channel_id=1, source_target_pairs={{0,12},{1,13},{2,14},{3,15},{4,0},{5,1},{6,2},{7,3},{8,4},{9,5},{1... | collective-permute-start | bytes 884744 | tf_op jit(solution)/shard_map/ppermute | solution.py:424
  227.6 9.1 %collective-permute-start.10 = (bf16[64,1536]{1,0:T(8,128)(2,1)}, bf16[64,1536]{1,0:T(8,128)(2,1)S(1)}, u32[]{:S(2)}, u32[]{:S(2)}) collective-permute-start(bf16[64,1536]{1,0:T(8,128)(2,1)} %get-tuple-element.47.refs_1_), channel_id=1, source_target_pairs={{0,1},{1,2},{2,3},{3,0},{4,5},{5,6},{6,7},{7,4},{8,9},{9,10},{10,1... | collective-permute-start | bytes 589832 | tf_op jit(solution)/shard_map/ppermute | solution.py:424
  228.0 8.8 %collective-permute-start.11 = (bf16[64,1536]{1,0:T(8,128)(2,1)}, bf16[64,1536]{1,0:T(8,128)(2,1)S(1)}, u32[]{:S(2)}, u32[]{:S(2)}) collective-permute-start(bf16[64,1536]{1,0:T(8,128)(2,1)} %get-tuple-element.46.refs_0_), channel_id=1, source_target_pairs={{0,3},{1,0},{2,1},{3,2},{4,7},{5,4},{6,5},{7,6},{8,11},{9,8},{10,9... | collective-permute-start | bytes 589832 | tf_op jit(solution)/shard_map/ppermute | solution.py:424
  230.9 8.1 %collective-permute-start.13 = (bf16[64,1536]{1,0:T(8,128)(2,1)S(1)}, bf16[64,1536]{1,0:T(8,128)(2,1)S(1)}, u32[]{:S(2)}, u32[]{:S(2)}) collective-permute-start(bf16[64,1536]{1,0:T(8,128)(2,1)S(1)} %collective-permute-done.9.refs_2_), channel_id=1, source_target_pairs={{0,1},{1,2},{2,3},{3,0},{4,5},{5,6},{6,7},{7,4},{8,9},{9,10},{10,1... | collective-permute-start | bytes 589832 | tf_op jit(solution)/shard_map/ppermute | solution.py:424
  230.9 8.1 %collective-permute-start.14 = (bf16[64,1536]{1,0:T(8,128)(2,1)S(1)}, bf16[64,1536]{1,0:T(8,128)(2,1)S(1)}, u32[]{:S(2)}, u32[]{:S(2)}) collective-permute-start(bf16[64,1536]{1,0:T(8,128)(2,1)S(1)} %collective-permute-done.12.refs_5_), channel_id=1, source_target_pairs={{0,3},{1,0},{2,1},{3,2},{4,7},{5,4},{6,5},{7,6},{8,11},{9,8},{10,9... | collective-permute-start | bytes 589832 | tf_op jit(solution)/shard_map/ppermute | solution.py:424
  239.0 1.1 copy-start.1
  247.0 15.2 %collective-permute-start.19 = (bf16[4,192,128]{2,1,0:T(8,128)(2,1)}, bf16[4,192,128]{2,1,0:T(8,128)(2,1)}, u32[]{:S(2)}, u32[]{:S(2)}) collective-permute-start(bf16[4,192,128]{2,1,0:T(8,128)(2,1)} %get-tuple-element.49), channel_id=1, source_target_pairs={{0,12},{1,13},{2,14},{3,15},{4,0},{5,1},{6,2},{7,3},{8,4},{9,5},{1... | collective-permute-start | bytes 589832 | tf_op jit(solution)/shard_map/ppermute | solution.py:424
  247.8 14.4 %collective-permute-start.20 = (bf16[4,192,128]{2,1,0:T(8,128)(2,1)}, bf16[4,192,128]{2,1,0:T(8,128)(2,1)}, u32[]{:S(2)}, u32[]{:S(2)}) collective-permute-start(bf16[4,192,128]{2,1,0:T(8,128)(2,1)} %get-tuple-element.50), channel_id=1, source_target_pairs={{0,8},{1,9},{2,10},{3,11},{4,12},{5,13},{6,14},{7,15},{8,0},{9,1},... | collective-permute-start | bytes 589832 | tf_op jit(solution)/shard_map/ppermute | solution.py:424
  247.9 14.3 %collective-permute-start.21 = (bf16[4,192,128]{2,1,0:T(8,128)(2,1)}, bf16[4,192,128]{2,1,0:T(8,128)(2,1)}, u32[]{:S(2)}, u32[]{:S(2)}) collective-permute-start(bf16[4,192,128]{2,1,0:T(8,128)(2,1)} %get-tuple-element.51), channel_id=1, source_target_pairs={{0,4},{1,5},{2,6},{3,7},{4,8},{5,9},{6,10},{7,11},{8,12},{9,13},{1... | collective-permute-start | bytes 589832 | tf_op jit(solution)/shard_map/ppermute | solution.py:424
  266.1 14.0 %all-to-all-start.3 = ((bf16[8,224,128]{2,1,0:T(8,128)(2,1)}), bf16[8,224,128]{2,1,0:T(8,128)(2,1)}, u32[]{:S(2)}, u32[]{:S(2)}) async-start(bf16[8,224,128]{2,1,0:T(8,128)(2,1)} %get-tuple-element.59), calls=%async_computation.3 | async-start | bytes 917504 | tf_op jit(solution)/shard_map/all_to_all | solution.py:564
  285.3 19.6 %all-to-all-start.4 = ((bf16[16,128,128]{2,1,0:T(8,128)(2,1)}), bf16[16,128,128]{2,1,0:T(8,128)(2,1)}, u32[]{:S(2)}, u32[]{:S(2)}) async-start(bf16[16,128,128]{2,1,0:T(8,128)(2,1)} %bitcast.19), calls=%async_computation.4 | async-start | bytes 1048576 | tf_op jit(solution)/shard_map/all_to_all | solution.py:596
  (5 other events, 4.2 us)

commit v2 on v0

--- a/solution.py
+++ b/solution.py
@@ -139,44 +139,43 @@
     out_ref[...] = dot(both, cat_buf[...], NN).astype(BF16)
 
 
-def combine_kernel(hi_ref, lo_ref, rows_ref, grad_ref, out_ref):
+def combine_kernel(hi_ref, lo_ref, rows_ref, grad_ref, out_ref, first_ref, second_ref):
     rows = rows_ref[...]
     total = dot(hi_ref[...], rows, NN) + dot(lo_ref[...], rows, NN)
-    out_ref[...] = (grad_ref[...].astype(F32) + total).astype(BF16)
-
-
-def project_kernel(place_ref, own_ref, other_ref, near_ref, up_ref, far_a_ref, far_b_ref, dn_ref, out_ref, toks_ref, buf_ref, sem):
-    core, z, y = place_ref[0], place_ref[1], place_ref[2]
-    rows = near_ref.shape[0]
+    resid = (grad_ref[...].astype(F32) + total).astype(BF16)
+    out_ref[...] = resid
+    half = first_ref.shape[0]
+    first_ref[...] = resid[:half]
+    second_ref[...] = resid[half:]
+
+
+def project_kernel(y_ref, *refs):
+    resids, projs, outs, toks_ref, buf_ref, sem = refs[:7], refs[7:12], refs[12:16], refs[16], refs[17], refs[18]
     copies = []
     at = 0
-    for k, source in enumerate((near_ref, up_ref, far_a_ref, far_b_ref, dn_ref)):
+    for k, source in enumerate(projs):
         n = source.shape[0]
         copies.append(pltpu.make_async_copy(source, buf_ref.at[pl.ds(at, n)], sem.at[k]))
         at += n
     for c in copies:
         c.start()
-    toks = own_ref.shape[0]
-    toks_ref[pl.ds(pl.multiple_of(core * toks, toks), toks), :] = own_ref[...]
-    toks_ref[pl.ds(pl.multiple_of((1 - core) * toks, toks), toks), :] = other_ref[...]
-    both = toks_ref[...]
-    part = out_ref.shape[2]
-    waits = ((0,), (1,), (2, 3), (4,))
-    for k, dz in enumerate((0, 3, 2, 1)):
-        for w in waits[k]:
+    toks = resids[0].shape[0]
+    half = toks // 2
+    for source, (dy, at) in zip(resids, ((0, 0), (3, 0), (3, half), (1, 0), (1, half), (2, 0), (2, half))):
+        place = ((y_ref[0] + dy) & 3) * toks + at
+        toks_ref[pl.ds(pl.multiple_of(place, half), source.shape[0]), :] = source[...]
+    line = toks_ref[...]
+    rows = outs[0].shape[1]
+    for k, waits in enumerate(((0,), (1,), (2, 3), (4,))):
+        for w in waits:
             copies[w].wait()
-        g = dot(buf_ref[k * rows : (k + 1) * rows, :], both, NT).astype(BF16)
-        for q, dy in enumerate((0, 3, 2, 1)):
-            head = ((z + dz) & 3) * 4 + ((y + dy) & 3)
-            for c in range(2):
-                out_ref[c, head] = g[q * part : (q + 1) * part, c * toks : (c + 1) * toks]
+        g = dot(buf_ref[k * rows : (k + 1) * rows, :], line, NT).astype(BF16)
+        for q in range(4):
+            outs[k][q] = g[:, q * toks : (q + 1) * toks]
 
 
 def block_grads(g_ref, k):
-    pieces = []
-    for j in (2 * k, 2 * k + 1):
-        pieces.append(jnp.concatenate([g_ref[0, j], g_ref[1, j]], axis=0))
-    return jnp.concatenate(pieces, axis=1)
+    return jnp.concatenate([g_ref[2 * k], g_ref[2 * k + 1]], axis=1)
 
 
 def head_rows(rows, heads, dim):
@@ -222,10 +221,12 @@
     tot_ref[...] = tot_ref[...] + block_sum
 
 
-def state_kernel(heads, g_ref, c_ref, ts_ref, bs_ref, tot_ref, fut_ref, pay_ref):
+def state_kernel(heads, z_ref, g0_ref, g1_ref, g2_ref, g3_ref, c_ref, ts_ref, bs_ref, tot_ref, fut_ref, pay_ref, g_ref):
     blocks, rows, lanes = fut_ref.shape
     dim = rows // heads
     n = c_ref.shape[0] // blocks
+    for dz, source in enumerate((g0_ref, g1_ref, g2_ref, g3_ref)):
+        g_ref[pl.ds(((z_ref[0] + dz) & 3) * 4, 4)] = source[...]
     states = []
     for k in range(blocks):
         at = slice(k * n, (k + 1) * n)
@@ -398,20 +399,13 @@
     recv_input = exchange(send_input)
     recv_grad = exchange(send_grad)
 
-    part = inner // 2
-
     def shift(rows, dz, dy):
         pairs = [(z * 4 + y, (z + dz) % 4 * 4 + (y + dy) % 4) for z in range(4) for y in range(4)]
         return lax.ppermute(rows, "head", pairs)
 
-    near = lax.dynamic_slice(out_proj, (core * part, 0), (part, width))
-    up, dn = shift(near, 0, 1), shift(near, 0, -1)
-    far_up = shift(up[: part // 2], 0, 1)
-    far_dn = shift(dn[part // 2 :], 0, -1)
-    line = jnp.concatenate([near, up, far_up, far_dn, dn], axis=0)
-    z_up, z_dn = shift(line, 1, 0), shift(line, -1, 0)
-    z_far_up = shift(z_up[: 2 * part], 1, 0)
-    z_far_dn = shift(z_dn[2 * part :], -1, 0)
+    proj_up, proj_dn = shift(out_proj, 1, 0), shift(out_proj, -1, 0)
+    proj_far_up = shift(proj_up[: inner // 2], 1, 0)
+    proj_far_dn = shift(proj_dn[inner // 2 :], -1, 0)
 
     flip = lambda i: blocks - 1 - i
     row_in = pl.BlockSpec((inner, BLOCK), lambda i: (0, flip(i)))
@@ -468,50 +462,81 @@
     )(recv_grad, factors, expert_down_t, expert_cat_t)
     returned = exchange(expert_rows)
 
-    resid_grad = pl.pallas_call(
+    resid_grad, first, second = pl.pallas_call(
         combine_kernel,
-        out_shape=sds((toks, width), BF16),
+        out_shape=(sds((toks, width), BF16),) + (sds((toks // 2, width), BF16),) * 2,
         compiler_params=params(),
         cost_estimate=cost(4 * slots * toks * width, 4 << 20),
         name="combine_rows",
     )(mix_hi, mix_lo, returned, out_grad)
-    resid_other = lax.ppermute(resid_grad, "core", [(0, 1), (1, 0)])
-    grad_all = pl.pallas_call(
+    up_first = shift(first, 0, 1)
+    dn_second = shift(second, 0, -1)
+    up_second = shift(second, 0, 1)
+    dn_first = shift(first, 0, -1)
+    far_first = shift(up_first, 0, 1)
+    far_second = shift(dn_second, 0, -1)
+    part_spec = whole((n_head // 4, inner, toks))
+    part_shape = sds((n_head // 4, inner, toks), BF16)
+    halves_spec = whole((toks // 2, width))
+    to_0, to_3, to_2, to_1 = pl.pallas_call(
         project_kernel,
         grid=(1,),
-        in_specs=[smem_spec] + [whole((toks, width))] * 2 + [any_spec] * 5,
-        out_specs=whole((2, n_head, part, toks)),
-        out_shape=sds((2, n_head, part, toks), BF16),
+        in_specs=[smem_spec, whole((toks, width))] + [halves_spec] * 6 + [any_spec] * 5,
+        out_specs=(part_spec,) * 4,
+        out_shape=(part_shape,) * 4,
         scratch_shapes=[
-            pltpu.VMEM((2 * toks, width), BF16),
-            pltpu.VMEM((n_head * part, width), BF16),
+            pltpu.VMEM((4 * toks, width), BF16),
+            pltpu.VMEM((4 * inner, width), BF16),
             pltpu.SemaphoreType.DMA((5,)),
         ],
-        compiler_params=params(),
-        cost_estimate=cost(4 * n_head * part * toks * width, 7 << 20),
+        compiler_params=params(60 << 20),
+        cost_estimate=cost(32 * inner * toks * width, 7 << 20),
         name="project_rows",
-    )(jnp.stack([core, head >> 2, head & 3]), resid_grad, resid_other, line, z_up, z_far_up, z_far_dn, z_dn)
-    grads = lax.all_to_all(
-        grad_all.reshape(2 * n_head, part, toks), ("core", "head"), split_axis=0, concat_axis=0, tiled=True
-    ).reshape(2, n_head, part, toks)
+    )(
+        (head & 3).reshape(1),
+        resid_grad,
+        up_first,
+        up_second,
+        dn_first,
+        dn_second,
+        far_first,
+        far_second,
+        out_proj,
+        proj_up,
+        proj_far_up,
+        proj_far_dn,
+        proj_dn,
+    )
+    from_2 = shift(to_2, 2, 0)
+    from_3 = shift(to_1, 1, 0)
+    from_1 = shift(to_3, -1, 0)
 
     pay_rows = inner + 32
-    future, payload = pl.pallas_call(
+    future, payload, grads = pl.pallas_call(
         functools.partial(state_kernel, heads),
-        out_shape=(sds((blocks, inner, state), F32), sds((n_seq, pay_rows, state), BF16)),
+        out_shape=(
+            sds((blocks, inner, state), F32),
+            sds((n_seq, pay_rows, state), BF16),
+            sds((n_head, inner, toks), BF16),
+        ),
         grid=(1,),
-        in_specs=[
-            whole((2, n_head, part, toks)),
+        in_specs=[smem_spec]
+        + [part_spec] * 4
+        + [
             whole((seq_rows, state)),
             whole((8, seq_rows)),
             whole((blocks, 8, state)),
             whole((8, state)),
         ],
-        out_specs=(whole((blocks, inner, state)), whole((n_seq, pay_rows, state))),
+        out_specs=(
+            whole((blocks, inner, state)),
+            whole((n_seq, pay_rows, state)),
+            whole((n_head, inner, toks)),
+        ),
         compiler_params=params(),
         cost_estimate=cost(1e9, 4 << 20),
         name="scan_state",
-    )(grads, c_proj, to_start, block_sum, total)
+    )((head >> 2).reshape(1), to_0, from_1, from_2, from_3, c_proj, to_start, block_sum, total)
     pays = lax.all_to_all(payload, seq_axes, split_axis=0, concat_axis=0, tiled=True)
     pair = 2
     spec = lambda *shape: pl.BlockSpec(shape, lambda i: (i,) + (0,) * (len(shape) - 1))
@@ -522,7 +547,7 @@
     part_x, part_b = pl.pallas_call(
         functools.partial(intra_kernel, heads),
         grid=(blocks // pair,),
-        in_specs=[smem_spec, w_spec, w_spec, pl.BlockSpec((2, pair * BLOCK // toks, part, toks), lambda i: (0, i, 0, 0))]
+        in_specs=[smem_spec, w_spec, w_spec, spec(pair * BLOCK // toks, inner, toks)]
         + [tok_in2] * 4
         + [row_82, tok_st2, tok_st2, spec(pair, inner, state)],
         out_specs=(row_in2, tok_st2),

time: 327 us -> 300 us (0.917)
  waiting for transfers between devices: 164 us -> 137 us
    ppermute x8 -> x13, waiting for transfers between devices: 78.4 us -> 53 us  [shift(): return lax.ppermute(rows, 'head', pairs)]
    ppermute x8 -> x13, starting transfers between devices: 11.8 us -> 17.2 us  [shift(): return lax.ppermute(rows, 'head', pairs)]
    all_to_all x1 -> x0, starting transfers between devices: 4.64 us -> none  [shards(): lax.all_to_all(grad_all.reshape(2 * n_head, part, toks), ('core', 'head')...]
  transfers between devices with their start and end apart: 24 -> 27, of which waited for: 13 -> 11; matrix products, arithmetic and copies ran while one was open for 1% -> 1% of each run, Pallas kernels for 15% -> 16%
where the time goes in v2:
time: 300 us; the launch traced here: 299 us
  waiting for transfers between devices  137 us (46%)
  Pallas kernels  77.8 us (26%)
  starting transfers between devices  76.9 us (26%)
  local copies, waits for them, and re-layouts  4.16 us (1%)
    ppermute x13, waiting for transfers between devices, shift(): return lax.ppermute(rows, 'head', pairs)  53 us
    ppermute x3, waiting for transfers between devices, shards(): y_halves.append(lax.ppermute(a, both, over_y))  40.1 us
    all_to_all x3, waiting for transfers between devices, exchange(): lax.all_to_all(shaped, both, split_axis=0, concat_axis=0, tiled=True)  35.9 us
    all_to_all x3, starting transfers between devices, exchange(): lax.all_to_all(shaped, both, split_axis=0, concat_axis=0, tiled=True)  28 us
    ppermute x13, starting transfers between devices, shift(): return lax.ppermute(rows, 'head', pairs)  17.2 us
    pallas_call x1, Pallas kernels, shards(): pl.pallas_call(prepare_kernel, grid=(blocks,), in_specs=[pl.BlockSpec((he...  13.1 us
    ppermute x3, starting transfers between devices, shards(): far_own.append(lax.ppermute(a, both, over_core))  12.2 us
    pallas_call x1, Pallas kernels, shards(): pl.pallas_call(back_kernel, grid=(slots // tile,), in_specs=[row_spec, ac...  10.8 us
  transfers between devices with their start and end apart: 27, of which 11 were waited for; matrix products, arithmetic and copies ran while one was open for 1% of the time, Pallas kernels for 16%

profile of v2, /device:TPU:0, one launch (start us, length us, event | category | flops | bytes accessed | tf_op | source)
XLA Modules:
  0.0 298.8 jit_solution(3072491909475312836)
XLA Ops:
  0.6 4.1 %select_rows.1 = (bf16[1024,128]{1,0:T(8,128)(2,1)}, bf16[1024,1536]{1,0:T(8,128)(2,1)}) custom-call(s32[6,128]{1,0:T(8,128)} %bitcast.21, bf16[128,1536]{1,0:T(8,128)(2,1)} %rows_ref.2), custom_call_target="tpu_custom_call" | custom-call | flops 402653184 | bytes 4194304 | tf_op jit(solution)/shard_map/select_rows/pallas_call | solution.py:380
  4.8 11.6 %all-to-all-start.1 = ((bf16[128,8,1536]{2,1,0:T(8,128)(2,1)}), bf16[128,8,1536]{2,1,0:T(8,128)(2,1)}, u32[]{:S(2)}, u32[]{:S(2)}) async-start(bf16[128,8,1536]{2,1,0:T(8,128)(2,1)} %bitcast.17), calls=%async_computation.1 | async-start | bytes 6291456 | tf_op jit(solution)/shard_map/all_to_all | solution.py:397
  16.4 4.1 %select_grads.1 = (bf16[1024,1536]{1,0:T(8,128)(2,1)}, bf16[128,1024]{1,0:T(8,128)(2,1)}, bf16[128,1024]{1,0:T(8,128)(2,1)}) custom-call(s32[6,128]{1,0:T(8,128)} %bitcast.22, f32[6,128]{1,0:T(8,128)} %bitcast.23, bf16[1024,128]{1,0:T(8,128)(2,1)} %get-tuple-element.39.sel_ref, bf16[128,1536]{1,0:T(8,128)(2,1)} %grad_ref.1), custom_call_target="tpu_custom_call" | custom-call | flops 402653184 | bytes 4194304 | tf_op jit(solution)/shard_map/select_grads/pallas_call | solution.py:387
  20.5 35.9 %all-to-all-done.1 = bf16[128,8,1536]{2,1,0:T(8,128)(2,1)} async-done(((bf16[128,8,1536]{2,1,0:T(8,128)(2,1)}), bf16[128,8,1536]{2,1,0:T(8,128)(2,1)}, u32[]{:S(2)}, u32[]{:S(2)}) %all-to-all-start.1) | async-done | bytes 3145760 | tf_op jit(solution)/shard_map/all_to_all | solution.py:397
  56.4 5.9 %all-to-all-start = ((bf16[128,8,1536]{2,1,0:T(8,128)(2,1)}), bf16[128,8,1536]{2,1,0:T(8,128)(2,1)}, u32[]{:S(2)}, u32[]{:S(2)}) async-start(bf16[128,8,1536]{2,1,0:T(8,128)(2,1)} %bitcast.15), calls=%async_computation | async-start | bytes 6291456 | tf_op jit(solution)/shard_map/all_to_all | solution.py:397
  63.6 3.3 %collective-permute-start.3 = (bf16[1,1536,256]{2,1,0:T(8,128)(2,1)S(1)}, bf16[1,1536,256]{2,1,0:T(8,128)(2,1)S(1)}, u32[]{:S(2)}, u32[]{:S(2)}) collective-permute-start(bf16[1,1536,256]{2,1,0:T(8,128)(2,1)S(1)} %copy-done), channel_id=1, source_target_pairs={{0,16},{2,18},{4,20},{6,22},{8,24},{10,26},{12,28},{14,30},{17,1},... | collective-permute-start | bytes 2359304 | tf_op jit(solution)/shard_map/ppermute | solution.py:363
  69.5 6.8 %collective-permute-start.5 = (bf16[1,1536,256]{2,1,0:T(8,128)(2,1)S(1)}, bf16[1,1536,256]{2,1,0:T(8,128)(2,1)}, u32[]{:S(2)}, u32[]{:S(2)}) collective-permute-start(bf16[1,1536,256]{2,1,0:T(8,128)(2,1)S(1)} %copy-done.1), channel_id=1, source_target_pairs={{0,16},{2,18},{4,20},{6,22},{8,24},{10,26},{12,28},{14,30},{17,1},... | collective-permute-start | bytes 2359304 | tf_op jit(solution)/shard_map/ppermute | solution.py:363
  76.3 28.9 %collective-permute-done.refs_1_ = bf16[1,1536,256]{2,1,0:T(8,128)(2,1)S(1)} collective-permute-done((bf16[1,1536,256]{2,1,0:T(8,128)(2,1)S(1)}, bf16[1,1536,256]{2,1,0:T(8,128)(2,1)S(1)}, u32[]{:S(2)}, u32[]{:S(2)}) %collective-permute-start) | collective-permute-done | bytes 786464 | tf_op jit(solution)/shard_map/ppermute | solution.py:361
  108.7 5.0 %collective-permute-done.1.refs_3_ = bf16[1,1536,256]{2,1,0:T(8,128)(2,1)} collective-permute-done((bf16[1,1536,256]{2,1,0:T(8,128)(2,1)S(1)}, bf16[1,1536,256]{2,1,0:T(8,128)(2,1)}, u32[]{:S(2)}, u32[]{:S(2)}) %collective-permute-start.1) | collective-permute-done | bytes 786464 | tf_op jit(solution)/shard_map/ppermute | solution.py:361
  113.7 2.2 collective-permute-start.6
  115.9 6.2 %collective-permute-done.2.refs_5_ = bf16[1,256,1536]{2,1,0:T(8,128)(2,1)} collective-permute-done((bf16[1,256,1536]{2,1,0:T(8,128)(2,1)S(1)}, bf16[1,256,1536]{2,1,0:T(8,128)(2,1)}, u32[]{:S(2)}, u32[]{:S(2)}) %collective-permute-start.2) | collective-permute-done | bytes 786464 | tf_op jit(solution)/shard_map/ppermute | solution.py:361
  122.2 2.2 collective-permute-start.8
  125.7 5.7 %expert_weights.1 = (bf16[1536,1024]{1,0:T(8,128)(2,1)}, bf16[1024,1536]{1,0:T(8,128)(2,1)}, bf16[1536,512]{1,0:T(8,128)(2,1)}) custom-call(s32[1]{0:T(128)} %bitcast.6.home_ref, bf16[1,1536,256]{2,1,0:T(8,128)(2,1)} %refs_0_.1, bf16[1,1536,256]{2,1,0:T(8,128)(2,1)} %copy-done.3, bf16[1,1536,256]{2,1,0:T(8,128)(2,1)} %refs_2_.1, ...), custom_call_target="tpu_custom_call" | custom-call | flops 1000000000 | bytes 12582912 | tf_op jit(solution)/shard_map/expert_weights/pallas_call | solution.py:369
  131.4 7.8 %expert_acts.1.act_ref = f32[1024,1024]{1,0:T(8,128)} custom-call(bf16[1024,1536]{1,0:T(8,128)(2,1)} %bitcast.5.x_ref, bf16[1536,1024]{1,0:T(8,128)(2,1)} %get-tuple-element.44.w_ref), custom_call_target="tpu_custom_call" | custom-call | flops 3221225472 | bytes 10485760 | tf_op jit(solution)/shard_map/expert_acts/pallas_call | solution.py:438
  139.2 10.8 %expert_back.1 = bf16[1024,1536]{1,0:T(8,128)(2,1)} custom-call(bf16[1024,1536]{1,0:T(8,128)(2,1)} %bitcast.3.g_ref, f32[1024,1024]{1,0:T(8,128)} %expert_acts.1.act_ref, bf16[1536,512]{1,0:T(8,128)(2,1)} %get-tuple-element.45.down_ref, bf16[1024,1536]{1,0:T(8,128)(2,1)} %get-tuple-element.46.cat_ref), custom_call_target="tpu_custom_call" | custom-call | flops 4831838208 | bytes 14680064 | tf_op jit(solution)/shard_map/expert_back/pallas_call | solution.py:448
  150.0 10.5 %all-to-all-start.2 = ((bf16[128,8,1536]{2,1,0:T(8,128)(2,1)}), bf16[128,8,1536]{2,1,0:T(8,128)(2,1)}, u32[]{:S(2)}, u32[]{:S(2)}) async-start(bf16[128,8,1536]{2,1,0:T(8,128)(2,1)} %bitcast.16), calls=%async_computation.2 | async-start | bytes 6291456 | tf_op jit(solution)/shard_map/all_to_all | solution.py:397
  161.6 2.2 collective-permute-start.17
  163.9 46.0 %collective-permute-done.15.refs_8_ = bf16[192,1536]{1,0:T(8,128)(2,1)S(1)} collective-permute-done((bf16[192,1536]{1,0:T(8,128)(2,1)}, bf16[192,1536]{1,0:T(8,128)(2,1)S(1)}, u32[]{:S(2)}, u32[]{:S(2)}) %collective-permute-start.15) | collective-permute-done | bytes 589856 | tf_op jit(solution)/shard_map/ppermute | solution.py:404
  211.5 3.9 %combine_rows.1 = (bf16[128,1536]{1,0:T(8,128)(2,1)}, bf16[64,1536]{1,0:T(8,128)(2,1)}, bf16[64,1536]{1,0:T(8,128)(2,1)}) custom-call(bf16[128,1024]{1,0:T(8,128)(2,1)} %get-tuple-element.40.hi_ref, bf16[128,1024]{1,0:T(8,128)(2,1)} %get-tuple-element.41.lo_ref, bf16[1024,1536]{1,0:T(8,128)(2,1)} %bitcast.8.rows_ref, bf16[128,1536]{1,0:T(8,128)(2,1)} %grad_ref.1), custom_call_target="tpu_custom_call" | custom-call | flops 805306368 | bytes 4194304 | tf_op jit(solution)/shard_map/combine_rows/pallas_call | solution.py:465
  219.6 3.3 %collective-permute-start.18 = (bf16[96,1536]{1,0:T(8,128)(2,1)S(1)}, bf16[96,1536]{1,0:T(8,128)(2,1)S(1)}, u32[]{:S(2)}, u32[]{:S(2)}) collective-permute-start(bf16[96,1536]{1,0:T(8,128)(2,1)S(1)} %slice.9), channel_id=1, source_target_pairs={{0,12},{1,13},{2,14},{3,15},{4,0},{5,1},{6,2},{7,3},{8,4},{9,5},{1... | collective-permute-start | bytes 884744 | tf_op jit(solution)/shard_map/ppermute | solution.py:404
  225.3 2.9 collective-permute-start.14
  228.2 2.4 collective-permute-done.11.refs_3_
  230.6 2.4 collective-permute-done.10.refs_2_
  235.9 5.9 %project_rows.1 = (bf16[4,192,128]{2,1,0:T(8,128)(2,1)}, bf16[4,192,128]{2,1,0:T(8,128)(2,1)}, bf16[4,192,128]{2,1,0:T(8,128)(2,1)}, bf16[4,192,128]{2,1,0:T(8,128)(2,1)}) custom-call(s32[1]{0:T(128)} %bitcast.11.y_ref, bf16[128,1536]{1,0:T(8,128)(2,1)} %get-tuple-element.36.refs_0_, bf16[64,1536]{1,0:T(8,128)(2,1)} %copy-done.8, ...), custom_call_target="tpu_custom_call" | custom-call | flops 1207959552 | bytes 7340032 | tf_op jit(solution)/shard_map/project_rows/pallas_call | solution.py:481
  243.9 13.1 %scan_prepare.1 = (bf16[8,3,256,256]{3,2,1,0:T(8,128)(2,1)}, bf16[8,3,256,256]{3,2,1,0:T(8,128)(2,1)}, f32[8,2048]{1,0:T(8,128)}, f32[8,2048]{1,0:T(8,128)}, f32...) custom-call(f32[3,2048]{1,0:T(4,128)} %d_ref.1, ...), custom_call_target="tpu_custom_call" | custom-call | flops 4000000000 | bytes 20971520 | tf_op jit(solution)/shard_map/scan_prepare/pallas_call | solution.py:421
  257.0 3.8 %scan_state.1 = (f32[8,192,128]{2,1,0:T(8,128)}, bf16[8,224,128]{2,1,0:T(8,128)(2,1)}, bf16[16,192,128]{2,1,0:T(8,128)(2,1)}) custom-call(s32[1]{0:T(128)} %bitcast.10.z_ref, bf16[4,192,128]{2,1,0:T(8,128)(2,1)} %get-tuple-element.50.g0_ref, bf16[4,192,128]{2,1,0:T(8,128)(2,1)} %collective-permute-done.19.g1_ref, ...), custom_call_target="tpu_custom_call" | custom-call | flops 1000000000 | bytes 4194304 | tf_op jit(solution)/shard_map/scan_state/pallas_call | solution.py:515
  260.8 4.2 %all-to-all-start.3 = ((bf16[8,224,128]{2,1,0:T(8,128)(2,1)}), bf16[8,224,128]{2,1,0:T(8,128)(2,1)}, u32[]{:S(2)}, u32[]{:S(2)}) async-start(bf16[8,224,128]{2,1,0:T(8,128)(2,1)} %get-tuple-element.57), calls=%async_computation.3 | async-start | bytes 917504 | tf_op jit(solution)/shard_map/all_to_all | solution.py:540
  265.1 9.5 %scan_intra.1 = (f32[192,2048]{1,0:T(8,128)}, f32[2048,128]{1,0:T(8,128)}) custom-call(f32[3]{0:T(128)} %skip_ref.1, bf16[8,3,256,256]{3,2,1,0:T(8,128)(2,1)} %get-tuple-element.60.wh_ref, bf16[8,3,256,256]{3,2,1,0:T(8,128)(2,1)} %get-tuple-element.61.wl_ref, bf16[16,192,128]{2,1,0:T(8,128)(2,1)} %get-tuple-element.62.g_ref, ...), custom_call_target="tpu_custom_call" | custom-call | flops 4000000000 | bytes 16777216 | tf_op jit(solution)/shard_map/scan_intra/pallas_call | solution.py:547
  274.8 4.6 %scan_finish_b.1 = (bf16[2048,128]{1,0:T(8,128)(2,1)}, bf16[192,128]{1,0:T(8,128)(2,1)}, bf16[192,128]{1,0:T(8,128)(2,1)}) custom-call(s32[1]{0:T(128)} %bitcast.9.seq_ref, bf16[8,224,128]{2,1,0:T(8,128)(2,1)} %all-to-all-done.3.pay_ref, bf16[2048,192]{1,0:T(8,128)(2,1)} %get-tuple-element.58.th_ref, bf16[2048,192]{1,0:T(8,128)(2,1)} %get-tuple-element.59.tl_ref, ...), custom_call_target="tpu_custom_call" | custom-call | flops 400000000 | bytes 6291456 | tf_op jit(solution)/shard_map/scan_finish_b/pallas_call | solution.py:559
  279.4 5.6 %all-to-all-start.4 = ((bf16[16,128,128]{2,1,0:T(8,128)(2,1)}), bf16[16,128,128]{2,1,0:T(8,128)(2,1)}, u32[]{:S(2)}, u32[]{:S(2)}) async-start(bf16[16,128,128]{2,1,0:T(8,128)(2,1)} %bitcast.19), calls=%async_computation.4 | async-start | bytes 1048576 | tf_op jit(solution)/shard_map/all_to_all | solution.py:569
  285.0 4.4 %scan_finish_x.1 = f32[192,2048]{1,0:T(8,128)} custom-call(bf16[192,128]{1,0:T(8,128)(2,1)} %get-tuple-element.70.hi_ref, bf16[192,128]{1,0:T(8,128)(2,1)} %get-tuple-element.71.lo_ref, f32[8,2048]{1,0:T(8,128)} %get-tuple-element.72.tt_ref, f32[2048,128]{1,0:T(8,128)} %b_ref.5, f32[192,2048]{1,0:T(8,128)} %get-tuple-element.73.gx_ref), custom_call_target="tpu_custom_call" | custom-call | flops 400000000 | bytes 6291456 | tf_op jit(solution)/shard_map/scan_finish_x/pallas_call | solution.py:572
  289.4 7.7 %all-to-all-done.4 = bf16[16,128,128]{2,1,0:T(8,128)(2,1)} async-done(((bf16[16,128,128]{2,1,0:T(8,128)(2,1)}), bf16[16,128,128]{2,1,0:T(8,128)(2,1)}, u32[]{:S(2)}, u32[]{:S(2)}) %all-to-all-start.4) | async-done | bytes 524320 | tf_op jit(solution)/shard_map/all_to_all | solution.py:569
  (65 shorter events, 24.9 us)
Async XLA Ops:
  4.8 51.7 %all-to-all-start.1 = ((bf16[128,8,1536]{2,1,0:T(8,128)(2,1)}), bf16[128,8,1536]{2,1,0:T(8,128)(2,1)}, u32[]{:S(2)}, u32[]{:S(2)}) async-start(bf16[128,8,1536]{2,1,0:T(8,128)(2,1)} %bitcast.17), calls=%async_computation.1 | async-start | bytes 6291456 | tf_op jit(solution)/shard_map/all_to_all | solution.py:397
  56.4 10.5 %copy-start.1 = (bf16[1,1536,256]{2,1,0:T(8,128)(2,1)S(1)}, bf16[1,1536,256]{2,1,0:T(8,128)(2,1)}, u32[]{:S(2)}) copy-start(bf16[1,1536,256]{2,1,0:T(8,128)(2,1)} %refs_2_.1) | copy-start | bytes 2359300
  56.4 11.8 %copy-start.2 = (bf16[1,256,1536]{2,1,0:T(8,128)(2,1)S(1)}, bf16[1,256,1536]{2,1,0:T(8,128)(2,1)}, u32[]{:S(2)}) copy-start(bf16[1,256,1536]{2,1,0:T(8,128)(2,1)} %refs_4_.1) | copy-start | bytes 2359300
  56.4 82.8 %all-to-all-start = ((bf16[128,8,1536]{2,1,0:T(8,128)(2,1)}), bf16[128,8,1536]{2,1,0:T(8,128)(2,1)}, u32[]{:S(2)}, u32[]{:S(2)}) async-start(bf16[128,8,1536]{2,1,0:T(8,128)(2,1)} %bitcast.15), calls=%async_computation | async-start | bytes 6291456 | tf_op jit(solution)/shard_map/all_to_all | solution.py:397
  62.3 42.9 %collective-permute-start = (bf16[1,1536,256]{2,1,0:T(8,128)(2,1)S(1)}, bf16[1,1536,256]{2,1,0:T(8,128)(2,1)S(1)}, u32[]{:S(2)}, u32[]{:S(2)}) collective-permute-start(bf16[1,1536,256]{2,1,0:T(8,128)(2,1)S(1)} %copy-done), channel_id=1, source_target_pairs={{1,0},{3,2},{5,4},{7,6},{9,8},{11,10},{13,12},{15,14},{16,17},{18,... | collective-permute-start | bytes 2359304 | tf_op jit(solution)/shard_map/ppermute | solution.py:361
  63.6 43.8 %collective-permute-start.3 = (bf16[1,1536,256]{2,1,0:T(8,128)(2,1)S(1)}, bf16[1,1536,256]{2,1,0:T(8,128)(2,1)S(1)}, u32[]{:S(2)}, u32[]{:S(2)}) collective-permute-start(bf16[1,1536,256]{2,1,0:T(8,128)(2,1)S(1)} %copy-done), channel_id=1, source_target_pairs={{0,16},{2,18},{4,20},{6,22},{8,24},{10,26},{12,28},{14,30},{17,1},... | collective-permute-start | bytes 2359304 | tf_op jit(solution)/shard_map/ppermute | solution.py:363
  66.9 46.8 %collective-permute-start.1 = (bf16[1,1536,256]{2,1,0:T(8,128)(2,1)S(1)}, bf16[1,1536,256]{2,1,0:T(8,128)(2,1)}, u32[]{:S(2)}, u32[]{:S(2)}) collective-permute-start(bf16[1,1536,256]{2,1,0:T(8,128)(2,1)S(1)} %copy-done.1), channel_id=1, source_target_pairs={{1,0},{3,2},{5,4},{7,6},{9,8},{11,10},{13,12},{15,14},{16,17},{18,... | collective-permute-start | bytes 2359304 | tf_op jit(solution)/shard_map/ppermute | solution.py:361
  68.2 53.9 %collective-permute-start.2 = (bf16[1,256,1536]{2,1,0:T(8,128)(2,1)S(1)}, bf16[1,256,1536]{2,1,0:T(8,128)(2,1)}, u32[]{:S(2)}, u32[]{:S(2)}) collective-permute-start(bf16[1,256,1536]{2,1,0:T(8,128)(2,1)S(1)} %copy-done.2), channel_id=1, source_target_pairs={{1,0},{3,2},{5,4},{7,6},{9,8},{11,10},{13,12},{15,14},{16,17},{18,... | collective-permute-start | bytes 2359304 | tf_op jit(solution)/shard_map/ppermute | solution.py:361
  69.5 54.8 %collective-permute-start.5 = (bf16[1,1536,256]{2,1,0:T(8,128)(2,1)S(1)}, bf16[1,1536,256]{2,1,0:T(8,128)(2,1)}, u32[]{:S(2)}, u32[]{:S(2)}) collective-permute-start(bf16[1,1536,256]{2,1,0:T(8,128)(2,1)S(1)} %copy-done.1), channel_id=1, source_target_pairs={{0,16},{2,18},{4,20},{6,22},{8,24},{10,26},{12,28},{14,30},{17,1},... | collective-permute-start | bytes 2359304 | tf_op jit(solution)/shard_map/ppermute | solution.py:363
  105.2 19.2 %copy-start.3 = (bf16[1,1536,256]{2,1,0:T(8,128)(2,1)}, bf16[1,1536,256]{2,1,0:T(8,128)(2,1)S(1)}, u32[]{:S(2)}) copy-start(bf16[1,1536,256]{2,1,0:T(8,128)(2,1)S(1)} %collective-permute-done.refs_1_) | copy-start | bytes 2359300
  105.2 19.2 %collective-permute-start.7 = (bf16[1,256,1536]{2,1,0:T(8,128)(2,1)S(1)}, bf16[1,256,1536]{2,1,0:T(8,128)(2,1)}, u32[]{:S(2)}, u32[]{:S(2)}) collective-permute-start(bf16[1,256,1536]{2,1,0:T(8,128)(2,1)S(1)} %copy-done.2), channel_id=1, source_target_pairs={{0,16},{2,18},{4,20},{6,22},{8,24},{10,26},{12,28},{14,30},{17,1},... | collective-permute-start | bytes 2359304 | tf_op jit(solution)/shard_map/ppermute | solution.py:363
  107.4 14.8 %copy-start.4 = (bf16[1,1536,256]{2,1,0:T(8,128)(2,1)}, bf16[1,1536,256]{2,1,0:T(8,128)(2,1)S(1)}, u32[]{:S(2)}) copy-start(bf16[1,1536,256]{2,1,0:T(8,128)(2,1)S(1)} %collective-permute-done.3.refs_6_) | copy-start | bytes 2359300
  107.4 17.0 %collective-permute-start.4 = (bf16[1,1536,256]{2,1,0:T(8,128)(2,1)S(1)}, bf16[1,1536,256]{2,1,0:T(8,128)(2,1)S(1)}, u32[]{:S(2)}, u32[]{:S(2)}) collective-permute-start(bf16[1,1536,256]{2,1,0:T(8,128)(2,1)S(1)} %collective-permute-done.refs_1_), channel_id=1, source_target_pairs={{0,16},{2,18},{4,20},{6,22},{8,24},{10,26},{12,28},{14,30},{17,1},... | collective-permute-start | bytes 2359304 | tf_op jit(solution)/shard_map/ppermute | solution.py:364
  113.7 11.6 %collective-permute-start.6 = (bf16[1,1536,256]{2,1,0:T(8,128)(2,1)}, bf16[1,1536,256]{2,1,0:T(8,128)(2,1)}, u32[]{:S(2)}, u32[]{:S(2)}) collective-permute-start(bf16[1,1536,256]{2,1,0:T(8,128)(2,1)} %collective-permute-done.1.refs_3_), channel_id=1, source_target_pairs={{0,16},{2,18},{4,20},{6,22},{8,24},{10,26},{12,28},{14,30},{17,1},... | collective-permute-start | bytes 2359304 | tf_op jit(solution)/shard_map/ppermute | solution.py:364
  122.2 3.5 %collective-permute-start.8 = (bf16[1,256,1536]{2,1,0:T(8,128)(2,1)}, bf16[1,256,1536]{2,1,0:T(8,128)(2,1)}, u32[]{:S(2)}, u32[]{:S(2)}) collective-permute-start(bf16[1,256,1536]{2,1,0:T(8,128)(2,1)} %collective-permute-done.2.refs_5_), channel_id=1, source_target_pairs={{0,16},{2,18},{4,20},{6,22},{8,24},{10,26},{12,28},{14,30},{17,1},... | collective-permute-start | bytes 2359304 | tf_op jit(solution)/shard_map/ppermute | solution.py:364
  150.0 61.4 %all-to-all-start.2 = ((bf16[128,8,1536]{2,1,0:T(8,128)(2,1)}), bf16[128,8,1536]{2,1,0:T(8,128)(2,1)}, u32[]{:S(2)}, u32[]{:S(2)}) async-start(bf16[128,8,1536]{2,1,0:T(8,128)(2,1)} %bitcast.16), calls=%async_computation.2 | async-start | bytes 6291456 | tf_op jit(solution)/shard_map/all_to_all | solution.py:397
  160.6 49.4 %collective-permute-start.15 = (bf16[192,1536]{1,0:T(8,128)(2,1)}, bf16[192,1536]{1,0:T(8,128)(2,1)S(1)}, u32[]{:S(2)}, u32[]{:S(2)}) collective-permute-start(bf16[192,1536]{1,0:T(8,128)(2,1)} %refs_7_.1), channel_id=1, source_target_pairs={{0,4},{1,5},{2,6},{3,7},{4,8},{5,9},{6,10},{7,11},{8,12},{9,13},{1... | collective-permute-start | bytes 1769480 | tf_op jit(solution)/shard_map/ppermute | solution.py:404
  161.6 57.0 %collective-permute-start.17 = (bf16[192,1536]{1,0:T(8,128)(2,1)}, bf16[192,1536]{1,0:T(8,128)(2,1)}, u32[]{:S(2)}, u32[]{:S(2)}) collective-permute-start(bf16[192,1536]{1,0:T(8,128)(2,1)} %refs_7_.1), channel_id=1, source_target_pairs={{0,12},{1,13},{2,14},{3,15},{4,0},{5,1},{6,2},{7,3},{8,4},{9,5},{1... | collective-permute-start | bytes 1769480 | tf_op jit(solution)/shard_map/ppermute | solution.py:404
  211.4 12.7 %collective-permute-start.16 = (bf16[96,1536]{1,0:T(8,128)(2,1)}, bf16[96,1536]{1,0:T(8,128)(2,1)}, u32[]{:S(2)}, u32[]{:S(2)}) collective-permute-start(bf16[96,1536]{1,0:T(8,128)(2,1)} %slice.8), channel_id=1, source_target_pairs={{0,4},{1,5},{2,6},{3,7},{4,8},{5,9},{6,10},{7,11},{8,12},{9,13},{1... | collective-permute-start | bytes 884744 | tf_op jit(solution)/shard_map/ppermute | solution.py:404
  215.4 9.6 %collective-permute-start.9 = (bf16[64,1536]{1,0:T(8,128)(2,1)}, bf16[64,1536]{1,0:T(8,128)(2,1)S(1)}, u32[]{:S(2)}, u32[]{:S(2)}) collective-permute-start(bf16[64,1536]{1,0:T(8,128)(2,1)} %get-tuple-element.48), channel_id=1, source_target_pairs={{0,1},{1,2},{2,3},{3,0},{4,5},{5,6},{6,7},{7,4},{8,9},{9,10},{10,1... | collective-permute-start | bytes 589832 | tf_op jit(solution)/shard_map/ppermute | solution.py:404
  216.9 8.4 %collective-permute-start.12 = (bf16[64,1536]{1,0:T(8,128)(2,1)}, bf16[64,1536]{1,0:T(8,128)(2,1)S(1)}, u32[]{:S(2)}, u32[]{:S(2)}) collective-permute-start(bf16[64,1536]{1,0:T(8,128)(2,1)} %get-tuple-element.49), channel_id=1, source_target_pairs={{0,3},{1,0},{2,1},{3,2},{4,7},{5,4},{6,5},{7,6},{8,11},{9,8},{10,9... | collective-permute-start | bytes 589832 | tf_op jit(solution)/shard_map/ppermute | solution.py:404
  219.6 8.6 %collective-permute-start.18 = (bf16[96,1536]{1,0:T(8,128)(2,1)S(1)}, bf16[96,1536]{1,0:T(8,128)(2,1)S(1)}, u32[]{:S(2)}, u32[]{:S(2)}) collective-permute-start(bf16[96,1536]{1,0:T(8,128)(2,1)S(1)} %slice.9), channel_id=1, source_target_pairs={{0,12},{1,13},{2,14},{3,15},{4,0},{5,1},{6,2},{7,3},{8,4},{9,5},{1... | collective-permute-start | bytes 884744 | tf_op jit(solution)/shard_map/ppermute | solution.py:404
  222.9 7.7 %collective-permute-start.11 = (bf16[64,1536]{1,0:T(8,128)(2,1)}, bf16[64,1536]{1,0:T(8,128)(2,1)S(1)}, u32[]{:S(2)}, u32[]{:S(2)}) collective-permute-start(bf16[64,1536]{1,0:T(8,128)(2,1)} %get-tuple-element.48), channel_id=1, source_target_pairs={{0,3},{1,0},{2,1},{3,2},{4,7},{5,4},{6,5},{7,6},{8,11},{9,8},{10,9... | collective-permute-start | bytes 589832 | tf_op jit(solution)/shard_map/ppermute | solution.py:404
  224.2 8.9 %collective-permute-start.10 = (bf16[64,1536]{1,0:T(8,128)(2,1)}, bf16[64,1536]{1,0:T(8,128)(2,1)S(1)}, u32[]{:S(2)}, u32[]{:S(2)}) collective-permute-start(bf16[64,1536]{1,0:T(8,128)(2,1)} %get-tuple-element.49), channel_id=1, source_target_pairs={{0,1},{1,2},{2,3},{3,0},{4,5},{5,6},{6,7},{7,4},{8,9},{9,10},{10,1... | collective-permute-start | bytes 589832 | tf_op jit(solution)/shard_map/ppermute | solution.py:404
  224.9 10.2 %copy-start.8 = (bf16[64,1536]{1,0:T(8,128)(2,1)}, bf16[64,1536]{1,0:T(8,128)(2,1)S(1)}, u32[]{:S(2)}) copy-start(bf16[64,1536]{1,0:T(8,128)(2,1)S(1)} %collective-permute-done.9.refs_1_) | copy-start | bytes 589828
  224.9 10.2 %collective-permute-start.13 = (bf16[64,1536]{1,0:T(8,128)(2,1)S(1)}, bf16[64,1536]{1,0:T(8,128)(2,1)S(1)}, u32[]{:S(2)}, u32[]{:S(2)}) collective-permute-start(bf16[64,1536]{1,0:T(8,128)(2,1)S(1)} %collective-permute-done.9.refs_1_), channel_id=1, source_target_pairs={{0,1},{1,2},{2,3},{3,0},{4,5},{5,6},{6,7},{7,4},{8,9},{9,10},{10,1... | collective-permute-start | bytes 589832 | tf_op jit(solution)/shard_map/ppermute | solution.py:404
  225.3 9.8 %collective-permute-start.14 = (bf16[64,1536]{1,0:T(8,128)(2,1)S(1)}, bf16[64,1536]{1,0:T(8,128)(2,1)S(1)}, u32[]{:S(2)}, u32[]{:S(2)}) collective-permute-start(bf16[64,1536]{1,0:T(8,128)(2,1)S(1)} %collective-permute-done.12.refs_4_), channel_id=1, source_target_pairs={{0,3},{1,0},{2,1},{3,2},{4,7},{5,4},{6,5},{7,6},{8,11},{9,8},{10,9... | collective-permute-start | bytes 589832 | tf_op jit(solution)/shard_map/ppermute | solution.py:404
  241.8 15.2 %collective-permute-start.19 = (bf16[4,192,128]{2,1,0:T(8,128)(2,1)}, bf16[4,192,128]{2,1,0:T(8,128)(2,1)}, u32[]{:S(2)}, u32[]{:S(2)}) collective-permute-start(bf16[4,192,128]{2,1,0:T(8,128)(2,1)} %get-tuple-element.51), channel_id=1, source_target_pairs={{0,12},{1,13},{2,14},{3,15},{4,0},{5,1},{6,2},{7,3},{8,4},{9,5},{1... | collective-permute-start | bytes 589832 | tf_op jit(solution)/shard_map/ppermute | solution.py:404
  242.4 14.6 %collective-permute-start.20 = (bf16[4,192,128]{2,1,0:T(8,128)(2,1)}, bf16[4,192,128]{2,1,0:T(8,128)(2,1)}, u32[]{:S(2)}, u32[]{:S(2)}) collective-permute-start(bf16[4,192,128]{2,1,0:T(8,128)(2,1)} %get-tuple-element.52), channel_id=1, source_target_pairs={{0,8},{1,9},{2,10},{3,11},{4,12},{5,13},{6,14},{7,15},{8,0},{9,1},... | collective-permute-start | bytes 589832 | tf_op jit(solution)/shard_map/ppermute | solution.py:404
  243.0 14.0 %collective-permute-start.21 = (bf16[4,192,128]{2,1,0:T(8,128)(2,1)}, bf16[4,192,128]{2,1,0:T(8,128)(2,1)}, u32[]{:S(2)}, u32[]{:S(2)}) collective-permute-start(bf16[4,192,128]{2,1,0:T(8,128)(2,1)} %get-tuple-element.53), channel_id=1, source_target_pairs={{0,4},{1,5},{2,6},{3,7},{4,8},{5,9},{6,10},{7,11},{8,12},{9,13},{1... | collective-permute-start | bytes 589832 | tf_op jit(solution)/shard_map/ppermute | solution.py:404
  260.8 13.9 %all-to-all-start.3 = ((bf16[8,224,128]{2,1,0:T(8,128)(2,1)}), bf16[8,224,128]{2,1,0:T(8,128)(2,1)}, u32[]{:S(2)}, u32[]{:S(2)}) async-start(bf16[8,224,128]{2,1,0:T(8,128)(2,1)} %get-tuple-element.57), calls=%async_computation.3 | async-start | bytes 917504 | tf_op jit(solution)/shard_map/all_to_all | solution.py:540
  279.4 17.6 %all-to-all-start.4 = ((bf16[16,128,128]{2,1,0:T(8,128)(2,1)}), bf16[16,128,128]{2,1,0:T(8,128)(2,1)}, u32[]{:S(2)}, u32[]{:S(2)}) async-start(bf16[16,128,128]{2,1,0:T(8,128)(2,1)} %bitcast.19), calls=%async_computation.4 | async-start | bytes 1048576 | tf_op jit(solution)/shard_map/all_to_all | solution.py:569
  (9 other events, 32.5 us)

commit v3 on v2

--- a/solution.py
+++ b/solution.py
@@ -78,15 +78,9 @@
     lo_ref[...] = lo
 
 
-def weights_kernel(home_ref, *refs):
-    own, far, (cat_ref, cat_t_ref, down_t_ref), bufs, sem = refs[:6], refs[6:12], refs[12:15], refs[15:17], refs[17]
-    half = bufs[0].shape[0]
-
+def copy_half(home_ref, own, far, targets, sem):
     def copies(sources):
-        targets = [cat_ref.at[:, pl.ds(k * half, half)] for k in range(4)] + list(bufs)
-        return [
-            pltpu.make_async_copy(s.at[0], t, sem.at[k]) for k, (s, t) in enumerate(zip(sources, targets))
-        ]
+        return [pltpu.make_async_copy(s.at[0], t, sem.at[k]) for k, (s, t) in enumerate(zip(sources, targets))]
 
     @pl.when(home_ref[0] == 1)
     def _():
@@ -98,12 +92,24 @@
         for c in copies(far):
             c.start()
 
-    for k, c in enumerate(copies(own)):
+    return copies(own)
+
+
+def weights_kernel(home_ref, *refs):
+    own, far, cat_ref, cat_t_ref, sem = refs[:4], refs[4:8], refs[8], refs[9], refs[10]
+    half = cat_ref.shape[1] // 4
+    targets = [cat_ref.at[:, pl.ds(k * half, half)] for k in range(4)]
+    for k, c in enumerate(copy_half(home_ref, own, far, targets, sem)):
         c.wait()
-        if k < 4:
-            cat_t_ref[k * half : (k + 1) * half, :] = cat_ref[:, k * half : (k + 1) * half].T
-        else:
-            down_t_ref[:, (k - 4) * half : (k - 3) * half] = bufs[k - 4][...].T
+        cat_t_ref[k * half : (k + 1) * half, :] = cat_ref[:, k * half : (k + 1) * half].T
+
+
+def down_kernel(home_ref, *refs):
+    own, far, down_t_ref, bufs, sem = refs[:2], refs[2:4], refs[4], refs[5:7], refs[7]
+    half = bufs[0].shape[0]
+    for k, c in enumerate(copy_half(home_ref, own, far, bufs, sem)):
+        c.wait()
+        down_t_ref[:, k * half : (k + 1) * half] = bufs[k][...].T
 
 
 def acts_kernel(x_ref, w_ref, out_ref):
@@ -361,20 +367,32 @@
         y_halves.append(lax.ppermute(a, both, over_y))
     for a in halves:
         far_own.append(lax.ppermute(a, both, over_core))
-    far_y = [lax.ppermute(a, both, over_core) for a in y_halves]
+    far_y = []
+    for a in y_halves:
+        far_y.append(lax.ppermute(a, both, over_core))
     own = [a for o, y in zip(halves, y_halves) for a in (o, y)]
     far = [a for o, y in zip(far_own, far_y) for a in (o, y)]
     _, width, half = gate_halves.shape
     hidden = 2 * half
-    expert_cat, expert_cat_t, expert_down_t = pl.pallas_call(
+    home_flag = home.astype(jnp.int32).reshape(1)
+    expert_cat, expert_cat_t = pl.pallas_call(
         weights_kernel,
-        in_specs=[smem_spec] + [any_spec] * 12,
-        out_shape=(sds((width, 2 * hidden), BF16), sds((2 * hidden, width), BF16), sds((width, hidden), BF16)),
-        scratch_shapes=[pltpu.VMEM((half, width), BF16)] * 2 + [pltpu.SemaphoreType.DMA((6,))],
-        compiler_params=params(),
-        cost_estimate=cost(1e9, 12 << 20),
+        in_specs=[smem_spec] + [any_spec] * 8,
+        out_shape=(sds((width, 2 * hidden), BF16), sds((2 * hidden, width), BF16)),
+        scratch_shapes=[pltpu.SemaphoreType.DMA((4,))],
+        compiler_params=params(),
+        cost_estimate=cost(1e9, 9 << 20),
         name="expert_weights",
-    )(home.astype(jnp.int32).reshape(1), *own, *far)
+    )(home_flag, *own[:4], *far[:4])
+    expert_down_t = pl.pallas_call(
+        down_kernel,
+        in_specs=[smem_spec] + [any_spec] * 4,
+        out_shape=sds((width, hidden), BF16),
+        scratch_shapes=[pltpu.VMEM((half, width), BF16)] * 2 + [pltpu.SemaphoreType.DMA((2,))],
+        compiler_params=params(),
+        cost_estimate=cost(1e9, 3 << 20),
+        name="expert_down",
+    )(home_flag, *own[4:], *far[4:])
 
     ids_t, gates_t = route_ids.T, route_gates.T
     sel, send_input = pl.pallas_call(
@@ -432,7 +450,7 @@
         name="scan_prepare",
     )(log_decay, b_proj, c_proj, ssd_x.T)
 
-    tile = 256
+    tile = 512
     row_spec = pl.BlockSpec((tile, width), lambda i: (i, 0))
     act_spec = pl.BlockSpec((tile, 2 * hidden), lambda i: (i, 0))
     factors = pl.pallas_call(
@@ -489,7 +507,7 @@
             pltpu.VMEM((4 * inner, width), BF16),
             pltpu.SemaphoreType.DMA((5,)),
         ],
-        compiler_params=params(60 << 20),
+        compiler_params=params(24 << 20),
         cost_estimate=cost(32 * inner * toks * width, 7 << 20),
         name="project_rows",
     )(
@@ -533,7 +551,7 @@
             whole((n_seq, pay_rows, state)),
             whole((n_head, inner, toks)),
         ),
-        compiler_params=params(),
+        compiler_params=params(66000000),
         cost_estimate=cost(1e9, 4 << 20),
         name="scan_state",
     )((head >> 2).reshape(1), to_0, from_1, from_2, from_3, c_proj, to_start, block_sum, total)

time: 300 us -> 304 us (1.013)
  waiting for transfers between devices: 137 us -> 142 us
    ppermute x3, waiting for transfers between devices: 40.1 us -> 45.2 us  [shards(): y_halves.append(lax.ppermute(a, both, over_y))]
    pallas_call x1 -> x2, Pallas kernels: 5.71 us -> 7.38 us  [the longest x1 4.58 us: shards(): pl.pallas_call(weights_kernel, in_specs=[smem_spec] + [any_spec] * 8, out...]
  transfers between devices with their start and end apart: 27 -> 27, of which waited for: 11 -> 10; matrix products, arithmetic and copies ran while one was open for 1% -> 1% of each run, Pallas kernels for 16% -> 17%
where the time goes in v3:
time: 304 us; the launch traced here: 302 us
  waiting for transfers between devices  142 us (47%)
  Pallas kernels  77.6 us (26%)
  starting transfers between devices  73.9 us (24%)
  local copies, waits for them, and re-layouts  6.21 us (2%)
    ppermute x13, waiting for transfers between devices, shift(): return lax.ppermute(rows, 'head', pairs)  53 us
    ppermute x3, waiting for transfers between devices, shards(): y_halves.append(lax.ppermute(a, both, over_y))  45.2 us
    all_to_all x3, waiting for transfers between devices, exchange(): lax.all_to_all(shaped, both, split_axis=0, concat_axis=0, tiled=True)  35.9 us
    all_to_all x3, starting transfers between devices, exchange(): lax.all_to_all(shaped, both, split_axis=0, concat_axis=0, tiled=True)  28 us
    ppermute x13, starting transfers between devices, shift(): return lax.ppermute(rows, 'head', pairs)  17.1 us
    pallas_call x1, Pallas kernels, shards(): pl.pallas_call(prepare_kernel, grid=(blocks,), in_specs=[pl.BlockSpec((he...  13.1 us
    pallas_call x1, Pallas kernels, shards(): pl.pallas_call(back_kernel, grid=(slots // tile,), in_specs=[row_spec, ac...  10.5 us
    pallas_call x1, Pallas kernels, shards(): pl.pallas_call(functools.partial(intra_kernel, heads), grid=(blocks // pa...  9.46 us
  transfers between devices with their start and end apart: 27, of which 10 were waited for; matrix products, arithmetic and copies ran while one was open for 1% of the time, Pallas kernels for 17%

profile of v3, /device:TPU:0, one launch (start us, length us, event | category | flops | bytes accessed | tf_op | source)
XLA Modules:
  0.0 302.3 jit_solution(14772849835559573562)
XLA Ops:
  0.6 4.0 %select_rows.1 = (bf16[1024,128]{1,0:T(8,128)(2,1)}, bf16[1024,1536]{1,0:T(8,128)(2,1)}) custom-call(s32[6,128]{1,0:T(8,128)} %bitcast.21, bf16[128,1536]{1,0:T(8,128)(2,1)} %rows_ref.2), custom_call_target="tpu_custom_call" | custom-call | flops 402653184 | bytes 4194304 | tf_op jit(solution)/shard_map/select_rows/pallas_call | solution.py:398
  4.7 11.6 %all-to-all-start.1 = ((bf16[128,8,1536]{2,1,0:T(8,128)(2,1)}), bf16[128,8,1536]{2,1,0:T(8,128)(2,1)}, u32[]{:S(2)}, u32[]{:S(2)}) async-start(bf16[128,8,1536]{2,1,0:T(8,128)(2,1)} %bitcast.17), calls=%async_computation.1 | async-start | bytes 6291456 | tf_op jit(solution)/shard_map/all_to_all | solution.py:415
  16.3 4.1 %select_grads.1 = (bf16[1024,1536]{1,0:T(8,128)(2,1)}, bf16[128,1024]{1,0:T(8,128)(2,1)}, bf16[128,1024]{1,0:T(8,128)(2,1)}) custom-call(s32[6,128]{1,0:T(8,128)} %bitcast.22, f32[6,128]{1,0:T(8,128)} %bitcast.23, bf16[1024,128]{1,0:T(8,128)(2,1)} %get-tuple-element.38.sel_ref, bf16[128,1536]{1,0:T(8,128)(2,1)} %grad_ref.1), custom_call_target="tpu_custom_call" | custom-call | flops 402653184 | bytes 4194304 | tf_op jit(solution)/shard_map/select_grads/pallas_call | solution.py:405
  20.5 35.9 %all-to-all-done.1 = bf16[128,8,1536]{2,1,0:T(8,128)(2,1)} async-done(((bf16[128,8,1536]{2,1,0:T(8,128)(2,1)}), bf16[128,8,1536]{2,1,0:T(8,128)(2,1)}, u32[]{:S(2)}, u32[]{:S(2)}) %all-to-all-start.1) | async-done | bytes 3145760 | tf_op jit(solution)/shard_map/all_to_all | solution.py:415
  56.4 5.9 %all-to-all-start = ((bf16[128,8,1536]{2,1,0:T(8,128)(2,1)}), bf16[128,8,1536]{2,1,0:T(8,128)(2,1)}, u32[]{:S(2)}, u32[]{:S(2)}) async-start(bf16[128,8,1536]{2,1,0:T(8,128)(2,1)} %bitcast.15), calls=%async_computation | async-start | bytes 6291456 | tf_op jit(solution)/shard_map/all_to_all | solution.py:415
  66.2 5.0 %collective-permute-start.7 = (bf16[1,256,1536]{2,1,0:T(8,128)(2,1)S(1)}, bf16[1,256,1536]{2,1,0:T(8,128)(2,1)S(1)}, u32[]{:S(2)}, u32[]{:S(2)}) collective-permute-start(bf16[1,256,1536]{2,1,0:T(8,128)(2,1)S(1)} %copy-done.4), channel_id=1, source_target_pairs={{0,16},{2,18},{4,20},{6,22},{8,24},{10,26},{12,28},{14,30},{17,1},... | collective-permute-start | bytes 2359304 | tf_op jit(solution)/shard_map/ppermute | solution.py:369
  71.2 33.9 %collective-permute-done.6.refs_1_ = bf16[1,256,1536]{2,1,0:T(8,128)(2,1)S(1)} collective-permute-done((bf16[1,256,1536]{2,1,0:T(8,128)(2,1)S(1)}, bf16[1,256,1536]{2,1,0:T(8,128)(2,1)S(1)}, u32[]{:S(2)}, u32[]{:S(2)}) %collective-permute-start.6) | collective-permute-done | bytes 786464 | tf_op jit(solution)/shard_map/ppermute | solution.py:367
  106.5 2.2 collective-permute-start.2
  108.7 5.0 %collective-permute-done.refs_1_ = bf16[1,1536,256]{2,1,0:T(8,128)(2,1)} collective-permute-done((bf16[1,1536,256]{2,1,0:T(8,128)(2,1)}, bf16[1,1536,256]{2,1,0:T(8,128)(2,1)}, u32[]{:S(2)}, u32[]{:S(2)}) %collective-permute-start) | collective-permute-done | bytes 786464 | tf_op jit(solution)/shard_map/ppermute | solution.py:367
  113.7 2.2 collective-permute-start.4
  115.8 6.3 %collective-permute-done.1.refs_3_ = bf16[1,1536,256]{2,1,0:T(8,128)(2,1)} collective-permute-done((bf16[1,1536,256]{2,1,0:T(8,128)(2,1)}, bf16[1,1536,256]{2,1,0:T(8,128)(2,1)}, u32[]{:S(2)}, u32[]{:S(2)}) %collective-permute-start.1) | collective-permute-done | bytes 786464 | tf_op jit(solution)/shard_map/ppermute | solution.py:367
  127.4 2.8 expert_down.1.down_ref
  130.2 4.6 %expert_weights.1 = (bf16[1536,1024]{1,0:T(8,128)(2,1)}, bf16[1024,1536]{1,0:T(8,128)(2,1)}) custom-call(s32[1]{0:T(128)} %bitcast.6.home_ref, bf16[1,1536,256]{2,1,0:T(8,128)(2,1)} %refs_0_.2, bf16[1,1536,256]{2,1,0:T(8,128)(2,1)} %collective-permute-done.refs_1_, bf16[1,1536,256]{2,1,0:T(8,128)(2,1)} %refs_2_.1, ...), custom_call_target="tpu_custom_call" | custom-call | flops 1000000000 | bytes 9437184 | tf_op jit(solution)/shard_map/expert_weights/pallas_call | solution.py:378
  134.8 7.6 %expert_acts.1.act_ref = f32[1024,1024]{1,0:T(8,128)} custom-call(bf16[1024,1536]{1,0:T(8,128)(2,1)} %bitcast.5.x_ref, bf16[1536,1024]{1,0:T(8,128)(2,1)} %get-tuple-element.43.w_ref), custom_call_target="tpu_custom_call" | custom-call | flops 3221225472 | bytes 10485760 | tf_op jit(solution)/shard_map/expert_acts/pallas_call | solution.py:456
  142.4 10.5 %expert_back.1 = bf16[1024,1536]{1,0:T(8,128)(2,1)} custom-call(bf16[1024,1536]{1,0:T(8,128)(2,1)} %bitcast.3.g_ref, f32[1024,1024]{1,0:T(8,128)} %expert_acts.1.act_ref, bf16[1536,512]{1,0:T(8,128)(2,1)} %expert_down.1.down_ref, bf16[1024,1536]{1,0:T(8,128)(2,1)} %get-tuple-element.44.cat_ref), custom_call_target="tpu_custom_call" | custom-call | flops 4831838208 | bytes 14680064 | tf_op jit(solution)/shard_map/expert_back/pallas_call | solution.py:466
  153.0 10.5 %all-to-all-start.2 = ((bf16[128,8,1536]{2,1,0:T(8,128)(2,1)}), bf16[128,8,1536]{2,1,0:T(8,128)(2,1)}, u32[]{:S(2)}, u32[]{:S(2)}) async-start(bf16[128,8,1536]{2,1,0:T(8,128)(2,1)} %bitcast.16), calls=%async_computation.2 | async-start | bytes 6291456 | tf_op jit(solution)/shard_map/all_to_all | solution.py:415
  164.6 2.2 collective-permute-start.17
  166.8 46.0 %collective-permute-done.15.refs_8_ = bf16[192,1536]{1,0:T(8,128)(2,1)S(1)} collective-permute-done((bf16[192,1536]{1,0:T(8,128)(2,1)}, bf16[192,1536]{1,0:T(8,128)(2,1)S(1)}, u32[]{:S(2)}, u32[]{:S(2)}) %collective-permute-start.15) | collective-permute-done | bytes 589856 | tf_op jit(solution)/shard_map/ppermute | solution.py:422
  214.4 4.0 %combine_rows.1 = (bf16[128,1536]{1,0:T(8,128)(2,1)}, bf16[64,1536]{1,0:T(8,128)(2,1)}, bf16[64,1536]{1,0:T(8,128)(2,1)}) custom-call(bf16[128,1024]{1,0:T(8,128)(2,1)} %get-tuple-element.39.hi_ref, bf16[128,1024]{1,0:T(8,128)(2,1)} %get-tuple-element.40.lo_ref, bf16[1024,1536]{1,0:T(8,128)(2,1)} %bitcast.8.rows_ref, bf16[128,1536]{1,0:T(8,128)(2,1)} %grad_ref.1), custom_call_target="tpu_custom_call" | custom-call | flops 805306368 | bytes 4194304 | tf_op jit(solution)/shard_map/combine_rows/pallas_call | solution.py:483
  222.6 3.3 %collective-permute-start.18 = (bf16[96,1536]{1,0:T(8,128)(2,1)S(1)}, bf16[96,1536]{1,0:T(8,128)(2,1)S(1)}, u32[]{:S(2)}, u32[]{:S(2)}) collective-permute-start(bf16[96,1536]{1,0:T(8,128)(2,1)S(1)} %slice.9), channel_id=1, source_target_pairs={{0,12},{1,13},{2,14},{3,15},{4,0},{5,1},{6,2},{7,3},{8,4},{9,5},{1... | collective-permute-start | bytes 884744 | tf_op jit(solution)/shard_map/ppermute | solution.py:422
  228.3 2.9 collective-permute-start.14
  231.2 2.4 collective-permute-done.11.refs_3_
  233.6 2.4 collective-permute-done.10.refs_2_
  240.2 4.4 %project_rows.1 = (bf16[4,192,128]{2,1,0:T(8,128)(2,1)S(1)}, bf16[4,192,128]{2,1,0:T(8,128)(2,1)}, bf16[4,192,128]{2,1,0:T(8,128)(2,1)}, bf16[4,192,128]{2,1,0:T(8,128)(2,1)}) custom-call(s32[1]{0:T(128)} %bitcast.11.y_ref, bf16[128,1536]{1,0:T(8,128)(2,1)S(1)} %copy-done.2, bf16[64,1536]{1,0:T(8,128)(2,1)S(1)} %collective-permute-done.9.refs_1_, ...), custom_call_target="tpu_custom_call" | custom-call | flops 1207959552 | bytes 7340032 | tf_op jit(solution)/shard_map/project_rows/pallas_call | solution.py:499
  247.3 13.1 %scan_prepare.1 = (bf16[8,3,256,256]{3,2,1,0:T(8,128)(2,1)}, bf16[8,3,256,256]{3,2,1,0:T(8,128)(2,1)}, f32[8,2048]{1,0:T(8,128)}, f32[8,2048]{1,0:T(8,128)}, f32...) custom-call(f32[3,2048]{1,0:T(4,128)} %d_ref.1, ...), custom_call_target="tpu_custom_call" | custom-call | flops 4000000000 | bytes 20971520 | tf_op jit(solution)/shard_map/scan_prepare/pallas_call | solution.py:439
  260.5 3.9 %scan_state.1 = (f32[8,192,128]{2,1,0:T(8,128)}, bf16[8,224,128]{2,1,0:T(8,128)(2,1)}, bf16[16,192,128]{2,1,0:T(8,128)(2,1)}) custom-call(s32[1]{0:T(128)} %bitcast.10.z_ref, bf16[4,192,128]{2,1,0:T(8,128)(2,1)} %copy-done.3, bf16[4,192,128]{2,1,0:T(8,128)(2,1)} %collective-permute-done.19.g1_ref, bf16[4,192,128]{2,1,0:T(8,128)(2,1)} %collective-permute-done.20.g2_ref, ...), custom_call_target="tpu_custom_call" | custom-call | flops 1000000000 | bytes 4194304 | tf_op jit(solution)/shard_map/scan_state/pallas_call | solution.py:533
  264.3 4.2 %all-to-all-start.3 = ((bf16[8,224,128]{2,1,0:T(8,128)(2,1)}), bf16[8,224,128]{2,1,0:T(8,128)(2,1)}, u32[]{:S(2)}, u32[]{:S(2)}) async-start(bf16[8,224,128]{2,1,0:T(8,128)(2,1)} %get-tuple-element.55), calls=%async_computation.3 | async-start | bytes 917504 | tf_op jit(solution)/shard_map/all_to_all | solution.py:558
  268.6 9.5 %scan_intra.1 = (f32[192,2048]{1,0:T(8,128)}, f32[2048,128]{1,0:T(8,128)}) custom-call(f32[3]{0:T(128)} %skip_ref.1, bf16[8,3,256,256]{3,2,1,0:T(8,128)(2,1)} %get-tuple-element.58.wh_ref, bf16[8,3,256,256]{3,2,1,0:T(8,128)(2,1)} %get-tuple-element.59.wl_ref, bf16[16,192,128]{2,1,0:T(8,128)(2,1)} %get-tuple-element.60.g_ref, ...), custom_call_target="tpu_custom_call" | custom-call | flops 4000000000 | bytes 16777216 | tf_op jit(solution)/shard_map/scan_intra/pallas_call | solution.py:565
  278.3 4.6 %scan_finish_b.1 = (bf16[2048,128]{1,0:T(8,128)(2,1)}, bf16[192,128]{1,0:T(8,128)(2,1)}, bf16[192,128]{1,0:T(8,128)(2,1)}) custom-call(s32[1]{0:T(128)} %bitcast.9.seq_ref, bf16[8,224,128]{2,1,0:T(8,128)(2,1)} %all-to-all-done.3.pay_ref, bf16[2048,192]{1,0:T(8,128)(2,1)} %get-tuple-element.56.th_ref, bf16[2048,192]{1,0:T(8,128)(2,1)} %get-tuple-element.57.tl_ref, ...), custom_call_target="tpu_custom_call" | custom-call | flops 400000000 | bytes 6291456 | tf_op jit(solution)/shard_map/scan_finish_b/pallas_call | solution.py:577
  282.9 5.6 %all-to-all-start.4 = ((bf16[16,128,128]{2,1,0:T(8,128)(2,1)}), bf16[16,128,128]{2,1,0:T(8,128)(2,1)}, u32[]{:S(2)}, u32[]{:S(2)}) async-start(bf16[16,128,128]{2,1,0:T(8,128)(2,1)} %bitcast.19), calls=%async_computation.4 | async-start | bytes 1048576 | tf_op jit(solution)/shard_map/all_to_all | solution.py:587
  288.5 4.4 %scan_finish_x.1 = f32[192,2048]{1,0:T(8,128)} custom-call(bf16[192,128]{1,0:T(8,128)(2,1)} %get-tuple-element.68.hi_ref, bf16[192,128]{1,0:T(8,128)(2,1)} %get-tuple-element.69.lo_ref, f32[8,2048]{1,0:T(8,128)} %get-tuple-element.70.tt_ref, f32[2048,128]{1,0:T(8,128)} %b_ref.5, f32[192,2048]{1,0:T(8,128)} %get-tuple-element.71.gx_ref), custom_call_target="tpu_custom_call" | custom-call | flops 400000000 | bytes 6291456 | tf_op jit(solution)/shard_map/scan_finish_x/pallas_call | solution.py:590
  292.9 7.6 %all-to-all-done.4 = bf16[16,128,128]{2,1,0:T(8,128)(2,1)} async-done(((bf16[16,128,128]{2,1,0:T(8,128)(2,1)}), bf16[16,128,128]{2,1,0:T(8,128)(2,1)}, u32[]{:S(2)}, u32[]{:S(2)}) %all-to-all-start.4) | async-done | bytes 524320 | tf_op jit(solution)/shard_map/all_to_all | solution.py:587
  (54 shorter events, 28.6 us)
Async XLA Ops:
  4.7 51.7 %all-to-all-start.1 = ((bf16[128,8,1536]{2,1,0:T(8,128)(2,1)}), bf16[128,8,1536]{2,1,0:T(8,128)(2,1)}, u32[]{:S(2)}, u32[]{:S(2)}) async-start(bf16[128,8,1536]{2,1,0:T(8,128)(2,1)} %bitcast.17), calls=%async_computation.1 | async-start | bytes 6291456 | tf_op jit(solution)/shard_map/all_to_all | solution.py:415
  56.4 5.9 %copy-start.4 = (bf16[1,256,1536]{2,1,0:T(8,128)(2,1)S(1)}, bf16[1,256,1536]{2,1,0:T(8,128)(2,1)}, u32[]{:S(2)}) copy-start(bf16[1,256,1536]{2,1,0:T(8,128)(2,1)} %refs_0_.3) | copy-start | bytes 2359300
  56.4 86.1 %all-to-all-start = ((bf16[128,8,1536]{2,1,0:T(8,128)(2,1)}), bf16[128,8,1536]{2,1,0:T(8,128)(2,1)}, u32[]{:S(2)}, u32[]{:S(2)}) async-start(bf16[128,8,1536]{2,1,0:T(8,128)(2,1)} %bitcast.15), calls=%async_computation | async-start | bytes 6291456 | tf_op jit(solution)/shard_map/all_to_all | solution.py:415
  62.3 42.9 %collective-permute-start.6 = (bf16[1,256,1536]{2,1,0:T(8,128)(2,1)S(1)}, bf16[1,256,1536]{2,1,0:T(8,128)(2,1)S(1)}, u32[]{:S(2)}, u32[]{:S(2)}) collective-permute-start(bf16[1,256,1536]{2,1,0:T(8,128)(2,1)S(1)} %copy-done.4), channel_id=1, source_target_pairs={{1,0},{3,2},{5,4},{7,6},{9,8},{11,10},{13,12},{15,14},{16,17},{18,... | collective-permute-start | bytes 2359304 | tf_op jit(solution)/shard_map/ppermute | solution.py:367
  63.6 50.1 %collective-permute-start = (bf16[1,1536,256]{2,1,0:T(8,128)(2,1)}, bf16[1,1536,256]{2,1,0:T(8,128)(2,1)}, u32[]{:S(2)}, u32[]{:S(2)}) collective-permute-start(bf16[1,1536,256]{2,1,0:T(8,128)(2,1)} %refs_0_.2), channel_id=1, source_target_pairs={{1,0},{3,2},{5,4},{7,6},{9,8},{11,10},{13,12},{15,14},{16,17},{18,... | collective-permute-start | bytes 2359304 | tf_op jit(solution)/shard_map/ppermute | solution.py:367
  64.9 57.2 %collective-permute-start.1 = (bf16[1,1536,256]{2,1,0:T(8,128)(2,1)}, bf16[1,1536,256]{2,1,0:T(8,128)(2,1)}, u32[]{:S(2)}, u32[]{:S(2)}) collective-permute-start(bf16[1,1536,256]{2,1,0:T(8,128)(2,1)} %refs_2_.1), channel_id=1, source_target_pairs={{1,0},{3,2},{5,4},{7,6},{9,8},{11,10},{13,12},{15,14},{16,17},{18,... | collective-permute-start | bytes 2359304 | tf_op jit(solution)/shard_map/ppermute | solution.py:367
  66.2 58.1 %collective-permute-start.7 = (bf16[1,256,1536]{2,1,0:T(8,128)(2,1)S(1)}, bf16[1,256,1536]{2,1,0:T(8,128)(2,1)S(1)}, u32[]{:S(2)}, u32[]{:S(2)}) collective-permute-start(bf16[1,256,1536]{2,1,0:T(8,128)(2,1)S(1)} %copy-done.4), channel_id=1, source_target_pairs={{0,16},{2,18},{4,20},{6,22},{8,24},{10,26},{12,28},{14,30},{17,1},... | collective-permute-start | bytes 2359304 | tf_op jit(solution)/shard_map/ppermute | solution.py:369
  105.1 19.1 %copy-start.5 = (bf16[1,256,1536]{2,1,0:T(8,128)(2,1)}, bf16[1,256,1536]{2,1,0:T(8,128)(2,1)S(1)}, u32[]{:S(2)}) copy-start(bf16[1,256,1536]{2,1,0:T(8,128)(2,1)S(1)} %collective-permute-done.6.refs_1_) | copy-start | bytes 2359300
  105.1 21.3 %collective-permute-start.8 = (bf16[1,256,1536]{2,1,0:T(8,128)(2,1)S(1)}, bf16[1,256,1536]{2,1,0:T(8,128)(2,1)S(1)}, u32[]{:S(2)}, u32[]{:S(2)}) collective-permute-start(bf16[1,256,1536]{2,1,0:T(8,128)(2,1)S(1)} %collective-permute-done.6.refs_1_), channel_id=1, source_target_pairs={{0,16},{2,18},{4,20},{6,22},{8,24},{10,26},{12,28},{14,30},{17,1},... | collective-permute-start | bytes 2359304 | tf_op jit(solution)/shard_map/ppermute | solution.py:372
  106.5 23.7 %collective-permute-start.2 = (bf16[1,1536,256]{2,1,0:T(8,128)(2,1)}, bf16[1,1536,256]{2,1,0:T(8,128)(2,1)}, u32[]{:S(2)}, u32[]{:S(2)}) collective-permute-start(bf16[1,1536,256]{2,1,0:T(8,128)(2,1)} %refs_0_.2), channel_id=1, source_target_pairs={{0,16},{2,18},{4,20},{6,22},{8,24},{10,26},{12,28},{14,30},{17,1},... | collective-permute-start | bytes 2359304 | tf_op jit(solution)/shard_map/ppermute | solution.py:369
  113.7 16.5 %collective-permute-start.4 = (bf16[1,1536,256]{2,1,0:T(8,128)(2,1)}, bf16[1,1536,256]{2,1,0:T(8,128)(2,1)}, u32[]{:S(2)}, u32[]{:S(2)}) collective-permute-start(bf16[1,1536,256]{2,1,0:T(8,128)(2,1)} %refs_2_.1), channel_id=1, source_target_pairs={{0,16},{2,18},{4,20},{6,22},{8,24},{10,26},{12,28},{14,30},{17,1},... | collective-permute-start | bytes 2359304 | tf_op jit(solution)/shard_map/ppermute | solution.py:369
  122.1 8.1 %collective-permute-start.3 = (bf16[1,1536,256]{2,1,0:T(8,128)(2,1)}, bf16[1,1536,256]{2,1,0:T(8,128)(2,1)}, u32[]{:S(2)}, u32[]{:S(2)}) collective-permute-start(bf16[1,1536,256]{2,1,0:T(8,128)(2,1)} %collective-permute-done.refs_1_), channel_id=1, source_target_pairs={{0,16},{2,18},{4,20},{6,22},{8,24},{10,26},{12,28},{14,30},{17,1},... | collective-permute-start | bytes 2359304 | tf_op jit(solution)/shard_map/ppermute | solution.py:372
  124.3 2.2 copy-start.6
  124.3 6.0 %collective-permute-start.5 = (bf16[1,1536,256]{2,1,0:T(8,128)(2,1)}, bf16[1,1536,256]{2,1,0:T(8,128)(2,1)}, u32[]{:S(2)}, u32[]{:S(2)}) collective-permute-start(bf16[1,1536,256]{2,1,0:T(8,128)(2,1)} %collective-permute-done.1.refs_3_), channel_id=1, source_target_pairs={{0,16},{2,18},{4,20},{6,22},{8,24},{10,26},{12,28},{14,30},{17,1},... | collective-permute-start | bytes 2359304 | tf_op jit(solution)/shard_map/ppermute | solution.py:372
  153.0 61.5 %all-to-all-start.2 = ((bf16[128,8,1536]{2,1,0:T(8,128)(2,1)}), bf16[128,8,1536]{2,1,0:T(8,128)(2,1)}, u32[]{:S(2)}, u32[]{:S(2)}) async-start(bf16[128,8,1536]{2,1,0:T(8,128)(2,1)} %bitcast.16), calls=%async_computation.2 | async-start | bytes 6291456 | tf_op jit(solution)/shard_map/all_to_all | solution.py:415
  163.5 49.4 %collective-permute-start.15 = (bf16[192,1536]{1,0:T(8,128)(2,1)}, bf16[192,1536]{1,0:T(8,128)(2,1)S(1)}, u32[]{:S(2)}, u32[]{:S(2)}) collective-permute-start(bf16[192,1536]{1,0:T(8,128)(2,1)} %refs_7_.1), channel_id=1, source_target_pairs={{0,4},{1,5},{2,6},{3,7},{4,8},{5,9},{6,10},{7,11},{8,12},{9,13},{1... | collective-permute-start | bytes 1769480 | tf_op jit(solution)/shard_map/ppermute | solution.py:422
  164.6 57.0 %collective-permute-start.17 = (bf16[192,1536]{1,0:T(8,128)(2,1)}, bf16[192,1536]{1,0:T(8,128)(2,1)}, u32[]{:S(2)}, u32[]{:S(2)}) collective-permute-start(bf16[192,1536]{1,0:T(8,128)(2,1)} %refs_7_.1), channel_id=1, source_target_pairs={{0,12},{1,13},{2,14},{3,15},{4,0},{5,1},{6,2},{7,3},{8,4},{9,5},{1... | collective-permute-start | bytes 1769480 | tf_op jit(solution)/shard_map/ppermute | solution.py:422
  214.4 12.7 %collective-permute-start.16 = (bf16[96,1536]{1,0:T(8,128)(2,1)}, bf16[96,1536]{1,0:T(8,128)(2,1)}, u32[]{:S(2)}, u32[]{:S(2)}) collective-permute-start(bf16[96,1536]{1,0:T(8,128)(2,1)} %slice.8), channel_id=1, source_target_pairs={{0,4},{1,5},{2,6},{3,7},{4,8},{5,9},{6,10},{7,11},{8,12},{9,13},{1... | collective-permute-start | bytes 884744 | tf_op jit(solution)/shard_map/ppermute | solution.py:422
  218.4 9.6 %collective-permute-start.9 = (bf16[64,1536]{1,0:T(8,128)(2,1)}, bf16[64,1536]{1,0:T(8,128)(2,1)S(1)}, u32[]{:S(2)}, u32[]{:S(2)}) collective-permute-start(bf16[64,1536]{1,0:T(8,128)(2,1)} %get-tuple-element.46), channel_id=1, source_target_pairs={{0,1},{1,2},{2,3},{3,0},{4,5},{5,6},{6,7},{7,4},{8,9},{9,10},{10,1... | collective-permute-start | bytes 589832 | tf_op jit(solution)/shard_map/ppermute | solution.py:422
  219.9 8.4 %collective-permute-start.12 = (bf16[64,1536]{1,0:T(8,128)(2,1)}, bf16[64,1536]{1,0:T(8,128)(2,1)S(1)}, u32[]{:S(2)}, u32[]{:S(2)}) collective-permute-start(bf16[64,1536]{1,0:T(8,128)(2,1)} %get-tuple-element.47), channel_id=1, source_target_pairs={{0,3},{1,0},{2,1},{3,2},{4,7},{5,4},{6,5},{7,6},{8,11},{9,8},{10,9... | collective-permute-start | bytes 589832 | tf_op jit(solution)/shard_map/ppermute | solution.py:422
  222.6 8.6 %collective-permute-start.18 = (bf16[96,1536]{1,0:T(8,128)(2,1)S(1)}, bf16[96,1536]{1,0:T(8,128)(2,1)S(1)}, u32[]{:S(2)}, u32[]{:S(2)}) collective-permute-start(bf16[96,1536]{1,0:T(8,128)(2,1)S(1)} %slice.9), channel_id=1, source_target_pairs={{0,12},{1,13},{2,14},{3,15},{4,0},{5,1},{6,2},{7,3},{8,4},{9,5},{1... | collective-permute-start | bytes 884744 | tf_op jit(solution)/shard_map/ppermute | solution.py:422
  225.9 7.7 %collective-permute-start.11 = (bf16[64,1536]{1,0:T(8,128)(2,1)}, bf16[64,1536]{1,0:T(8,128)(2,1)S(1)}, u32[]{:S(2)}, u32[]{:S(2)}) collective-permute-start(bf16[64,1536]{1,0:T(8,128)(2,1)} %get-tuple-element.46), channel_id=1, source_target_pairs={{0,3},{1,0},{2,1},{3,2},{4,7},{5,4},{6,5},{7,6},{8,11},{9,8},{10,9... | collective-permute-start | bytes 589832 | tf_op jit(solution)/shard_map/ppermute | solution.py:422
  227.2 8.9 %collective-permute-start.10 = (bf16[64,1536]{1,0:T(8,128)(2,1)}, bf16[64,1536]{1,0:T(8,128)(2,1)S(1)}, u32[]{:S(2)}, u32[]{:S(2)}) collective-permute-start(bf16[64,1536]{1,0:T(8,128)(2,1)} %get-tuple-element.47), channel_id=1, source_target_pairs={{0,1},{1,2},{2,3},{3,0},{4,5},{5,6},{6,7},{7,4},{8,9},{9,10},{10,1... | collective-permute-start | bytes 589832 | tf_op jit(solution)/shard_map/ppermute | solution.py:422
  228.0 10.2 %collective-permute-start.13 = (bf16[64,1536]{1,0:T(8,128)(2,1)S(1)}, bf16[64,1536]{1,0:T(8,128)(2,1)S(1)}, u32[]{:S(2)}, u32[]{:S(2)}) collective-permute-start(bf16[64,1536]{1,0:T(8,128)(2,1)S(1)} %collective-permute-done.9.refs_1_), channel_id=1, source_target_pairs={{0,1},{1,2},{2,3},{3,0},{4,5},{5,6},{6,7},{7,4},{8,9},{9,10},{10,1... | collective-permute-start | bytes 589832 | tf_op jit(solution)/shard_map/ppermute | solution.py:422
  228.3 9.8 %collective-permute-start.14 = (bf16[64,1536]{1,0:T(8,128)(2,1)S(1)}, bf16[64,1536]{1,0:T(8,128)(2,1)S(1)}, u32[]{:S(2)}, u32[]{:S(2)}) collective-permute-start(bf16[64,1536]{1,0:T(8,128)(2,1)S(1)} %collective-permute-done.12.refs_4_), channel_id=1, source_target_pairs={{0,3},{1,0},{2,1},{3,2},{4,7},{5,4},{6,5},{7,6},{8,11},{9,8},{10,9... | collective-permute-start | bytes 589832 | tf_op jit(solution)/shard_map/ppermute | solution.py:422
  238.1 1.1 copy-start.1
  239.2 1.0 copy-start.2
  245.3 15.2 %collective-permute-start.19 = (bf16[4,192,128]{2,1,0:T(8,128)(2,1)}, bf16[4,192,128]{2,1,0:T(8,128)(2,1)}, u32[]{:S(2)}, u32[]{:S(2)}) collective-permute-start(bf16[4,192,128]{2,1,0:T(8,128)(2,1)} %get-tuple-element.49), channel_id=1, source_target_pairs={{0,12},{1,13},{2,14},{3,15},{4,0},{5,1},{6,2},{7,3},{8,4},{9,5},{1... | collective-permute-start | bytes 589832 | tf_op jit(solution)/shard_map/ppermute | solution.py:422
  245.7 14.8 %collective-permute-start.20 = (bf16[4,192,128]{2,1,0:T(8,128)(2,1)}, bf16[4,192,128]{2,1,0:T(8,128)(2,1)}, u32[]{:S(2)}, u32[]{:S(2)}) collective-permute-start(bf16[4,192,128]{2,1,0:T(8,128)(2,1)} %get-tuple-element.50), channel_id=1, source_target_pairs={{0,8},{1,9},{2,10},{3,11},{4,12},{5,13},{6,14},{7,15},{8,0},{9,1},... | collective-permute-start | bytes 589832 | tf_op jit(solution)/shard_map/ppermute | solution.py:422
  246.4 14.0 %collective-permute-start.21 = (bf16[4,192,128]{2,1,0:T(8,128)(2,1)}, bf16[4,192,128]{2,1,0:T(8,128)(2,1)}, u32[]{:S(2)}, u32[]{:S(2)}) collective-permute-start(bf16[4,192,128]{2,1,0:T(8,128)(2,1)} %get-tuple-element.51), channel_id=1, source_target_pairs={{0,4},{1,5},{2,6},{3,7},{4,8},{5,9},{6,10},{7,11},{8,12},{9,13},{1... | collective-permute-start | bytes 589832 | tf_op jit(solution)/shard_map/ppermute | solution.py:422
  264.3 13.9 %all-to-all-start.3 = ((bf16[8,224,128]{2,1,0:T(8,128)(2,1)}), bf16[8,224,128]{2,1,0:T(8,128)(2,1)}, u32[]{:S(2)}, u32[]{:S(2)}) async-start(bf16[8,224,128]{2,1,0:T(8,128)(2,1)} %get-tuple-element.55), calls=%async_computation.3 | async-start | bytes 917504 | tf_op jit(solution)/shard_map/all_to_all | solution.py:558
  282.9 17.6 %all-to-all-start.4 = ((bf16[16,128,128]{2,1,0:T(8,128)(2,1)}), bf16[16,128,128]{2,1,0:T(8,128)(2,1)}, u32[]{:S(2)}, u32[]{:S(2)}) async-start(bf16[16,128,128]{2,1,0:T(8,128)(2,1)} %bitcast.19), calls=%async_computation.4 | async-start | bytes 1048576 | tf_op jit(solution)/shard_map/all_to_all | solution.py:587
  (3 other events, 2.4 us)

commit v4 on v3

--- a/solution.py
+++ b/solution.py
@@ -46,7 +46,18 @@
     return expert, 2 * slot + core
 
 
-def select_kernel(ids_ref, rows_ref, sel_ref, out_ref):
+def send_chunks(sel, rows, out_ref, buf_ref, sem):
+    n = buf_ref.shape[1]
+    copies = []
+    for k in range(buf_ref.shape[0]):
+        buf_ref[k] = dot(sel[k * n : (k + 1) * n], rows, NN).astype(BF16)
+        copies.append(pltpu.make_async_copy(buf_ref.at[k], out_ref.at[pl.ds(k * n, n)], sem.at[k]))
+        copies[-1].start()
+    for c in copies:
+        c.wait()
+
+
+def select_kernel(ids_ref, rows_ref, sel_ref, out_ref, buf_ref, sem):
     slots, toks = sel_ref.shape
     expert, rank = slot_experts(slots, toks)
     named = ids_ref[0:1, :] == expert
@@ -62,10 +73,10 @@
     before = dot(named.astype(BF16), earlier.astype(BF16), NN)
     sel = jnp.where(before == rank.astype(F32), named, 0.0).astype(BF16)
     sel_ref[...] = sel
-    out_ref[...] = dot(sel, rows_ref[...], NN).astype(BF16)
-
-
-def second_kernel(ids_ref, gates_ref, sel_ref, rows_ref, out_ref, hi_ref, lo_ref):
+    send_chunks(sel, rows_ref[...], out_ref, buf_ref, sem)
+
+
+def second_kernel(ids_ref, gates_ref, sel_ref, rows_ref, out_ref, mix_ref):
     slots, toks = sel_ref.shape
     out_ref[...] = dot(sel_ref[...], rows_ref[...], NN).astype(BF16)
     expert, _ = slot_experts(slots, toks)
@@ -73,9 +84,7 @@
     for k in range(ids_ref.shape[0]):
         gate = jnp.where(ids_ref[k : k + 1, :] == expert, gates_ref[k : k + 1, :], gate)
     mix = (gate * sel_ref[...].astype(F32)).T
-    hi, lo = split(mix)
-    hi_ref[...] = hi
-    lo_ref[...] = lo
+    mix_ref[:toks, :], mix_ref[toks:, :] = split(mix)
 
 
 def copy_half(home_ref, own, far, targets, sem):
@@ -104,14 +113,6 @@
         cat_t_ref[k * half : (k + 1) * half, :] = cat_ref[:, k * half : (k + 1) * half].T
 
 
-def down_kernel(home_ref, *refs):
-    own, far, down_t_ref, bufs, sem = refs[:2], refs[2:4], refs[4], refs[5:7], refs[7]
-    half = bufs[0].shape[0]
-    for k, c in enumerate(copy_half(home_ref, own, far, bufs, sem)):
-        c.wait()
-        down_t_ref[:, k * half : (k + 1) * half] = bufs[k][...].T
-
-
 def acts_kernel(x_ref, w_ref, out_ref):
     act = dot(x_ref[...], w_ref[...], NN)
     hidden = act.shape[1] // 2
@@ -121,18 +122,21 @@
     out_ref[:, hidden:] = gate * sig
 
 
-def back_kernel(g_ref, act_ref, down_ref, cat_ref, out_ref, down_buf, cat_buf, sem):
+def back_kernel(home_ref, g_ref, act_ref, cat_ref, *refs):
+    own, far, out_ref, down_buf, cat_buf, sem, cat_sem = refs[:2], refs[2:4], *refs[4:]
     first = pl.program_id(0) == 0
-    down_copy = pltpu.make_async_copy(down_ref, down_buf, sem.at[0])
-    cat_copy = pltpu.make_async_copy(cat_ref, cat_buf, sem.at[1])
+    half = down_buf.shape[0] // 2
+    targets = [down_buf.at[pl.ds(k * half, half)] for k in range(2)]
+    cat_copy = pltpu.make_async_copy(cat_ref, cat_buf, cat_sem)
 
     @pl.when(first)
     def _():
-        down_copy.start()
+        waits = copy_half(home_ref, own, far, targets, sem)
         cat_copy.start()
-        down_copy.wait()
-
-    grad = dot(g_ref[...], down_buf[...], NN)
+        for c in waits:
+            c.wait()
+
+    grad = dot(g_ref[...], down_buf[...], NT)
     hidden = grad.shape[1]
     both = jnp.concatenate(
         [(grad * act_ref[:, :hidden]).astype(BF16), (grad * act_ref[:, hidden:]).astype(BF16)], axis=1
@@ -145,14 +149,23 @@
     out_ref[...] = dot(both, cat_buf[...], NN).astype(BF16)
 
 
-def combine_kernel(hi_ref, lo_ref, rows_ref, grad_ref, out_ref, first_ref, second_ref):
-    rows = rows_ref[...]
-    total = dot(hi_ref[...], rows, NN) + dot(lo_ref[...], rows, NN)
-    resid = (grad_ref[...].astype(F32) + total).astype(BF16)
+def combine_kernel(mix_ref, rows_ref, grad_ref, out_ref, first_ref, second_ref, buf_ref, sem):
+    n = buf_ref.shape[1]
+    copies = [
+        pltpu.make_async_copy(rows_ref.at[pl.ds(k * n, n)], buf_ref.at[k], sem.at[k]) for k in range(buf_ref.shape[0])
+    ]
+    for c in copies:
+        c.start()
+    total = None
+    for k, c in enumerate(copies):
+        c.wait()
+        part = dot(mix_ref[:, k * n : (k + 1) * n], buf_ref[k], NN)
+        total = part if total is None else total + part
+    toks = out_ref.shape[0]
+    resid = (grad_ref[...].astype(F32) + total[:toks] + total[toks:]).astype(BF16)
     out_ref[...] = resid
-    half = first_ref.shape[0]
-    first_ref[...] = resid[:half]
-    second_ref[...] = resid[half:]
+    first_ref[...] = resid[: toks // 2]
+    second_ref[...] = resid[toks // 2 :]
 
 
 def project_kernel(y_ref, *refs):
@@ -172,12 +185,13 @@
         toks_ref[pl.ds(pl.multiple_of(place, half), source.shape[0]), :] = source[...]
     line = toks_ref[...]
     rows = outs[0].shape[1]
-    for k, waits in enumerate(((0,), (1,), (2, 3), (4,))):
+    for k, waits in enumerate(((0, 1), (2, 3, 4))):
         for w in waits:
             copies[w].wait()
-        g = dot(buf_ref[k * rows : (k + 1) * rows, :], line, NT).astype(BF16)
-        for q in range(4):
-            outs[k][q] = g[:, q * toks : (q + 1) * toks]
+        g = dot(buf_ref[2 * k * rows : 2 * (k + 1) * rows, :], line, NT).astype(BF16)
+        for i in range(2):
+            for q in range(4):
+                outs[2 * k + i][q] = g[i * rows : (i + 1) * rows, q * toks : (q + 1) * toks]
 
 
 def block_grads(g_ref, k):
@@ -239,7 +253,8 @@
         g = block_grads(g_ref, k).astype(F32)
         ghi, glo = split(g * head_rows(ts_ref[:, at], heads, dim))
         chi, clo = split(c_ref[at, :])
-        states.append(dot(ghi, chi, NN) + dot(ghi, clo, NN) + dot(glo, chi, NN))
+        wide = dot(ghi, jnp.concatenate([chi, clo], axis=1), NN)
+        states.append(wide[:, :lanes] + wide[:, lanes:] + dot(glo, chi, NN))
     carry = jnp.zeros((rows, lanes), F32)
     for k in reversed(range(blocks)):
         fut_ref[k] = carry
@@ -306,7 +321,8 @@
 
     hi = hi_ref[...]
     th = th_ref[...]
-    total = pb_ref[...] + dot(th, hi, NN) + dot(th, lo_ref[...], NN) + dot(tl_ref[...], hi, NN)
+    wide = dot(th, jnp.concatenate([hi, lo_ref[...]], axis=1), NN)
+    total = pb_ref[...] + wide[:, :lanes] + wide[:, lanes:] + dot(tl_ref[...], hi, NN)
     out_ref[...] = total.astype(out_ref.dtype)
 
 
@@ -384,27 +400,21 @@
         cost_estimate=cost(1e9, 9 << 20),
         name="expert_weights",
     )(home_flag, *own[:4], *far[:4])
-    expert_down_t = pl.pallas_call(
-        down_kernel,
-        in_specs=[smem_spec] + [any_spec] * 4,
-        out_shape=sds((width, hidden), BF16),
-        scratch_shapes=[pltpu.VMEM((half, width), BF16)] * 2 + [pltpu.SemaphoreType.DMA((2,))],
-        compiler_params=params(),
-        cost_estimate=cost(1e9, 3 << 20),
-        name="expert_down",
-    )(home_flag, *own[4:], *far[4:])
-
     ids_t, gates_t = route_ids.T, route_gates.T
     sel, send_input = pl.pallas_call(
         select_kernel,
+        grid=(1,),
+        in_specs=[whole(ids_t.shape), whole((toks, width))],
+        out_specs=(whole((slots, toks)), any_spec),
         out_shape=(sds((slots, toks), BF16), sds((slots, width), BF16)),
+        scratch_shapes=[pltpu.VMEM((4, slots // 4, width), BF16), pltpu.SemaphoreType.DMA((4,))],
         compiler_params=params(),
         cost_estimate=cost(2 * slots * toks * width, 4 << 20),
         name="select_rows",
     )(ids_t, moe_input)
-    send_grad, mix_hi, mix_lo = pl.pallas_call(
+    send_grad, mix = pl.pallas_call(
         second_kernel,
-        out_shape=(sds((slots, width), BF16), sds((toks, slots), BF16), sds((toks, slots), BF16)),
+        out_shape=(sds((slots, width), BF16), sds((2 * toks, slots), BF16)),
         compiler_params=params(),
         cost_estimate=cost(2 * slots * toks * width, 4 << 20),
         name="select_grads",
@@ -466,27 +476,32 @@
     expert_rows = pl.pallas_call(
         back_kernel,
         grid=(slots // tile,),
-        in_specs=[row_spec, act_spec, any_spec, any_spec],
+        in_specs=[smem_spec, row_spec, act_spec] + [any_spec] * 5,
         out_specs=row_spec,
         out_shape=sds((slots, width), BF16),
         scratch_shapes=[
-            pltpu.VMEM((width, hidden), BF16),
+            pltpu.VMEM((hidden, width), BF16),
             pltpu.VMEM((2 * hidden, width), BF16),
             pltpu.SemaphoreType.DMA((2,)),
+            pltpu.SemaphoreType.DMA,
         ],
         compiler_params=params(),
         cost_estimate=cost(6 * slots * width * hidden, 14 << 20),
         name="expert_back",
-    )(recv_grad, factors, expert_down_t, expert_cat_t)
+    )(home_flag, recv_grad, factors, expert_cat_t, *own[4:], *far[4:])
     returned = exchange(expert_rows)
 
     resid_grad, first, second = pl.pallas_call(
         combine_kernel,
+        grid=(1,),
+        in_specs=[whole((2 * toks, slots)), any_spec, whole((toks, width))],
+        out_specs=(whole((toks, width)),) + (whole((toks // 2, width)),) * 2,
         out_shape=(sds((toks, width), BF16),) + (sds((toks // 2, width), BF16),) * 2,
+        scratch_shapes=[pltpu.VMEM((2, slots // 2, width), BF16), pltpu.SemaphoreType.DMA((2,))],
         compiler_params=params(),
         cost_estimate=cost(4 * slots * toks * width, 4 << 20),
         name="combine_rows",
-    )(mix_hi, mix_lo, returned, out_grad)
+    )(mix, returned, out_grad)
     up_first = shift(first, 0, 1)
     dn_second = shift(second, 0, -1)
     up_second = shift(second, 0, 1)
@@ -576,9 +591,15 @@
     )(skip_gain, w_hi, w_lo, grads, x_hi, x_lo, e_hi, e_lo, to_end, b_proj, c_proj, future)
     partial_b, in_hi, in_lo = pl.pallas_call(
         functools.partial(finish_b_kernel, heads),
-        grid=(blocks // pair,),
-        in_specs=[smem_spec, whole((n_seq, pay_rows, state)), tok_in2, tok_in2, tok_st2],
-        out_specs=(tok_st2, whole((inner, state)), whole((inner, state))),
+        grid=(2,),
+        in_specs=[
+            smem_spec,
+            whole((n_seq, pay_rows, state)),
+            spec(seq_rows // 2, inner),
+            spec(seq_rows // 2, inner),
+            spec(seq_rows // 2, state),
+        ],
+        out_specs=(spec(seq_rows // 2, state), whole((inner, state)), whole((inner, state))),
         out_shape=(sds((seq_rows, state), BF16), sds((inner, state), BF16), sds((inner, state), BF16)),
         compiler_params=params(),
         cost_estimate=cost(4e8, 6 << 20),

time: 304 us -> 299 us (0.984)
  waiting for transfers between devices: 142 us -> 134 us
  starting transfers between devices: 73.9 us -> 80.8 us
  Pallas kernels: 77.6 us -> 74.5 us
    ppermute x3, waiting for transfers between devices: 45.2 us -> 39.3 us  [shards(): y_halves.append(lax.ppermute(a, both, over_y))]
    pallas_call x5 -> x4, Pallas kernels: 26 us -> 24 us  [the longest x1 11.5 us: shards(): pl.pallas_call(back_kernel, grid=(slots // tile,), in_specs=[smem_spec, r...]
  transfers between devices with their start and end apart: 27 -> 27, of which waited for: 10 -> 9; matrix products, arithmetic and copies ran while one was open for 1% -> 1% of each run, Pallas kernels for 17% -> 16%
where the time goes in v4:
time: 299 us; the launch traced here: 298 us
  waiting for transfers between devices  134 us (45%)
  starting transfers between devices  80.8 us (27%)
  Pallas kernels  74.5 us (25%)
  local copies, waits for them, and re-layouts  6.17 us (2%)
    ppermute x13, waiting for transfers between devices, shift(): return lax.ppermute(rows, 'head', pairs)  50.9 us
    ppermute x3, waiting for transfers between devices, shards(): y_halves.append(lax.ppermute(a, both, over_y))  39.3 us
    all_to_all x3, waiting for transfers between devices, exchange(): lax.all_to_all(shaped, both, split_axis=0, concat_axis=0, tiled=True)  35.9 us
    all_to_all x3, starting transfers between devices, exchange(): lax.all_to_all(shaped, both, split_axis=0, concat_axis=0, tiled=True)  28 us
    ppermute x13, starting transfers between devices, shift(): return lax.ppermute(rows, 'head', pairs)  18.4 us
    pallas_call x1, Pallas kernels, shards(): pl.pallas_call(prepare_kernel, grid=(blocks,), in_specs=[pl.BlockSpec((he...  13.1 us
    pallas_call x1, Pallas kernels, shards(): pl.pallas_call(back_kernel, grid=(slots // tile,), in_specs=[smem_spec, r...  11.5 us
    ppermute x3, starting transfers between devices, shards(): far_own.append(lax.ppermute(a, both, over_core))  11.4 us
  transfers between devices with their start and end apart: 27, of which 9 were waited for; matrix products, arithmetic and copies ran while one was open for 1% of the time, Pallas kernels for 16%

profile of v4, /device:TPU:0, one launch (start us, length us, event | category | flops | bytes accessed | tf_op | source)
XLA Modules:
  0.0 298.0 jit_solution(12450048198301900053)
XLA Ops:
  0.6 4.3 %select_rows.1 = (bf16[1024,128]{1,0:T(8,128)(2,1)}, bf16[1024,1536]{1,0:T(8,128)(2,1)}) custom-call(s32[6,128]{1,0:T(8,128)} %bitcast.21, bf16[128,1536]{1,0:T(8,128)(2,1)} %rows_ref.2), custom_call_target="tpu_custom_call" | custom-call | flops 402653184 | bytes 4194304 | tf_op jit(solution)/shard_map/select_rows/pallas_call | solution.py:404
  4.9 11.6 %all-to-all-start.1 = ((bf16[128,8,1536]{2,1,0:T(8,128)(2,1)}), bf16[128,8,1536]{2,1,0:T(8,128)(2,1)}, u32[]{:S(2)}, u32[]{:S(2)}) async-start(bf16[128,8,1536]{2,1,0:T(8,128)(2,1)} %bitcast.17), calls=%async_computation.1 | async-start | bytes 6291456 | tf_op jit(solution)/shard_map/all_to_all | solution.py:425
  16.6 4.2 %select_grads.1 = (bf16[1024,1536]{1,0:T(8,128)(2,1)}, bf16[256,1024]{1,0:T(8,128)(2,1)}) custom-call(s32[6,128]{1,0:T(8,128)} %bitcast.22, f32[6,128]{1,0:T(8,128)} %bitcast.23, bf16[1024,128]{1,0:T(8,128)(2,1)} %get-tuple-element.37.sel_ref, bf16[128,1536]{1,0:T(8,128)(2,1)} %grad_ref.1), custom_call_target="tpu_custom_call" | custom-call | flops 402653184 | bytes 4194304 | tf_op jit(solution)/shard_map/select_grads/pallas_call | solution.py:415
  20.7 35.9 %all-to-all-done.1 = bf16[128,8,1536]{2,1,0:T(8,128)(2,1)} async-done(((bf16[128,8,1536]{2,1,0:T(8,128)(2,1)}), bf16[128,8,1536]{2,1,0:T(8,128)(2,1)}, u32[]{:S(2)}, u32[]{:S(2)}) %all-to-all-start.1) | async-done | bytes 3145760 | tf_op jit(solution)/shard_map/all_to_all | solution.py:425
  56.6 5.9 %all-to-all-start = ((bf16[128,8,1536]{2,1,0:T(8,128)(2,1)}), bf16[128,8,1536]{2,1,0:T(8,128)(2,1)}, u32[]{:S(2)}, u32[]{:S(2)}) async-start(bf16[128,8,1536]{2,1,0:T(8,128)(2,1)} %bitcast.15), calls=%async_computation | async-start | bytes 6291456 | tf_op jit(solution)/shard_map/all_to_all | solution.py:425
  65.1 3.3 %collective-permute-start.2 = (bf16[1,1536,256]{2,1,0:T(8,128)(2,1)S(1)}, bf16[1,1536,256]{2,1,0:T(8,128)(2,1)S(1)}, u32[]{:S(2)}, u32[]{:S(2)}) collective-permute-start(bf16[1,1536,256]{2,1,0:T(8,128)(2,1)S(1)} %copy-done.4), channel_id=1, source_target_pairs={{0,16},{2,18},{4,20},{6,22},{8,24},{10,26},{12,28},{14,30},{17,1},... | collective-permute-start | bytes 2359304 | tf_op jit(solution)/shard_map/ppermute | solution.py:385
  69.7 5.9 %collective-permute-start.4 = (bf16[1,1536,256]{2,1,0:T(8,128)(2,1)S(1)}, bf16[1,1536,256]{2,1,0:T(8,128)(2,1)}, u32[]{:S(2)}, u32[]{:S(2)}) collective-permute-start(bf16[1,1536,256]{2,1,0:T(8,128)(2,1)S(1)} %copy-done.5), channel_id=1, source_target_pairs={{0,16},{2,18},{4,20},{6,22},{8,24},{10,26},{12,28},{14,30},{17,1},... | collective-permute-start | bytes 2359304 | tf_op jit(solution)/shard_map/ppermute | solution.py:385
  75.6 29.8 %collective-permute-done.refs_1_ = bf16[1,1536,256]{2,1,0:T(8,128)(2,1)S(1)} collective-permute-done((bf16[1,1536,256]{2,1,0:T(8,128)(2,1)S(1)}, bf16[1,1536,256]{2,1,0:T(8,128)(2,1)S(1)}, u32[]{:S(2)}, u32[]{:S(2)}) %collective-permute-start) | collective-permute-done | bytes 786464 | tf_op jit(solution)/shard_map/ppermute | solution.py:383
  105.4 2.2 collective-permute-start.3
  107.6 6.2 %collective-permute-done.1.refs_3_ = bf16[1,1536,256]{2,1,0:T(8,128)(2,1)S(1)} collective-permute-done((bf16[1,1536,256]{2,1,0:T(8,128)(2,1)S(1)}, bf16[1,1536,256]{2,1,0:T(8,128)(2,1)S(1)}, u32[]{:S(2)}, u32[]{:S(2)}) %collective-permute-start.1) | collective-permute-done | bytes 786464 | tf_op jit(solution)/shard_map/ppermute | solution.py:383
  119.0 3.3 %collective-permute-done.6.refs_1_ = bf16[1,256,1536]{2,1,0:T(8,128)(2,1)} collective-permute-done((bf16[1,256,1536]{2,1,0:T(8,128)(2,1)}, bf16[1,256,1536]{2,1,0:T(8,128)(2,1)}, u32[]{:S(2)}, u32[]{:S(2)}) %collective-permute-start.6) | collective-permute-done | bytes 786464 | tf_op jit(solution)/shard_map/ppermute | solution.py:383
  122.3 2.2 collective-permute-start.8
  124.6 4.6 %expert_weights.1 = (bf16[1536,1024]{1,0:T(8,128)(2,1)}, bf16[1024,1536]{1,0:T(8,128)(2,1)}) custom-call(s32[1]{0:T(128)} %bitcast.2.home_ref, bf16[1,1536,256]{2,1,0:T(8,128)(2,1)} %refs_0_.2, bf16[1,1536,256]{2,1,0:T(8,128)(2,1)} %copy-done.6, bf16[1,1536,256]{2,1,0:T(8,128)(2,1)} %refs_2_.1, bf16[1,1536,256]{2,1,0:T(8,128)(2,1)} %copy-done.7, ...), custom_call_target="tpu_custom_call" | custom-call | flops 1000000000 | bytes 9437184 | tf_op jit(solution)/shard_map/expert_weights/pallas_call | solution.py:394
  129.2 7.6 %expert_acts.1.act_ref = f32[1024,1024]{1,0:T(8,128)} custom-call(bf16[1024,1536]{1,0:T(8,128)(2,1)} %bitcast.6.x_ref, bf16[1536,1024]{1,0:T(8,128)(2,1)} %get-tuple-element.41.w_ref), custom_call_target="tpu_custom_call" | custom-call | flops 3221225472 | bytes 10485760 | tf_op jit(solution)/shard_map/expert_acts/pallas_call | solution.py:466
  136.8 11.5 %expert_back.1 = bf16[1024,1536]{1,0:T(8,128)(2,1)} custom-call(s32[1]{0:T(128)} %bitcast.2.home_ref, bf16[1024,1536]{1,0:T(8,128)(2,1)} %bitcast.4.g_ref, f32[1024,1024]{1,0:T(8,128)} %expert_acts.1.act_ref, bf16[1024,1536]{1,0:T(8,128)(2,1)} %get-tuple-element.42.cat_ref, bf16[1,256,1536]{2,1,0:T(8,128)(2,1)} %refs_0_.3, ...), custom_call_target="tpu_custom_call" | custom-call | flops 4831838208 | bytes 14680064 | tf_op jit(solution)/shard_map/expert_back/pallas_call | solution.py:476
  148.3 10.5 %all-to-all-start.2 = ((bf16[128,8,1536]{2,1,0:T(8,128)(2,1)}), bf16[128,8,1536]{2,1,0:T(8,128)(2,1)}, u32[]{:S(2)}, u32[]{:S(2)}) async-start(bf16[128,8,1536]{2,1,0:T(8,128)(2,1)} %bitcast.16), calls=%async_computation.2 | async-start | bytes 6291456 | tf_op jit(solution)/shard_map/all_to_all | solution.py:425
  159.9 2.2 collective-permute-start.17
  162.1 46.0 %collective-permute-done.15.refs_8_ = bf16[192,1536]{1,0:T(8,128)(2,1)S(1)} collective-permute-done((bf16[192,1536]{1,0:T(8,128)(2,1)}, bf16[192,1536]{1,0:T(8,128)(2,1)S(1)}, u32[]{:S(2)}, u32[]{:S(2)}) %collective-permute-start.15) | collective-permute-done | bytes 589856 | tf_op jit(solution)/shard_map/ppermute | solution.py:432
  209.8 4.9 %combine_rows.1 = (bf16[128,1536]{1,0:T(8,128)(2,1)}, bf16[64,1536]{1,0:T(8,128)(2,1)}, bf16[64,1536]{1,0:T(8,128)(2,1)}) custom-call(bf16[256,1024]{1,0:T(8,128)(2,1)} %get-tuple-element.38.mix_ref, bf16[1024,1536]{1,0:T(8,128)(2,1)} %bitcast.8.rows_ref, bf16[128,1536]{1,0:T(8,128)(2,1)} %grad_ref.1), custom_call_target="tpu_custom_call" | custom-call | flops 805306368 | bytes 4194304 | tf_op jit(solution)/shard_map/combine_rows/pallas_call | solution.py:494
  218.9 3.3 %collective-permute-start.18 = (bf16[96,1536]{1,0:T(8,128)(2,1)S(1)}, bf16[96,1536]{1,0:T(8,128)(2,1)S(1)}, u32[]{:S(2)}, u32[]{:S(2)}) collective-permute-start(bf16[96,1536]{1,0:T(8,128)(2,1)S(1)} %slice.9), channel_id=1, source_target_pairs={{0,12},{1,13},{2,14},{3,15},{4,0},{5,1},{6,2},{7,3},{8,4},{9,5},{1... | collective-permute-start | bytes 884744 | tf_op jit(solution)/shard_map/ppermute | solution.py:432
  222.6 2.9 collective-permute-start.11
  225.5 3.2 %collective-permute-start.14 = (bf16[64,1536]{1,0:T(8,128)(2,1)S(1)}, bf16[64,1536]{1,0:T(8,128)(2,1)S(1)}, u32[]{:S(2)}, u32[]{:S(2)}) collective-permute-start(bf16[64,1536]{1,0:T(8,128)(2,1)S(1)} %collective-permute-done.12.refs_4_), channel_id=1, source_target_pairs={{0,3},{1,0},{2,1},{3,2},{4,7},{5,4},{6,5},{7,6},{8,11},{9,8},{10,9... | collective-permute-start | bytes 589832 | tf_op jit(solution)/shard_map/ppermute | solution.py:432
  228.7 2.6 collective-permute-done.10.refs_2_
  235.6 3.4 %project_rows.1 = (bf16[4,192,128]{2,1,0:T(8,128)(2,1)S(1)}, bf16[4,192,128]{2,1,0:T(8,128)(2,1)}, bf16[4,192,128]{2,1,0:T(8,128)(2,1)}, bf16[4,192,128]{2,1,0:T(8,128)(2,1)}) custom-call(s32[1]{0:T(128)} %bitcast.11.y_ref, bf16[128,1536]{1,0:T(8,128)(2,1)S(1)} %copy-done.2, bf16[64,1536]{1,0:T(8,128)(2,1)S(1)} %collective-permute-done.9.refs_1_, ...), custom_call_target="tpu_custom_call" | custom-call | flops 1207959552 | bytes 7340032 | tf_op jit(solution)/shard_map/project_rows/pallas_call | solution.py:514
  241.8 13.1 %scan_prepare.1 = (bf16[8,3,256,256]{3,2,1,0:T(8,128)(2,1)}, bf16[8,3,256,256]{3,2,1,0:T(8,128)(2,1)}, f32[8,2048]{1,0:T(8,128)}, f32[8,2048]{1,0:T(8,128)}, f32...) custom-call(f32[3,2048]{1,0:T(4,128)} %d_ref.1, ...), custom_call_target="tpu_custom_call" | custom-call | flops 4000000000 | bytes 20971520 | tf_op jit(solution)/shard_map/scan_prepare/pallas_call | solution.py:449
  254.9 3.7 %scan_state.1 = (f32[8,192,128]{2,1,0:T(8,128)}, bf16[8,224,128]{2,1,0:T(8,128)(2,1)}, bf16[16,192,128]{2,1,0:T(8,128)(2,1)}) custom-call(s32[1]{0:T(128)} %bitcast.10.z_ref, bf16[4,192,128]{2,1,0:T(8,128)(2,1)} %copy-done.3, bf16[4,192,128]{2,1,0:T(8,128)(2,1)} %collective-permute-done.19.g1_ref, bf16[4,192,128]{2,1,0:T(8,128)(2,1)} %collective-permute-done.20.g2_ref, ...), custom_call_target="tpu_custom_call" | custom-call | flops 1000000000 | bytes 4194304 | tf_op jit(solution)/shard_map/scan_state/pallas_call | solution.py:548
  258.6 4.3 %all-to-all-start.3 = ((bf16[8,224,128]{2,1,0:T(8,128)(2,1)}), bf16[8,224,128]{2,1,0:T(8,128)(2,1)}, u32[]{:S(2)}, u32[]{:S(2)}) async-start(bf16[8,224,128]{2,1,0:T(8,128)(2,1)} %get-tuple-element.53), calls=%async_computation.3 | async-start | bytes 917504 | tf_op jit(solution)/shard_map/all_to_all | solution.py:573
  262.9 9.5 %scan_intra.1 = (f32[192,2048]{1,0:T(8,128)}, f32[2048,128]{1,0:T(8,128)}) custom-call(f32[3]{0:T(128)} %skip_ref.1, bf16[8,3,256,256]{3,2,1,0:T(8,128)(2,1)} %get-tuple-element.56.wh_ref, bf16[8,3,256,256]{3,2,1,0:T(8,128)(2,1)} %get-tuple-element.57.wl_ref, bf16[16,192,128]{2,1,0:T(8,128)(2,1)} %get-tuple-element.58.g_ref, ...), custom_call_target="tpu_custom_call" | custom-call | flops 4000000000 | bytes 16777216 | tf_op jit(solution)/shard_map/scan_intra/pallas_call | solution.py:580
  272.6 3.4 %scan_finish_b.1 = (bf16[2048,128]{1,0:T(8,128)(2,1)}, bf16[192,128]{1,0:T(8,128)(2,1)}, bf16[192,128]{1,0:T(8,128)(2,1)}) custom-call(s32[1]{0:T(128)} %bitcast.9.seq_ref, bf16[8,224,128]{2,1,0:T(8,128)(2,1)} %all-to-all-done.3.pay_ref, bf16[2048,192]{1,0:T(8,128)(2,1)} %get-tuple-element.54.th_ref, bf16[2048,192]{1,0:T(8,128)(2,1)} %get-tuple-element.55.tl_ref, ...), custom_call_target="tpu_custom_call" | custom-call | flops 400000000 | bytes 6291456 | tf_op jit(solution)/shard_map/scan_finish_b/pallas_call | solution.py:592
  276.0 8.2 %all-to-all-start.4 = ((bf16[16,128,128]{2,1,0:T(8,128)(2,1)}), bf16[16,128,128]{2,1,0:T(8,128)(2,1)}, u32[]{:S(2)}, u32[]{:S(2)}) async-start(bf16[16,128,128]{2,1,0:T(8,128)(2,1)} %bitcast.19), calls=%async_computation.4 | async-start | bytes 1048576 | tf_op jit(solution)/shard_map/all_to_all | solution.py:608
  284.2 4.4 %scan_finish_x.1 = f32[192,2048]{1,0:T(8,128)} custom-call(bf16[192,128]{1,0:T(8,128)(2,1)} %get-tuple-element.66.hi_ref, bf16[192,128]{1,0:T(8,128)(2,1)} %get-tuple-element.67.lo_ref, f32[8,2048]{1,0:T(8,128)} %get-tuple-element.68.tt_ref, f32[2048,128]{1,0:T(8,128)} %b_ref.5, f32[192,2048]{1,0:T(8,128)} %get-tuple-element.69.gx_ref), custom_call_target="tpu_custom_call" | custom-call | flops 400000000 | bytes 6291456 | tf_op jit(solution)/shard_map/scan_finish_x/pallas_call | solution.py:611
  288.6 7.7 %all-to-all-done.4 = bf16[16,128,128]{2,1,0:T(8,128)(2,1)} async-done(((bf16[16,128,128]{2,1,0:T(8,128)(2,1)}), bf16[16,128,128]{2,1,0:T(8,128)(2,1)}, u32[]{:S(2)}, u32[]{:S(2)}) %all-to-all-start.4) | async-done | bytes 524320 | tf_op jit(solution)/shard_map/all_to_all | solution.py:608
  (55 shorter events, 25.4 us)
Async XLA Ops:
  4.9 51.7 %all-to-all-start.1 = ((bf16[128,8,1536]{2,1,0:T(8,128)(2,1)}), bf16[128,8,1536]{2,1,0:T(8,128)(2,1)}, u32[]{:S(2)}, u32[]{:S(2)}) async-start(bf16[128,8,1536]{2,1,0:T(8,128)(2,1)} %bitcast.17), calls=%async_computation.1 | async-start | bytes 6291456 | tf_op jit(solution)/shard_map/all_to_all | solution.py:425
  56.6 5.9 %copy-start.4 = (bf16[1,1536,256]{2,1,0:T(8,128)(2,1)S(1)}, bf16[1,1536,256]{2,1,0:T(8,128)(2,1)}, u32[]{:S(2)}) copy-start(bf16[1,1536,256]{2,1,0:T(8,128)(2,1)} %refs_0_.2) | copy-start | bytes 2359300
  56.6 7.2 %copy-start.5 = (bf16[1,1536,256]{2,1,0:T(8,128)(2,1)S(1)}, bf16[1,1536,256]{2,1,0:T(8,128)(2,1)}, u32[]{:S(2)}) copy-start(bf16[1,1536,256]{2,1,0:T(8,128)(2,1)} %refs_2_.1) | copy-start | bytes 2359300
  56.6 80.2 %all-to-all-start = ((bf16[128,8,1536]{2,1,0:T(8,128)(2,1)}), bf16[128,8,1536]{2,1,0:T(8,128)(2,1)}, u32[]{:S(2)}, u32[]{:S(2)}) async-start(bf16[128,8,1536]{2,1,0:T(8,128)(2,1)} %bitcast.15), calls=%async_computation | async-start | bytes 6291456 | tf_op jit(solution)/shard_map/all_to_all | solution.py:425
  62.5 42.9 %collective-permute-start = (bf16[1,1536,256]{2,1,0:T(8,128)(2,1)S(1)}, bf16[1,1536,256]{2,1,0:T(8,128)(2,1)S(1)}, u32[]{:S(2)}, u32[]{:S(2)}) collective-permute-start(bf16[1,1536,256]{2,1,0:T(8,128)(2,1)S(1)} %copy-done.4), channel_id=1, source_target_pairs={{1,0},{3,2},{5,4},{7,6},{9,8},{11,10},{13,12},{15,14},{16,17},{18,... | collective-permute-start | bytes 2359304 | tf_op jit(solution)/shard_map/ppermute | solution.py:383
  63.8 50.0 %collective-permute-start.1 = (bf16[1,1536,256]{2,1,0:T(8,128)(2,1)S(1)}, bf16[1,1536,256]{2,1,0:T(8,128)(2,1)S(1)}, u32[]{:S(2)}, u32[]{:S(2)}) collective-permute-start(bf16[1,1536,256]{2,1,0:T(8,128)(2,1)S(1)} %copy-done.5), channel_id=1, source_target_pairs={{1,0},{3,2},{5,4},{7,6},{9,8},{11,10},{13,12},{15,14},{16,17},{18,... | collective-permute-start | bytes 2359304 | tf_op jit(solution)/shard_map/ppermute | solution.py:383
  65.1 50.9 %collective-permute-start.2 = (bf16[1,1536,256]{2,1,0:T(8,128)(2,1)S(1)}, bf16[1,1536,256]{2,1,0:T(8,128)(2,1)S(1)}, u32[]{:S(2)}, u32[]{:S(2)}) collective-permute-start(bf16[1,1536,256]{2,1,0:T(8,128)(2,1)S(1)} %copy-done.4), channel_id=1, source_target_pairs={{0,16},{2,18},{4,20},{6,22},{8,24},{10,26},{12,28},{14,30},{17,1},... | collective-permute-start | bytes 2359304 | tf_op jit(solution)/shard_map/ppermute | solution.py:385
  68.4 53.9 %collective-permute-start.6 = (bf16[1,256,1536]{2,1,0:T(8,128)(2,1)}, bf16[1,256,1536]{2,1,0:T(8,128)(2,1)}, u32[]{:S(2)}, u32[]{:S(2)}) collective-permute-start(bf16[1,256,1536]{2,1,0:T(8,128)(2,1)} %refs_0_.3), channel_id=1, source_target_pairs={{1,0},{3,2},{5,4},{7,6},{9,8},{11,10},{13,12},{15,14},{16,17},{18,... | collective-permute-start | bytes 2359304 | tf_op jit(solution)/shard_map/ppermute | solution.py:383
  69.7 54.8 %collective-permute-start.4 = (bf16[1,1536,256]{2,1,0:T(8,128)(2,1)S(1)}, bf16[1,1536,256]{2,1,0:T(8,128)(2,1)}, u32[]{:S(2)}, u32[]{:S(2)}) collective-permute-start(bf16[1,1536,256]{2,1,0:T(8,128)(2,1)S(1)} %copy-done.5), channel_id=1, source_target_pairs={{0,16},{2,18},{4,20},{6,22},{8,24},{10,26},{12,28},{14,30},{17,1},... | collective-permute-start | bytes 2359304 | tf_op jit(solution)/shard_map/ppermute | solution.py:385
  105.4 19.2 %copy-start.6 = (bf16[1,1536,256]{2,1,0:T(8,128)(2,1)}, bf16[1,1536,256]{2,1,0:T(8,128)(2,1)S(1)}, u32[]{:S(2)}) copy-start(bf16[1,1536,256]{2,1,0:T(8,128)(2,1)S(1)} %collective-permute-done.refs_1_) | copy-start | bytes 2359300
  105.4 19.2 %collective-permute-start.3 = (bf16[1,1536,256]{2,1,0:T(8,128)(2,1)S(1)}, bf16[1,1536,256]{2,1,0:T(8,128)(2,1)}, u32[]{:S(2)}, u32[]{:S(2)}) collective-permute-start(bf16[1,1536,256]{2,1,0:T(8,128)(2,1)S(1)} %collective-permute-done.refs_1_), channel_id=1, source_target_pairs={{0,16},{2,18},{4,20},{6,22},{8,24},{10,26},{12,28},{14,30},{17,1},... | collective-permute-start | bytes 2359304 | tf_op jit(solution)/shard_map/ppermute | solution.py:388
  113.8 10.8 %copy-start.7 = (bf16[1,1536,256]{2,1,0:T(8,128)(2,1)}, bf16[1,1536,256]{2,1,0:T(8,128)(2,1)S(1)}, u32[]{:S(2)}) copy-start(bf16[1,1536,256]{2,1,0:T(8,128)(2,1)S(1)} %collective-permute-done.1.refs_3_) | copy-start | bytes 2359300
  113.8 10.8 %collective-permute-start.5 = (bf16[1,1536,256]{2,1,0:T(8,128)(2,1)S(1)}, bf16[1,1536,256]{2,1,0:T(8,128)(2,1)}, u32[]{:S(2)}, u32[]{:S(2)}) collective-permute-start(bf16[1,1536,256]{2,1,0:T(8,128)(2,1)S(1)} %collective-permute-done.1.refs_3_), channel_id=1, source_target_pairs={{0,16},{2,18},{4,20},{6,22},{8,24},{10,26},{12,28},{14,30},{17,1},... | collective-permute-start | bytes 2359304 | tf_op jit(solution)/shard_map/ppermute | solution.py:388
  116.9 19.9 %collective-permute-start.7 = (bf16[1,256,1536]{2,1,0:T(8,128)(2,1)}, bf16[1,256,1536]{2,1,0:T(8,128)(2,1)}, u32[]{:S(2)}, u32[]{:S(2)}) collective-permute-start(bf16[1,256,1536]{2,1,0:T(8,128)(2,1)} %refs_0_.3), channel_id=1, source_target_pairs={{0,16},{2,18},{4,20},{6,22},{8,24},{10,26},{12,28},{14,30},{17,1},... | collective-permute-start | bytes 2359304 | tf_op jit(solution)/shard_map/ppermute | solution.py:385
  122.3 14.5 %collective-permute-start.8 = (bf16[1,256,1536]{2,1,0:T(8,128)(2,1)}, bf16[1,256,1536]{2,1,0:T(8,128)(2,1)}, u32[]{:S(2)}, u32[]{:S(2)}) collective-permute-start(bf16[1,256,1536]{2,1,0:T(8,128)(2,1)} %collective-permute-done.6.refs_1_), channel_id=1, source_target_pairs={{0,16},{2,18},{4,20},{6,22},{8,24},{10,26},{12,28},{14,30},{17,1},... | collective-permute-start | bytes 2359304 | tf_op jit(solution)/shard_map/ppermute | solution.py:388
  148.3 61.5 %all-to-all-start.2 = ((bf16[128,8,1536]{2,1,0:T(8,128)(2,1)}), bf16[128,8,1536]{2,1,0:T(8,128)(2,1)}, u32[]{:S(2)}, u32[]{:S(2)}) async-start(bf16[128,8,1536]{2,1,0:T(8,128)(2,1)} %bitcast.16), calls=%async_computation.2 | async-start | bytes 6291456 | tf_op jit(solution)/shard_map/all_to_all | solution.py:425
  158.8 49.4 %collective-permute-start.15 = (bf16[192,1536]{1,0:T(8,128)(2,1)}, bf16[192,1536]{1,0:T(8,128)(2,1)S(1)}, u32[]{:S(2)}, u32[]{:S(2)}) collective-permute-start(bf16[192,1536]{1,0:T(8,128)(2,1)} %refs_7_.1), channel_id=1, source_target_pairs={{0,4},{1,5},{2,6},{3,7},{4,8},{5,9},{6,10},{7,11},{8,12},{9,13},{1... | collective-permute-start | bytes 1769480 | tf_op jit(solution)/shard_map/ppermute | solution.py:432
  159.9 58.1 %collective-permute-start.17 = (bf16[192,1536]{1,0:T(8,128)(2,1)}, bf16[192,1536]{1,0:T(8,128)(2,1)}, u32[]{:S(2)}, u32[]{:S(2)}) collective-permute-start(bf16[192,1536]{1,0:T(8,128)(2,1)} %refs_7_.1), channel_id=1, source_target_pairs={{0,12},{1,13},{2,14},{3,15},{4,0},{5,1},{6,2},{7,3},{8,4},{9,5},{1... | collective-permute-start | bytes 1769480 | tf_op jit(solution)/shard_map/ppermute | solution.py:432
  209.7 12.8 %collective-permute-start.16 = (bf16[96,1536]{1,0:T(8,128)(2,1)}, bf16[96,1536]{1,0:T(8,128)(2,1)}, u32[]{:S(2)}, u32[]{:S(2)}) collective-permute-start(bf16[96,1536]{1,0:T(8,128)(2,1)} %slice.8), channel_id=1, source_target_pairs={{0,4},{1,5},{2,6},{3,7},{4,8},{5,9},{6,10},{7,11},{8,12},{9,13},{1... | collective-permute-start | bytes 884744 | tf_op jit(solution)/shard_map/ppermute | solution.py:432
  214.7 10.8 %collective-permute-start.9 = (bf16[64,1536]{1,0:T(8,128)(2,1)}, bf16[64,1536]{1,0:T(8,128)(2,1)S(1)}, u32[]{:S(2)}, u32[]{:S(2)}) collective-permute-start(bf16[64,1536]{1,0:T(8,128)(2,1)} %get-tuple-element.44), channel_id=1, source_target_pairs={{0,1},{1,2},{2,3},{3,0},{4,5},{5,6},{6,7},{7,4},{8,9},{9,10},{10,1... | collective-permute-start | bytes 589832 | tf_op jit(solution)/shard_map/ppermute | solution.py:432
  216.3 9.2 %collective-permute-start.12 = (bf16[64,1536]{1,0:T(8,128)(2,1)}, bf16[64,1536]{1,0:T(8,128)(2,1)S(1)}, u32[]{:S(2)}, u32[]{:S(2)}) collective-permute-start(bf16[64,1536]{1,0:T(8,128)(2,1)} %get-tuple-element.45), channel_id=1, source_target_pairs={{0,3},{1,0},{2,1},{3,2},{4,7},{5,4},{6,5},{7,6},{8,11},{9,8},{10,9... | collective-permute-start | bytes 589832 | tf_op jit(solution)/shard_map/ppermute | solution.py:432
  218.9 9.8 %collective-permute-start.18 = (bf16[96,1536]{1,0:T(8,128)(2,1)S(1)}, bf16[96,1536]{1,0:T(8,128)(2,1)S(1)}, u32[]{:S(2)}, u32[]{:S(2)}) collective-permute-start(bf16[96,1536]{1,0:T(8,128)(2,1)S(1)} %slice.9), channel_id=1, source_target_pairs={{0,12},{1,13},{2,14},{3,15},{4,0},{5,1},{6,2},{7,3},{8,4},{9,5},{1... | collective-permute-start | bytes 884744 | tf_op jit(solution)/shard_map/ppermute | solution.py:432
  222.3 9.1 %collective-permute-start.10 = (bf16[64,1536]{1,0:T(8,128)(2,1)}, bf16[64,1536]{1,0:T(8,128)(2,1)S(1)}, u32[]{:S(2)}, u32[]{:S(2)}) collective-permute-start(bf16[64,1536]{1,0:T(8,128)(2,1)} %get-tuple-element.45), channel_id=1, source_target_pairs={{0,1},{1,2},{2,3},{3,0},{4,5},{5,6},{6,7},{7,4},{8,9},{9,10},{10,1... | collective-permute-start | bytes 589832 | tf_op jit(solution)/shard_map/ppermute | solution.py:432
  222.6 8.8 %collective-permute-start.11 = (bf16[64,1536]{1,0:T(8,128)(2,1)}, bf16[64,1536]{1,0:T(8,128)(2,1)S(1)}, u32[]{:S(2)}, u32[]{:S(2)}) collective-permute-start(bf16[64,1536]{1,0:T(8,128)(2,1)} %get-tuple-element.44), channel_id=1, source_target_pairs={{0,3},{1,0},{2,1},{3,2},{4,7},{5,4},{6,5},{7,6},{8,11},{9,8},{10,9... | collective-permute-start | bytes 589832 | tf_op jit(solution)/shard_map/ppermute | solution.py:432
  225.5 8.1 %collective-permute-start.13 = (bf16[64,1536]{1,0:T(8,128)(2,1)S(1)}, bf16[64,1536]{1,0:T(8,128)(2,1)S(1)}, u32[]{:S(2)}, u32[]{:S(2)}) collective-permute-start(bf16[64,1536]{1,0:T(8,128)(2,1)S(1)} %collective-permute-done.9.refs_1_), channel_id=1, source_target_pairs={{0,1},{1,2},{2,3},{3,0},{4,5},{5,6},{6,7},{7,4},{8,9},{9,10},{10,1... | collective-permute-start | bytes 589832 | tf_op jit(solution)/shard_map/ppermute | solution.py:432
  225.5 8.1 %collective-permute-start.14 = (bf16[64,1536]{1,0:T(8,128)(2,1)S(1)}, bf16[64,1536]{1,0:T(8,128)(2,1)S(1)}, u32[]{:S(2)}, u32[]{:S(2)}) collective-permute-start(bf16[64,1536]{1,0:T(8,128)(2,1)S(1)} %collective-permute-done.12.refs_4_), channel_id=1, source_target_pairs={{0,3},{1,0},{2,1},{3,2},{4,7},{5,4},{6,5},{7,6},{8,11},{9,8},{10,9... | collective-permute-start | bytes 589832 | tf_op jit(solution)/shard_map/ppermute | solution.py:432
  233.6 1.1 copy-start.1
  239.7 15.2 %collective-permute-start.19 = (bf16[4,192,128]{2,1,0:T(8,128)(2,1)}, bf16[4,192,128]{2,1,0:T(8,128)(2,1)}, u32[]{:S(2)}, u32[]{:S(2)}) collective-permute-start(bf16[4,192,128]{2,1,0:T(8,128)(2,1)} %get-tuple-element.47), channel_id=1, source_target_pairs={{0,12},{1,13},{2,14},{3,15},{4,0},{5,1},{6,2},{7,3},{8,4},{9,5},{1... | collective-permute-start | bytes 589832 | tf_op jit(solution)/shard_map/ppermute | solution.py:432
  240.5 14.4 %collective-permute-start.20 = (bf16[4,192,128]{2,1,0:T(8,128)(2,1)}, bf16[4,192,128]{2,1,0:T(8,128)(2,1)}, u32[]{:S(2)}, u32[]{:S(2)}) collective-permute-start(bf16[4,192,128]{2,1,0:T(8,128)(2,1)} %get-tuple-element.48), channel_id=1, source_target_pairs={{0,8},{1,9},{2,10},{3,11},{4,12},{5,13},{6,14},{7,15},{8,0},{9,1},... | collective-permute-start | bytes 589832 | tf_op jit(solution)/shard_map/ppermute | solution.py:432
  240.6 14.3 %collective-permute-start.21 = (bf16[4,192,128]{2,1,0:T(8,128)(2,1)}, bf16[4,192,128]{2,1,0:T(8,128)(2,1)}, u32[]{:S(2)}, u32[]{:S(2)}) collective-permute-start(bf16[4,192,128]{2,1,0:T(8,128)(2,1)} %get-tuple-element.49), channel_id=1, source_target_pairs={{0,4},{1,5},{2,6},{3,7},{4,8},{5,9},{6,10},{7,11},{8,12},{9,13},{1... | collective-permute-start | bytes 589832 | tf_op jit(solution)/shard_map/ppermute | solution.py:432
  258.6 14.0 %all-to-all-start.3 = ((bf16[8,224,128]{2,1,0:T(8,128)(2,1)}), bf16[8,224,128]{2,1,0:T(8,128)(2,1)}, u32[]{:S(2)}, u32[]{:S(2)}) async-start(bf16[8,224,128]{2,1,0:T(8,128)(2,1)} %get-tuple-element.53), calls=%async_computation.3 | async-start | bytes 917504 | tf_op jit(solution)/shard_map/all_to_all | solution.py:573
  276.0 20.2 %all-to-all-start.4 = ((bf16[16,128,128]{2,1,0:T(8,128)(2,1)}), bf16[16,128,128]{2,1,0:T(8,128)(2,1)}, u32[]{:S(2)}, u32[]{:S(2)}) async-start(bf16[16,128,128]{2,1,0:T(8,128)(2,1)} %bitcast.19), calls=%async_computation.4 | async-start | bytes 1048576 | tf_op jit(solution)/shard_map/all_to_all | solution.py:608
  (4 other events, 3.4 us)

commit v5 on v4

--- a/solution.py
+++ b/solution.py
@@ -38,28 +38,17 @@
     return lax.dot_general(a, b, dims, precision=HIGHEST, preferred_element_type=F32)
 
 
-def slot_experts(rows, toks):
-    row = lax.broadcasted_iota(jnp.int32, (rows, toks), 0)
+def slot_experts(rows, toks, at=0):
+    row = lax.broadcasted_iota(jnp.int32, (rows, toks), 0) + at
     dev, slot = row >> 3, row & 7
     x, core, z, y = dev >> 5, (dev >> 4) & 1, (dev >> 2) & 3, dev & 3
     expert = (2 * x + (y & 1)) * 8 + 2 * z + (y >> 1)
     return expert, 2 * slot + core
 
 
-def send_chunks(sel, rows, out_ref, buf_ref, sem):
-    n = buf_ref.shape[1]
-    copies = []
-    for k in range(buf_ref.shape[0]):
-        buf_ref[k] = dot(sel[k * n : (k + 1) * n], rows, NN).astype(BF16)
-        copies.append(pltpu.make_async_copy(buf_ref.at[k], out_ref.at[pl.ds(k * n, n)], sem.at[k]))
-        copies[-1].start()
-    for c in copies:
-        c.wait()
-
-
-def select_kernel(ids_ref, rows_ref, sel_ref, out_ref, buf_ref, sem):
+def select_kernel(ids_ref, rows_ref, sel_ref, out_ref):
     slots, toks = sel_ref.shape
-    expert, rank = slot_experts(slots, toks)
+    expert, rank = slot_experts(slots, toks, pl.program_id(0) * slots)
     named = ids_ref[0:1, :] == expert
     for k in range(1, ids_ref.shape[0]):
         named = jnp.logical_or(named, ids_ref[k : k + 1, :] == expert)
@@ -73,10 +62,10 @@
     before = dot(named.astype(BF16), earlier.astype(BF16), NN)
     sel = jnp.where(before == rank.astype(F32), named, 0.0).astype(BF16)
     sel_ref[...] = sel
-    send_chunks(sel, rows_ref[...], out_ref, buf_ref, sem)
-
-
-def second_kernel(ids_ref, gates_ref, sel_ref, rows_ref, out_ref, mix_ref):
+    out_ref[...] = dot(sel, rows_ref[...], NN).astype(BF16)
+
+
+def second_kernel(ids_ref, gates_ref, sel_ref, rows_ref, out_ref, hi_ref, lo_ref):
     slots, toks = sel_ref.shape
     out_ref[...] = dot(sel_ref[...], rows_ref[...], NN).astype(BF16)
     expert, _ = slot_experts(slots, toks)
@@ -84,7 +73,9 @@
     for k in range(ids_ref.shape[0]):
         gate = jnp.where(ids_ref[k : k + 1, :] == expert, gates_ref[k : k + 1, :], gate)
     mix = (gate * sel_ref[...].astype(F32)).T
-    mix_ref[:toks, :], mix_ref[toks:, :] = split(mix)
+    hi, lo = split(mix)
+    hi_ref[...] = hi
+    lo_ref[...] = lo
 
 
 def copy_half(home_ref, own, far, targets, sem):
@@ -149,23 +140,25 @@
     out_ref[...] = dot(both, cat_buf[...], NN).astype(BF16)
 
 
-def combine_kernel(mix_ref, rows_ref, grad_ref, out_ref, first_ref, second_ref, buf_ref, sem):
-    n = buf_ref.shape[1]
-    copies = [
-        pltpu.make_async_copy(rows_ref.at[pl.ds(k * n, n)], buf_ref.at[k], sem.at[k]) for k in range(buf_ref.shape[0])
-    ]
-    for c in copies:
-        c.start()
-    total = None
-    for k, c in enumerate(copies):
-        c.wait()
-        part = dot(mix_ref[:, k * n : (k + 1) * n], buf_ref[k], NN)
-        total = part if total is None else total + part
-    toks = out_ref.shape[0]
-    resid = (grad_ref[...].astype(F32) + total[:toks] + total[toks:]).astype(BF16)
-    out_ref[...] = resid
-    first_ref[...] = resid[: toks // 2]
-    second_ref[...] = resid[toks // 2 :]
+def combine_kernel(hi_ref, lo_ref, rows_ref, grad_ref, out_ref, first_ref, second_ref, acc_ref):
+    rows = rows_ref[...]
+    part = dot(hi_ref[...], rows, NN) + dot(lo_ref[...], rows, NN)
+
+    @pl.when(pl.program_id(0) == 0)
+    def _():
+        acc_ref[...] = grad_ref[...].astype(F32) + part
+
+    @pl.when(pl.program_id(0) > 0)
+    def _():
+        acc_ref[...] = acc_ref[...] + part
+
+    @pl.when(pl.program_id(0) == pl.num_programs(0) - 1)
+    def _():
+        resid = acc_ref[...].astype(BF16)
+        out_ref[...] = resid
+        half = first_ref.shape[0]
+        first_ref[...] = resid[:half]
+        second_ref[...] = resid[half:]
 
 
 def project_kernel(y_ref, *refs):
@@ -400,21 +393,21 @@
         cost_estimate=cost(1e9, 9 << 20),
         name="expert_weights",
     )(home_flag, *own[:4], *far[:4])
+    strip = lambda columns: pl.BlockSpec((slots // 4, columns), lambda i: (i, 0))
     ids_t, gates_t = route_ids.T, route_gates.T
     sel, send_input = pl.pallas_call(
         select_kernel,
-        grid=(1,),
+        grid=(4,),
         in_specs=[whole(ids_t.shape), whole((toks, width))],
-        out_specs=(whole((slots, toks)), any_spec),
+        out_specs=(strip(toks), strip(width)),
         out_shape=(sds((slots, toks), BF16), sds((slots, width), BF16)),
-        scratch_shapes=[pltpu.VMEM((4, slots // 4, width), BF16), pltpu.SemaphoreType.DMA((4,))],
         compiler_params=params(),
         cost_estimate=cost(2 * slots * toks * width, 4 << 20),
         name="select_rows",
     )(ids_t, moe_input)
-    send_grad, mix = pl.pallas_call(
+    send_grad, mix_hi, mix_lo = pl.pallas_call(
         second_kernel,
-        out_shape=(sds((slots, width), BF16), sds((2 * toks, slots), BF16)),
+        out_shape=(sds((slots, width), BF16), sds((toks, slots), BF16), sds((toks, slots), BF16)),
         compiler_params=params(),
         cost_estimate=cost(2 * slots * toks * width, 4 << 20),
         name="select_grads",
@@ -493,15 +486,16 @@
 
     resid_grad, first, second = pl.pallas_call(
         combine_kernel,
-        grid=(1,),
-        in_specs=[whole((2 * toks, slots)), any_spec, whole((toks, width))],
+        grid=(2,),
+        in_specs=[pl.BlockSpec((toks, slots // 2), lambda i: (0, i))] * 2
+        + [pl.BlockSpec((slots // 2, width), lambda i: (i, 0)), whole((toks, width))],
         out_specs=(whole((toks, width)),) + (whole((toks // 2, width)),) * 2,
         out_shape=(sds((toks, width), BF16),) + (sds((toks // 2, width), BF16),) * 2,
-        scratch_shapes=[pltpu.VMEM((2, slots // 2, width), BF16), pltpu.SemaphoreType.DMA((2,))],
+        scratch_shapes=[pltpu.VMEM((toks, width), F32)],
         compiler_params=params(),
         cost_estimate=cost(4 * slots * toks * width, 4 << 20),
         name="combine_rows",
-    )(mix, returned, out_grad)
+    )(mix_hi, mix_lo, returned, out_grad)
     up_first = shift(first, 0, 1)
     dn_second = shift(second, 0, -1)
     up_second = shift(second, 0, 1)

time: 299 us -> 298 us (level)
  no operation moved by 1% of the time
where the time goes in v5:
time: 298 us; the launch traced here: 297 us
  waiting for transfers between devices  134 us (45%)
  starting transfers between devices  80.7 us (27%)
  Pallas kernels  73.6 us (25%)
  local copies, waits for them, and re-layouts  6.17 us (2%)
    ppermute x13, waiting for transfers between devices, shift(): return lax.ppermute(rows, 'head', pairs)  50.9 us
    ppermute x3, waiting for transfers between devices, shards(): y_halves.append(lax.ppermute(a, both, over_y))  39.3 us
    all_to_all x3, waiting for transfers between devices, exchange(): lax.all_to_all(shaped, both, split_axis=0, concat_axis=0, tiled=True)  35.9 us
    all_to_all x3, starting transfers between devices, exchange(): lax.all_to_all(shaped, both, split_axis=0, concat_axis=0, tiled=True)  28 us
    ppermute x13, starting transfers between devices, shift(): return lax.ppermute(rows, 'head', pairs)  18.3 us
    pallas_call x1, Pallas kernels, shards(): pl.pallas_call(prepare_kernel, grid=(blocks,), in_specs=[pl.BlockSpec((he...  13.1 us
    pallas_call x1, Pallas kernels, shards(): pl.pallas_call(back_kernel, grid=(slots // tile,), in_specs=[smem_spec, r...  11.5 us
    ppermute x3, starting transfers between devices, shards(): far_own.append(lax.ppermute(a, both, over_core))  11.4 us
  transfers between devices with their start and end apart: 27, of which 9 were waited for; matrix products, arithmetic and copies ran while one was open for 1% of the time, Pallas kernels for 16%

profile of v5, /device:TPU:0, one launch (start us, length us, event | category | flops | bytes accessed | tf_op | source)
XLA Modules:
  0.0 297.0 jit_solution(13223489607692358156)
XLA Ops:
  0.6 4.4 %select_rows.1 = (bf16[1024,128]{1,0:T(8,128)(2,1)}, bf16[1024,1536]{1,0:T(8,128)(2,1)}) custom-call(s32[6,128]{1,0:T(8,128)} %bitcast.21, bf16[128,1536]{1,0:T(8,128)(2,1)} %rows_ref.2), custom_call_target="tpu_custom_call" | custom-call | flops 402653184 | bytes 4194304 | tf_op jit(solution)/shard_map/select_rows/pallas_call | solution.py:398
  5.0 11.6 %all-to-all-start.1 = ((bf16[128,8,1536]{2,1,0:T(8,128)(2,1)}), bf16[128,8,1536]{2,1,0:T(8,128)(2,1)}, u32[]{:S(2)}, u32[]{:S(2)}) async-start(bf16[128,8,1536]{2,1,0:T(8,128)(2,1)} %bitcast.17), calls=%async_computation.1 | async-start | bytes 6291456 | tf_op jit(solution)/shard_map/all_to_all | solution.py:418
  16.6 4.2 %select_grads.1 = (bf16[1024,1536]{1,0:T(8,128)(2,1)}, bf16[128,1024]{1,0:T(8,128)(2,1)}, bf16[128,1024]{1,0:T(8,128)(2,1)}) custom-call(s32[6,128]{1,0:T(8,128)} %bitcast.22, f32[6,128]{1,0:T(8,128)} %bitcast.23, bf16[1024,128]{1,0:T(8,128)(2,1)} %get-tuple-element.38.sel_ref, bf16[128,1536]{1,0:T(8,128)(2,1)} %grad_ref.1), custom_call_target="tpu_custom_call" | custom-call | flops 402653184 | bytes 4194304 | tf_op jit(solution)/shard_map/select_grads/pallas_call | solution.py:408
  20.8 35.9 %all-to-all-done.1 = bf16[128,8,1536]{2,1,0:T(8,128)(2,1)} async-done(((bf16[128,8,1536]{2,1,0:T(8,128)(2,1)}), bf16[128,8,1536]{2,1,0:T(8,128)(2,1)}, u32[]{:S(2)}, u32[]{:S(2)}) %all-to-all-start.1) | async-done | bytes 3145760 | tf_op jit(solution)/shard_map/all_to_all | solution.py:418
  56.7 5.9 %all-to-all-start = ((bf16[128,8,1536]{2,1,0:T(8,128)(2,1)}), bf16[128,8,1536]{2,1,0:T(8,128)(2,1)}, u32[]{:S(2)}, u32[]{:S(2)}) async-start(bf16[128,8,1536]{2,1,0:T(8,128)(2,1)} %bitcast.15), calls=%async_computation | async-start | bytes 6291456 | tf_op jit(solution)/shard_map/all_to_all | solution.py:418
  65.2 3.3 %collective-permute-start.2 = (bf16[1,1536,256]{2,1,0:T(8,128)(2,1)S(1)}, bf16[1,1536,256]{2,1,0:T(8,128)(2,1)S(1)}, u32[]{:S(2)}, u32[]{:S(2)}) collective-permute-start(bf16[1,1536,256]{2,1,0:T(8,128)(2,1)S(1)} %copy-done.4), channel_id=1, source_target_pairs={{0,16},{2,18},{4,20},{6,22},{8,24},{10,26},{12,28},{14,30},{17,1},... | collective-permute-start | bytes 2359304 | tf_op jit(solution)/shard_map/ppermute | solution.py:378
  69.8 5.9 %collective-permute-start.4 = (bf16[1,1536,256]{2,1,0:T(8,128)(2,1)S(1)}, bf16[1,1536,256]{2,1,0:T(8,128)(2,1)}, u32[]{:S(2)}, u32[]{:S(2)}) collective-permute-start(bf16[1,1536,256]{2,1,0:T(8,128)(2,1)S(1)} %copy-done.5), channel_id=1, source_target_pairs={{0,16},{2,18},{4,20},{6,22},{8,24},{10,26},{12,28},{14,30},{17,1},... | collective-permute-start | bytes 2359304 | tf_op jit(solution)/shard_map/ppermute | solution.py:378
  75.7 29.8 %collective-permute-done.refs_1_ = bf16[1,1536,256]{2,1,0:T(8,128)(2,1)S(1)} collective-permute-done((bf16[1,1536,256]{2,1,0:T(8,128)(2,1)S(1)}, bf16[1,1536,256]{2,1,0:T(8,128)(2,1)S(1)}, u32[]{:S(2)}, u32[]{:S(2)}) %collective-permute-start) | collective-permute-done | bytes 786464 | tf_op jit(solution)/shard_map/ppermute | solution.py:376
  105.4 2.2 collective-permute-start.3
  107.6 6.2 %collective-permute-done.1.refs_3_ = bf16[1,1536,256]{2,1,0:T(8,128)(2,1)S(1)} collective-permute-done((bf16[1,1536,256]{2,1,0:T(8,128)(2,1)S(1)}, bf16[1,1536,256]{2,1,0:T(8,128)(2,1)S(1)}, u32[]{:S(2)}, u32[]{:S(2)}) %collective-permute-start.1) | collective-permute-done | bytes 786464 | tf_op jit(solution)/shard_map/ppermute | solution.py:376
  119.1 3.3 %collective-permute-done.6.refs_1_ = bf16[1,256,1536]{2,1,0:T(8,128)(2,1)} collective-permute-done((bf16[1,256,1536]{2,1,0:T(8,128)(2,1)}, bf16[1,256,1536]{2,1,0:T(8,128)(2,1)}, u32[]{:S(2)}, u32[]{:S(2)}) %collective-permute-start.6) | collective-permute-done | bytes 786464 | tf_op jit(solution)/shard_map/ppermute | solution.py:376
  122.4 2.2 collective-permute-start.8
  124.6 4.6 %expert_weights.1 = (bf16[1536,1024]{1,0:T(8,128)(2,1)}, bf16[1024,1536]{1,0:T(8,128)(2,1)}) custom-call(s32[1]{0:T(128)} %bitcast.2.home_ref, bf16[1,1536,256]{2,1,0:T(8,128)(2,1)} %refs_0_.2, bf16[1,1536,256]{2,1,0:T(8,128)(2,1)} %copy-done.6, bf16[1,1536,256]{2,1,0:T(8,128)(2,1)} %refs_2_.1, bf16[1,1536,256]{2,1,0:T(8,128)(2,1)} %copy-done.7, ...), custom_call_target="tpu_custom_call" | custom-call | flops 1000000000 | bytes 9437184 | tf_op jit(solution)/shard_map/expert_weights/pallas_call | solution.py:387
  129.2 7.6 %expert_acts.1.act_ref = f32[1024,1024]{1,0:T(8,128)} custom-call(bf16[1024,1536]{1,0:T(8,128)(2,1)} %bitcast.6.x_ref, bf16[1536,1024]{1,0:T(8,128)(2,1)} %get-tuple-element.43.w_ref), custom_call_target="tpu_custom_call" | custom-call | flops 3221225472 | bytes 10485760 | tf_op jit(solution)/shard_map/expert_acts/pallas_call | solution.py:459
  136.9 11.5 %expert_back.1 = bf16[1024,1536]{1,0:T(8,128)(2,1)} custom-call(s32[1]{0:T(128)} %bitcast.2.home_ref, bf16[1024,1536]{1,0:T(8,128)(2,1)} %bitcast.4.g_ref, f32[1024,1024]{1,0:T(8,128)} %expert_acts.1.act_ref, bf16[1024,1536]{1,0:T(8,128)(2,1)} %get-tuple-element.44.cat_ref, bf16[1,256,1536]{2,1,0:T(8,128)(2,1)} %refs_0_.3, ...), custom_call_target="tpu_custom_call" | custom-call | flops 4831838208 | bytes 14680064 | tf_op jit(solution)/shard_map/expert_back/pallas_call | solution.py:469
  148.3 10.5 %all-to-all-start.2 = ((bf16[128,8,1536]{2,1,0:T(8,128)(2,1)}), bf16[128,8,1536]{2,1,0:T(8,128)(2,1)}, u32[]{:S(2)}, u32[]{:S(2)}) async-start(bf16[128,8,1536]{2,1,0:T(8,128)(2,1)} %bitcast.16), calls=%async_computation.2 | async-start | bytes 6291456 | tf_op jit(solution)/shard_map/all_to_all | solution.py:418
  160.0 2.2 collective-permute-start.17
  162.2 46.0 %collective-permute-done.15.refs_8_ = bf16[192,1536]{1,0:T(8,128)(2,1)S(1)} collective-permute-done((bf16[192,1536]{1,0:T(8,128)(2,1)}, bf16[192,1536]{1,0:T(8,128)(2,1)S(1)}, u32[]{:S(2)}, u32[]{:S(2)}) %collective-permute-start.15) | collective-permute-done | bytes 589856 | tf_op jit(solution)/shard_map/ppermute | solution.py:425
  209.8 3.9 %combine_rows.1 = (bf16[128,1536]{1,0:T(8,128)(2,1)}, bf16[64,1536]{1,0:T(8,128)(2,1)}, bf16[64,1536]{1,0:T(8,128)(2,1)}) custom-call(bf16[128,1024]{1,0:T(8,128)(2,1)} %get-tuple-element.39.hi_ref, bf16[128,1024]{1,0:T(8,128)(2,1)} %get-tuple-element.40.lo_ref, bf16[1024,1536]{1,0:T(8,128)(2,1)} %bitcast.8.rows_ref, bf16[128,1536]{1,0:T(8,128)(2,1)} %grad_ref.1), custom_call_target="tpu_custom_call" | custom-call | flops 805306368 | bytes 4194304 | tf_op jit(solution)/shard_map/combine_rows/pallas_call | solution.py:487
  218.0 3.3 %collective-permute-start.18 = (bf16[96,1536]{1,0:T(8,128)(2,1)S(1)}, bf16[96,1536]{1,0:T(8,128)(2,1)S(1)}, u32[]{:S(2)}, u32[]{:S(2)}) collective-permute-start(bf16[96,1536]{1,0:T(8,128)(2,1)S(1)} %slice.9), channel_id=1, source_target_pairs={{0,12},{1,13},{2,14},{3,15},{4,0},{5,1},{6,2},{7,3},{8,4},{9,5},{1... | collective-permute-start | bytes 884744 | tf_op jit(solution)/shard_map/ppermute | solution.py:425
  221.6 2.9 collective-permute-start.11
  224.5 3.2 %collective-permute-start.14 = (bf16[64,1536]{1,0:T(8,128)(2,1)S(1)}, bf16[64,1536]{1,0:T(8,128)(2,1)S(1)}, u32[]{:S(2)}, u32[]{:S(2)}) collective-permute-start(bf16[64,1536]{1,0:T(8,128)(2,1)S(1)} %collective-permute-done.12.refs_4_), channel_id=1, source_target_pairs={{0,3},{1,0},{2,1},{3,2},{4,7},{5,4},{6,5},{7,6},{8,11},{9,8},{10,9... | collective-permute-start | bytes 589832 | tf_op jit(solution)/shard_map/ppermute | solution.py:425
  227.7 2.6 collective-permute-done.10.refs_2_
  234.6 3.4 %project_rows.1 = (bf16[4,192,128]{2,1,0:T(8,128)(2,1)S(1)}, bf16[4,192,128]{2,1,0:T(8,128)(2,1)}, bf16[4,192,128]{2,1,0:T(8,128)(2,1)}, bf16[4,192,128]{2,1,0:T(8,128)(2,1)}) custom-call(s32[1]{0:T(128)} %bitcast.11.y_ref, bf16[128,1536]{1,0:T(8,128)(2,1)S(1)} %copy-done.2, bf16[64,1536]{1,0:T(8,128)(2,1)S(1)} %collective-permute-done.9.refs_1_, ...), custom_call_target="tpu_custom_call" | custom-call | flops 1207959552 | bytes 7340032 | tf_op jit(solution)/shard_map/project_rows/pallas_call | solution.py:508
  240.8 13.1 %scan_prepare.1 = (bf16[8,3,256,256]{3,2,1,0:T(8,128)(2,1)}, bf16[8,3,256,256]{3,2,1,0:T(8,128)(2,1)}, f32[8,2048]{1,0:T(8,128)}, f32[8,2048]{1,0:T(8,128)}, f32...) custom-call(f32[3,2048]{1,0:T(4,128)} %d_ref.1, ...), custom_call_target="tpu_custom_call" | custom-call | flops 4000000000 | bytes 20971520 | tf_op jit(solution)/shard_map/scan_prepare/pallas_call | solution.py:442
  253.9 3.7 %scan_state.1 = (f32[8,192,128]{2,1,0:T(8,128)}, bf16[8,224,128]{2,1,0:T(8,128)(2,1)}, bf16[16,192,128]{2,1,0:T(8,128)(2,1)}) custom-call(s32[1]{0:T(128)} %bitcast.10.z_ref, bf16[4,192,128]{2,1,0:T(8,128)(2,1)} %copy-done.3, bf16[4,192,128]{2,1,0:T(8,128)(2,1)} %collective-permute-done.19.g1_ref, bf16[4,192,128]{2,1,0:T(8,128)(2,1)} %collective-permute-done.20.g2_ref, ...), custom_call_target="tpu_custom_call" | custom-call | flops 1000000000 | bytes 4194304 | tf_op jit(solution)/shard_map/scan_state/pallas_call | solution.py:542
  257.6 4.3 %all-to-all-start.3 = ((bf16[8,224,128]{2,1,0:T(8,128)(2,1)}), bf16[8,224,128]{2,1,0:T(8,128)(2,1)}, u32[]{:S(2)}, u32[]{:S(2)}) async-start(bf16[8,224,128]{2,1,0:T(8,128)(2,1)} %get-tuple-element.55), calls=%async_computation.3 | async-start | bytes 917504 | tf_op jit(solution)/shard_map/all_to_all | solution.py:567
  261.9 9.5 %scan_intra.1 = (f32[192,2048]{1,0:T(8,128)}, f32[2048,128]{1,0:T(8,128)}) custom-call(f32[3]{0:T(128)} %skip_ref.1, bf16[8,3,256,256]{3,2,1,0:T(8,128)(2,1)} %get-tuple-element.58.wh_ref, bf16[8,3,256,256]{3,2,1,0:T(8,128)(2,1)} %get-tuple-element.59.wl_ref, bf16[16,192,128]{2,1,0:T(8,128)(2,1)} %get-tuple-element.60.g_ref, ...), custom_call_target="tpu_custom_call" | custom-call | flops 4000000000 | bytes 16777216 | tf_op jit(solution)/shard_map/scan_intra/pallas_call | solution.py:574
  271.6 3.4 %scan_finish_b.1 = (bf16[2048,128]{1,0:T(8,128)(2,1)}, bf16[192,128]{1,0:T(8,128)(2,1)}, bf16[192,128]{1,0:T(8,128)(2,1)}) custom-call(s32[1]{0:T(128)} %bitcast.9.seq_ref, bf16[8,224,128]{2,1,0:T(8,128)(2,1)} %all-to-all-done.3.pay_ref, bf16[2048,192]{1,0:T(8,128)(2,1)} %get-tuple-element.56.th_ref, bf16[2048,192]{1,0:T(8,128)(2,1)} %get-tuple-element.57.tl_ref, ...), custom_call_target="tpu_custom_call" | custom-call | flops 400000000 | bytes 6291456 | tf_op jit(solution)/shard_map/scan_finish_b/pallas_call | solution.py:586
  275.0 8.2 %all-to-all-start.4 = ((bf16[16,128,128]{2,1,0:T(8,128)(2,1)}), bf16[16,128,128]{2,1,0:T(8,128)(2,1)}, u32[]{:S(2)}, u32[]{:S(2)}) async-start(bf16[16,128,128]{2,1,0:T(8,128)(2,1)} %bitcast.19), calls=%async_computation.4 | async-start | bytes 1048576 | tf_op jit(solution)/shard_map/all_to_all | solution.py:602
  283.2 4.4 %scan_finish_x.1 = f32[192,2048]{1,0:T(8,128)} custom-call(bf16[192,128]{1,0:T(8,128)(2,1)} %get-tuple-element.68.hi_ref, bf16[192,128]{1,0:T(8,128)(2,1)} %get-tuple-element.69.lo_ref, f32[8,2048]{1,0:T(8,128)} %get-tuple-element.70.tt_ref, f32[2048,128]{1,0:T(8,128)} %b_ref.5, f32[192,2048]{1,0:T(8,128)} %get-tuple-element.71.gx_ref), custom_call_target="tpu_custom_call" | custom-call | flops 400000000 | bytes 6291456 | tf_op jit(solution)/shard_map/scan_finish_x/pallas_call | solution.py:605
  287.6 7.7 %all-to-all-done.4 = bf16[16,128,128]{2,1,0:T(8,128)(2,1)} async-done(((bf16[16,128,128]{2,1,0:T(8,128)(2,1)}), bf16[16,128,128]{2,1,0:T(8,128)(2,1)}, u32[]{:S(2)}, u32[]{:S(2)}) %all-to-all-start.4) | async-done | bytes 524320 | tf_op jit(solution)/shard_map/all_to_all | solution.py:602
  (55 shorter events, 25.3 us)
Async XLA Ops:
  5.0 51.7 %all-to-all-start.1 = ((bf16[128,8,1536]{2,1,0:T(8,128)(2,1)}), bf16[128,8,1536]{2,1,0:T(8,128)(2,1)}, u32[]{:S(2)}, u32[]{:S(2)}) async-start(bf16[128,8,1536]{2,1,0:T(8,128)(2,1)} %bitcast.17), calls=%async_computation.1 | async-start | bytes 6291456 | tf_op jit(solution)/shard_map/all_to_all | solution.py:418
  56.7 5.9 %copy-start.4 = (bf16[1,1536,256]{2,1,0:T(8,128)(2,1)S(1)}, bf16[1,1536,256]{2,1,0:T(8,128)(2,1)}, u32[]{:S(2)}) copy-start(bf16[1,1536,256]{2,1,0:T(8,128)(2,1)} %refs_0_.2) | copy-start | bytes 2359300
  56.7 7.2 %copy-start.5 = (bf16[1,1536,256]{2,1,0:T(8,128)(2,1)S(1)}, bf16[1,1536,256]{2,1,0:T(8,128)(2,1)}, u32[]{:S(2)}) copy-start(bf16[1,1536,256]{2,1,0:T(8,128)(2,1)} %refs_2_.1) | copy-start | bytes 2359300
  56.7 80.2 %all-to-all-start = ((bf16[128,8,1536]{2,1,0:T(8,128)(2,1)}), bf16[128,8,1536]{2,1,0:T(8,128)(2,1)}, u32[]{:S(2)}, u32[]{:S(2)}) async-start(bf16[128,8,1536]{2,1,0:T(8,128)(2,1)} %bitcast.15), calls=%async_computation | async-start | bytes 6291456 | tf_op jit(solution)/shard_map/all_to_all | solution.py:418
  62.6 42.9 %collective-permute-start = (bf16[1,1536,256]{2,1,0:T(8,128)(2,1)S(1)}, bf16[1,1536,256]{2,1,0:T(8,128)(2,1)S(1)}, u32[]{:S(2)}, u32[]{:S(2)}) collective-permute-start(bf16[1,1536,256]{2,1,0:T(8,128)(2,1)S(1)} %copy-done.4), channel_id=1, source_target_pairs={{1,0},{3,2},{5,4},{7,6},{9,8},{11,10},{13,12},{15,14},{16,17},{18,... | collective-permute-start | bytes 2359304 | tf_op jit(solution)/shard_map/ppermute | solution.py:376
  63.9 50.0 %collective-permute-start.1 = (bf16[1,1536,256]{2,1,0:T(8,128)(2,1)S(1)}, bf16[1,1536,256]{2,1,0:T(8,128)(2,1)S(1)}, u32[]{:S(2)}, u32[]{:S(2)}) collective-permute-start(bf16[1,1536,256]{2,1,0:T(8,128)(2,1)S(1)} %copy-done.5), channel_id=1, source_target_pairs={{1,0},{3,2},{5,4},{7,6},{9,8},{11,10},{13,12},{15,14},{16,17},{18,... | collective-permute-start | bytes 2359304 | tf_op jit(solution)/shard_map/ppermute | solution.py:376
  65.2 50.9 %collective-permute-start.2 = (bf16[1,1536,256]{2,1,0:T(8,128)(2,1)S(1)}, bf16[1,1536,256]{2,1,0:T(8,128)(2,1)S(1)}, u32[]{:S(2)}, u32[]{:S(2)}) collective-permute-start(bf16[1,1536,256]{2,1,0:T(8,128)(2,1)S(1)} %copy-done.4), channel_id=1, source_target_pairs={{0,16},{2,18},{4,20},{6,22},{8,24},{10,26},{12,28},{14,30},{17,1},... | collective-permute-start | bytes 2359304 | tf_op jit(solution)/shard_map/ppermute | solution.py:378
  68.5 53.9 %collective-permute-start.6 = (bf16[1,256,1536]{2,1,0:T(8,128)(2,1)}, bf16[1,256,1536]{2,1,0:T(8,128)(2,1)}, u32[]{:S(2)}, u32[]{:S(2)}) collective-permute-start(bf16[1,256,1536]{2,1,0:T(8,128)(2,1)} %refs_0_.3), channel_id=1, source_target_pairs={{1,0},{3,2},{5,4},{7,6},{9,8},{11,10},{13,12},{15,14},{16,17},{18,... | collective-permute-start | bytes 2359304 | tf_op jit(solution)/shard_map/ppermute | solution.py:376
  69.8 54.8 %collective-permute-start.4 = (bf16[1,1536,256]{2,1,0:T(8,128)(2,1)S(1)}, bf16[1,1536,256]{2,1,0:T(8,128)(2,1)}, u32[]{:S(2)}, u32[]{:S(2)}) collective-permute-start(bf16[1,1536,256]{2,1,0:T(8,128)(2,1)S(1)} %copy-done.5), channel_id=1, source_target_pairs={{0,16},{2,18},{4,20},{6,22},{8,24},{10,26},{12,28},{14,30},{17,1},... | collective-permute-start | bytes 2359304 | tf_op jit(solution)/shard_map/ppermute | solution.py:378
  105.4 19.2 %copy-start.6 = (bf16[1,1536,256]{2,1,0:T(8,128)(2,1)}, bf16[1,1536,256]{2,1,0:T(8,128)(2,1)S(1)}, u32[]{:S(2)}) copy-start(bf16[1,1536,256]{2,1,0:T(8,128)(2,1)S(1)} %collective-permute-done.refs_1_) | copy-start | bytes 2359300
  105.4 19.2 %collective-permute-start.3 = (bf16[1,1536,256]{2,1,0:T(8,128)(2,1)S(1)}, bf16[1,1536,256]{2,1,0:T(8,128)(2,1)}, u32[]{:S(2)}, u32[]{:S(2)}) collective-permute-start(bf16[1,1536,256]{2,1,0:T(8,128)(2,1)S(1)} %collective-permute-done.refs_1_), channel_id=1, source_target_pairs={{0,16},{2,18},{4,20},{6,22},{8,24},{10,26},{12,28},{14,30},{17,1},... | collective-permute-start | bytes 2359304 | tf_op jit(solution)/shard_map/ppermute | solution.py:381
  113.9 10.8 %copy-start.7 = (bf16[1,1536,256]{2,1,0:T(8,128)(2,1)}, bf16[1,1536,256]{2,1,0:T(8,128)(2,1)S(1)}, u32[]{:S(2)}) copy-start(bf16[1,1536,256]{2,1,0:T(8,128)(2,1)S(1)} %collective-permute-done.1.refs_3_) | copy-start | bytes 2359300
  113.9 10.8 %collective-permute-start.5 = (bf16[1,1536,256]{2,1,0:T(8,128)(2,1)S(1)}, bf16[1,1536,256]{2,1,0:T(8,128)(2,1)}, u32[]{:S(2)}, u32[]{:S(2)}) collective-permute-start(bf16[1,1536,256]{2,1,0:T(8,128)(2,1)S(1)} %collective-permute-done.1.refs_3_), channel_id=1, source_target_pairs={{0,16},{2,18},{4,20},{6,22},{8,24},{10,26},{12,28},{14,30},{17,1},... | collective-permute-start | bytes 2359304 | tf_op jit(solution)/shard_map/ppermute | solution.py:381
  116.9 19.9 %collective-permute-start.7 = (bf16[1,256,1536]{2,1,0:T(8,128)(2,1)}, bf16[1,256,1536]{2,1,0:T(8,128)(2,1)}, u32[]{:S(2)}, u32[]{:S(2)}) collective-permute-start(bf16[1,256,1536]{2,1,0:T(8,128)(2,1)} %refs_0_.3), channel_id=1, source_target_pairs={{0,16},{2,18},{4,20},{6,22},{8,24},{10,26},{12,28},{14,30},{17,1},... | collective-permute-start | bytes 2359304 | tf_op jit(solution)/shard_map/ppermute | solution.py:378
  122.4 14.5 %collective-permute-start.8 = (bf16[1,256,1536]{2,1,0:T(8,128)(2,1)}, bf16[1,256,1536]{2,1,0:T(8,128)(2,1)}, u32[]{:S(2)}, u32[]{:S(2)}) collective-permute-start(bf16[1,256,1536]{2,1,0:T(8,128)(2,1)} %collective-permute-done.6.refs_1_), channel_id=1, source_target_pairs={{0,16},{2,18},{4,20},{6,22},{8,24},{10,26},{12,28},{14,30},{17,1},... | collective-permute-start | bytes 2359304 | tf_op jit(solution)/shard_map/ppermute | solution.py:381
  148.3 61.5 %all-to-all-start.2 = ((bf16[128,8,1536]{2,1,0:T(8,128)(2,1)}), bf16[128,8,1536]{2,1,0:T(8,128)(2,1)}, u32[]{:S(2)}, u32[]{:S(2)}) async-start(bf16[128,8,1536]{2,1,0:T(8,128)(2,1)} %bitcast.16), calls=%async_computation.2 | async-start | bytes 6291456 | tf_op jit(solution)/shard_map/all_to_all | solution.py:418
  158.9 49.4 %collective-permute-start.15 = (bf16[192,1536]{1,0:T(8,128)(2,1)}, bf16[192,1536]{1,0:T(8,128)(2,1)S(1)}, u32[]{:S(2)}, u32[]{:S(2)}) collective-permute-start(bf16[192,1536]{1,0:T(8,128)(2,1)} %refs_7_.1), channel_id=1, source_target_pairs={{0,4},{1,5},{2,6},{3,7},{4,8},{5,9},{6,10},{7,11},{8,12},{9,13},{1... | collective-permute-start | bytes 1769480 | tf_op jit(solution)/shard_map/ppermute | solution.py:425
  160.0 57.0 %collective-permute-start.17 = (bf16[192,1536]{1,0:T(8,128)(2,1)}, bf16[192,1536]{1,0:T(8,128)(2,1)}, u32[]{:S(2)}, u32[]{:S(2)}) collective-permute-start(bf16[192,1536]{1,0:T(8,128)(2,1)} %refs_7_.1), channel_id=1, source_target_pairs={{0,12},{1,13},{2,14},{3,15},{4,0},{5,1},{6,2},{7,3},{8,4},{9,5},{1... | collective-permute-start | bytes 1769480 | tf_op jit(solution)/shard_map/ppermute | solution.py:425
  209.8 11.8 %collective-permute-start.16 = (bf16[96,1536]{1,0:T(8,128)(2,1)}, bf16[96,1536]{1,0:T(8,128)(2,1)}, u32[]{:S(2)}, u32[]{:S(2)}) collective-permute-start(bf16[96,1536]{1,0:T(8,128)(2,1)} %slice.8), channel_id=1, source_target_pairs={{0,4},{1,5},{2,6},{3,7},{4,8},{5,9},{6,10},{7,11},{8,12},{9,13},{1... | collective-permute-start | bytes 884744 | tf_op jit(solution)/shard_map/ppermute | solution.py:425
  213.7 10.8 %collective-permute-start.9 = (bf16[64,1536]{1,0:T(8,128)(2,1)}, bf16[64,1536]{1,0:T(8,128)(2,1)S(1)}, u32[]{:S(2)}, u32[]{:S(2)}) collective-permute-start(bf16[64,1536]{1,0:T(8,128)(2,1)} %get-tuple-element.46), channel_id=1, source_target_pairs={{0,1},{1,2},{2,3},{3,0},{4,5},{5,6},{6,7},{7,4},{8,9},{9,10},{10,1... | collective-permute-start | bytes 589832 | tf_op jit(solution)/shard_map/ppermute | solution.py:425
  215.3 9.2 %collective-permute-start.12 = (bf16[64,1536]{1,0:T(8,128)(2,1)}, bf16[64,1536]{1,0:T(8,128)(2,1)S(1)}, u32[]{:S(2)}, u32[]{:S(2)}) collective-permute-start(bf16[64,1536]{1,0:T(8,128)(2,1)} %get-tuple-element.47), channel_id=1, source_target_pairs={{0,3},{1,0},{2,1},{3,2},{4,7},{5,4},{6,5},{7,6},{8,11},{9,8},{10,9... | collective-permute-start | bytes 589832 | tf_op jit(solution)/shard_map/ppermute | solution.py:425
  218.0 9.8 %collective-permute-start.18 = (bf16[96,1536]{1,0:T(8,128)(2,1)S(1)}, bf16[96,1536]{1,0:T(8,128)(2,1)S(1)}, u32[]{:S(2)}, u32[]{:S(2)}) collective-permute-start(bf16[96,1536]{1,0:T(8,128)(2,1)S(1)} %slice.9), channel_id=1, source_target_pairs={{0,12},{1,13},{2,14},{3,15},{4,0},{5,1},{6,2},{7,3},{8,4},{9,5},{1... | collective-permute-start | bytes 884744 | tf_op jit(solution)/shard_map/ppermute | solution.py:425
  221.3 9.1 %collective-permute-start.10 = (bf16[64,1536]{1,0:T(8,128)(2,1)}, bf16[64,1536]{1,0:T(8,128)(2,1)S(1)}, u32[]{:S(2)}, u32[]{:S(2)}) collective-permute-start(bf16[64,1536]{1,0:T(8,128)(2,1)} %get-tuple-element.47), channel_id=1, source_target_pairs={{0,1},{1,2},{2,3},{3,0},{4,5},{5,6},{6,7},{7,4},{8,9},{9,10},{10,1... | collective-permute-start | bytes 589832 | tf_op jit(solution)/shard_map/ppermute | solution.py:425
  221.6 8.8 %collective-permute-start.11 = (bf16[64,1536]{1,0:T(8,128)(2,1)}, bf16[64,1536]{1,0:T(8,128)(2,1)S(1)}, u32[]{:S(2)}, u32[]{:S(2)}) collective-permute-start(bf16[64,1536]{1,0:T(8,128)(2,1)} %get-tuple-element.46), channel_id=1, source_target_pairs={{0,3},{1,0},{2,1},{3,2},{4,7},{5,4},{6,5},{7,6},{8,11},{9,8},{10,9... | collective-permute-start | bytes 589832 | tf_op jit(solution)/shard_map/ppermute | solution.py:425
  224.5 8.1 %collective-permute-start.13 = (bf16[64,1536]{1,0:T(8,128)(2,1)S(1)}, bf16[64,1536]{1,0:T(8,128)(2,1)S(1)}, u32[]{:S(2)}, u32[]{:S(2)}) collective-permute-start(bf16[64,1536]{1,0:T(8,128)(2,1)S(1)} %collective-permute-done.9.refs_1_), channel_id=1, source_target_pairs={{0,1},{1,2},{2,3},{3,0},{4,5},{5,6},{6,7},{7,4},{8,9},{9,10},{10,1... | collective-permute-start | bytes 589832 | tf_op jit(solution)/shard_map/ppermute | solution.py:425
  224.5 8.1 %collective-permute-start.14 = (bf16[64,1536]{1,0:T(8,128)(2,1)S(1)}, bf16[64,1536]{1,0:T(8,128)(2,1)S(1)}, u32[]{:S(2)}, u32[]{:S(2)}) collective-permute-start(bf16[64,1536]{1,0:T(8,128)(2,1)S(1)} %collective-permute-done.12.refs_4_), channel_id=1, source_target_pairs={{0,3},{1,0},{2,1},{3,2},{4,7},{5,4},{6,5},{7,6},{8,11},{9,8},{10,9... | collective-permute-start | bytes 589832 | tf_op jit(solution)/shard_map/ppermute | solution.py:425
  232.6 1.1 copy-start.1
  238.7 15.2 %collective-permute-start.19 = (bf16[4,192,128]{2,1,0:T(8,128)(2,1)}, bf16[4,192,128]{2,1,0:T(8,128)(2,1)}, u32[]{:S(2)}, u32[]{:S(2)}) collective-permute-start(bf16[4,192,128]{2,1,0:T(8,128)(2,1)} %get-tuple-element.49), channel_id=1, source_target_pairs={{0,12},{1,13},{2,14},{3,15},{4,0},{5,1},{6,2},{7,3},{8,4},{9,5},{1... | collective-permute-start | bytes 589832 | tf_op jit(solution)/shard_map/ppermute | solution.py:425
  239.5 14.4 %collective-permute-start.20 = (bf16[4,192,128]{2,1,0:T(8,128)(2,1)}, bf16[4,192,128]{2,1,0:T(8,128)(2,1)}, u32[]{:S(2)}, u32[]{:S(2)}) collective-permute-start(bf16[4,192,128]{2,1,0:T(8,128)(2,1)} %get-tuple-element.50), channel_id=1, source_target_pairs={{0,8},{1,9},{2,10},{3,11},{4,12},{5,13},{6,14},{7,15},{8,0},{9,1},... | collective-permute-start | bytes 589832 | tf_op jit(solution)/shard_map/ppermute | solution.py:425
  239.6 14.3 %collective-permute-start.21 = (bf16[4,192,128]{2,1,0:T(8,128)(2,1)}, bf16[4,192,128]{2,1,0:T(8,128)(2,1)}, u32[]{:S(2)}, u32[]{:S(2)}) collective-permute-start(bf16[4,192,128]{2,1,0:T(8,128)(2,1)} %get-tuple-element.51), channel_id=1, source_target_pairs={{0,4},{1,5},{2,6},{3,7},{4,8},{5,9},{6,10},{7,11},{8,12},{9,13},{1... | collective-permute-start | bytes 589832 | tf_op jit(solution)/shard_map/ppermute | solution.py:425
  257.6 14.0 %all-to-all-start.3 = ((bf16[8,224,128]{2,1,0:T(8,128)(2,1)}), bf16[8,224,128]{2,1,0:T(8,128)(2,1)}, u32[]{:S(2)}, u32[]{:S(2)}) async-start(bf16[8,224,128]{2,1,0:T(8,128)(2,1)} %get-tuple-element.55), calls=%async_computation.3 | async-start | bytes 917504 | tf_op jit(solution)/shard_map/all_to_all | solution.py:567
  275.0 20.2 %all-to-all-start.4 = ((bf16[16,128,128]{2,1,0:T(8,128)(2,1)}), bf16[16,128,128]{2,1,0:T(8,128)(2,1)}, u32[]{:S(2)}, u32[]{:S(2)}) async-start(bf16[16,128,128]{2,1,0:T(8,128)(2,1)} %bitcast.19), calls=%async_computation.4 | async-start | bytes 1048576 | tf_op jit(solution)/shard_map/all_to_all | solution.py:602
  (4 other events, 3.4 us)

commit v6 on v5

--- a/solution.py
+++ b/solution.py
@@ -38,8 +38,8 @@
     return lax.dot_general(a, b, dims, precision=HIGHEST, preferred_element_type=F32)
 
 
-def slot_experts(rows, toks, at=0):
-    row = lax.broadcasted_iota(jnp.int32, (rows, toks), 0) + at
+def slot_experts(rows, toks):
+    row = lax.broadcasted_iota(jnp.int32, (rows, toks), 0)
     dev, slot = row >> 3, row & 7
     x, core, z, y = dev >> 5, (dev >> 4) & 1, (dev >> 2) & 3, dev & 3
     expert = (2 * x + (y & 1)) * 8 + 2 * z + (y >> 1)
@@ -48,7 +48,7 @@
 
 def select_kernel(ids_ref, rows_ref, sel_ref, out_ref):
     slots, toks = sel_ref.shape
-    expert, rank = slot_experts(slots, toks, pl.program_id(0) * slots)
+    expert, rank = slot_experts(slots, toks)
     named = ids_ref[0:1, :] == expert
     for k in range(1, ids_ref.shape[0]):
         named = jnp.logical_or(named, ids_ref[k : k + 1, :] == expert)
@@ -393,13 +393,9 @@
         cost_estimate=cost(1e9, 9 << 20),
         name="expert_weights",
     )(home_flag, *own[:4], *far[:4])
-    strip = lambda columns: pl.BlockSpec((slots // 4, columns), lambda i: (i, 0))
     ids_t, gates_t = route_ids.T, route_gates.T
     sel, send_input = pl.pallas_call(
         select_kernel,
-        grid=(4,),
-        in_specs=[whole(ids_t.shape), whole((toks, width))],
-        out_specs=(strip(toks), strip(width)),
         out_shape=(sds((slots, toks), BF16), sds((slots, width), BF16)),
         compiler_params=params(),
         cost_estimate=cost(2 * slots * toks * width, 4 << 20),
@@ -516,7 +512,7 @@
             pltpu.VMEM((4 * inner, width), BF16),
             pltpu.SemaphoreType.DMA((5,)),
         ],
-        compiler_params=params(24 << 20),
+        compiler_params=params(54000000),
         cost_estimate=cost(32 * inner * toks * width, 7 << 20),
         name="project_rows",
     )(
@@ -560,7 +556,7 @@
             whole((n_seq, pay_rows, state)),
             whole((n_head, inner, toks)),
         ),
-        compiler_params=params(66000000),
+        compiler_params=params(55500000),
         cost_estimate=cost(1e9, 4 << 20),
         name="scan_state",
     )((head >> 2).reshape(1), to_0, from_1, from_2, from_3, c_proj, to_start, block_sum, total)

time: 298 us -> 300 us (level)
  no operation moved by 1% of the time
where the time goes in v6:
time: 300 us; the launch traced here: 299 us
  waiting for transfers between devices  134 us (45%)
  starting transfers between devices  80.7 us (27%)
  Pallas kernels  74.3 us (25%)
  local copies, waits for them, and re-layouts  7.33 us (2%)
    ppermute x13, waiting for transfers between devices, shift(): return lax.ppermute(rows, 'head', pairs)  50.9 us
    ppermute x3, waiting for transfers between devices, shards(): y_halves.append(lax.ppermute(a, both, over_y))  39.3 us
    all_to_all x3, waiting for transfers between devices, exchange(): lax.all_to_all(shaped, both, split_axis=0, concat_axis=0, tiled=True)  35.9 us
    all_to_all x3, starting transfers between devices, exchange(): lax.all_to_all(shaped, both, split_axis=0, concat_axis=0, tiled=True)  28 us
    ppermute x13, starting transfers between devices, shift(): return lax.ppermute(rows, 'head', pairs)  18.3 us
    pallas_call x1, Pallas kernels, shards(): pl.pallas_call(prepare_kernel, grid=(blocks,), in_specs=[pl.BlockSpec((he...  13.1 us
    pallas_call x1, Pallas kernels, shards(): pl.pallas_call(back_kernel, grid=(slots // tile,), in_specs=[smem_spec, r...  11.5 us
    ppermute x3, starting transfers between devices, shards(): far_own.append(lax.ppermute(a, both, over_core))  11.4 us
  transfers between devices with their start and end apart: 27, of which 9 were waited for; matrix products, arithmetic and copies ran while one was open for 1% of the time, Pallas kernels for 16%

profile of v6, /device:TPU:0, one launch (start us, length us, event | category | flops | bytes accessed | tf_op | source)
XLA Modules:
  0.0 298.9 jit_solution(11806978477293835992)
XLA Ops:
  0.6 4.0 %select_rows.1 = (bf16[1024,128]{1,0:T(8,128)(2,1)}, bf16[1024,1536]{1,0:T(8,128)(2,1)}) custom-call(s32[6,128]{1,0:T(8,128)} %bitcast.21, bf16[128,1536]{1,0:T(8,128)(2,1)} %rows_ref.2), custom_call_target="tpu_custom_call" | custom-call | flops 402653184 | bytes 4194304 | tf_op jit(solution)/shard_map/select_rows/pallas_call | solution.py:397
  4.7 11.6 %all-to-all-start.1 = ((bf16[128,8,1536]{2,1,0:T(8,128)(2,1)}), bf16[128,8,1536]{2,1,0:T(8,128)(2,1)}, u32[]{:S(2)}, u32[]{:S(2)}) async-start(bf16[128,8,1536]{2,1,0:T(8,128)(2,1)} %bitcast.17), calls=%async_computation.1 | async-start | bytes 6291456 | tf_op jit(solution)/shard_map/all_to_all | solution.py:414
  16.3 4.2 %select_grads.1 = (bf16[1024,1536]{1,0:T(8,128)(2,1)}, bf16[128,1024]{1,0:T(8,128)(2,1)}, bf16[128,1024]{1,0:T(8,128)(2,1)}) custom-call(s32[6,128]{1,0:T(8,128)} %bitcast.22, f32[6,128]{1,0:T(8,128)} %bitcast.23, bf16[1024,128]{1,0:T(8,128)(2,1)} %get-tuple-element.38.sel_ref, bf16[128,1536]{1,0:T(8,128)(2,1)} %grad_ref.1), custom_call_target="tpu_custom_call" | custom-call | flops 402653184 | bytes 4194304 | tf_op jit(solution)/shard_map/select_grads/pallas_call | solution.py:404
  20.5 35.9 %all-to-all-done.1 = bf16[128,8,1536]{2,1,0:T(8,128)(2,1)} async-done(((bf16[128,8,1536]{2,1,0:T(8,128)(2,1)}), bf16[128,8,1536]{2,1,0:T(8,128)(2,1)}, u32[]{:S(2)}, u32[]{:S(2)}) %all-to-all-start.1) | async-done | bytes 3145760 | tf_op jit(solution)/shard_map/all_to_all | solution.py:414
  56.3 5.9 %all-to-all-start = ((bf16[128,8,1536]{2,1,0:T(8,128)(2,1)}), bf16[128,8,1536]{2,1,0:T(8,128)(2,1)}, u32[]{:S(2)}, u32[]{:S(2)}) async-start(bf16[128,8,1536]{2,1,0:T(8,128)(2,1)} %bitcast.15), calls=%async_computation | async-start | bytes 6291456 | tf_op jit(solution)/shard_map/all_to_all | solution.py:414
  64.8 3.3 %collective-permute-start.2 = (bf16[1,1536,256]{2,1,0:T(8,128)(2,1)S(1)}, bf16[1,1536,256]{2,1,0:T(8,128)(2,1)S(1)}, u32[]{:S(2)}, u32[]{:S(2)}) collective-permute-start(bf16[1,1536,256]{2,1,0:T(8,128)(2,1)S(1)} %copy-done.5), channel_id=1, source_target_pairs={{0,16},{2,18},{4,20},{6,22},{8,24},{10,26},{12,28},{14,30},{17,1},... | collective-permute-start | bytes 2359304 | tf_op jit(solution)/shard_map/ppermute | solution.py:378
  69.5 5.9 %collective-permute-start.4 = (bf16[1,1536,256]{2,1,0:T(8,128)(2,1)S(1)}, bf16[1,1536,256]{2,1,0:T(8,128)(2,1)}, u32[]{:S(2)}, u32[]{:S(2)}) collective-permute-start(bf16[1,1536,256]{2,1,0:T(8,128)(2,1)S(1)} %copy-done.6), channel_id=1, source_target_pairs={{0,16},{2,18},{4,20},{6,22},{8,24},{10,26},{12,28},{14,30},{17,1},... | collective-permute-start | bytes 2359304 | tf_op jit(solution)/shard_map/ppermute | solution.py:378
  75.3 29.7 %collective-permute-done.refs_1_ = bf16[1,1536,256]{2,1,0:T(8,128)(2,1)S(1)} collective-permute-done((bf16[1,1536,256]{2,1,0:T(8,128)(2,1)S(1)}, bf16[1,1536,256]{2,1,0:T(8,128)(2,1)S(1)}, u32[]{:S(2)}, u32[]{:S(2)}) %collective-permute-start) | collective-permute-done | bytes 786464 | tf_op jit(solution)/shard_map/ppermute | solution.py:376
  105.1 2.2 collective-permute-start.3
  107.3 6.2 %collective-permute-done.1.refs_3_ = bf16[1,1536,256]{2,1,0:T(8,128)(2,1)S(1)} collective-permute-done((bf16[1,1536,256]{2,1,0:T(8,128)(2,1)S(1)}, bf16[1,1536,256]{2,1,0:T(8,128)(2,1)S(1)}, u32[]{:S(2)}, u32[]{:S(2)}) %collective-permute-start.1) | collective-permute-done | bytes 786464 | tf_op jit(solution)/shard_map/ppermute | solution.py:376
  118.8 3.3 %collective-permute-done.6.refs_1_ = bf16[1,256,1536]{2,1,0:T(8,128)(2,1)} collective-permute-done((bf16[1,256,1536]{2,1,0:T(8,128)(2,1)}, bf16[1,256,1536]{2,1,0:T(8,128)(2,1)}, u32[]{:S(2)}, u32[]{:S(2)}) %collective-permute-start.6) | collective-permute-done | bytes 786464 | tf_op jit(solution)/shard_map/ppermute | solution.py:376
  122.1 2.2 collective-permute-start.8
  124.3 4.6 %expert_weights.1 = (bf16[1536,1024]{1,0:T(8,128)(2,1)}, bf16[1024,1536]{1,0:T(8,128)(2,1)}) custom-call(s32[1]{0:T(128)} %bitcast.2.home_ref, bf16[1,1536,256]{2,1,0:T(8,128)(2,1)} %refs_0_.2, bf16[1,1536,256]{2,1,0:T(8,128)(2,1)} %copy-done.7, bf16[1,1536,256]{2,1,0:T(8,128)(2,1)} %refs_2_.1, bf16[1,1536,256]{2,1,0:T(8,128)(2,1)} %copy-done.8, ...), custom_call_target="tpu_custom_call" | custom-call | flops 1000000000 | bytes 9437184 | tf_op jit(solution)/shard_map/expert_weights/pallas_call | solution.py:387
  128.9 7.6 %expert_acts.1.act_ref = f32[1024,1024]{1,0:T(8,128)} custom-call(bf16[1024,1536]{1,0:T(8,128)(2,1)} %bitcast.6.x_ref, bf16[1536,1024]{1,0:T(8,128)(2,1)} %get-tuple-element.43.w_ref), custom_call_target="tpu_custom_call" | custom-call | flops 3221225472 | bytes 10485760 | tf_op jit(solution)/shard_map/expert_acts/pallas_call | solution.py:455
  136.5 11.5 %expert_back.1 = bf16[1024,1536]{1,0:T(8,128)(2,1)} custom-call(s32[1]{0:T(128)} %bitcast.2.home_ref, bf16[1024,1536]{1,0:T(8,128)(2,1)} %bitcast.4.g_ref, f32[1024,1024]{1,0:T(8,128)} %expert_acts.1.act_ref, bf16[1024,1536]{1,0:T(8,128)(2,1)} %get-tuple-element.44.cat_ref, bf16[1,256,1536]{2,1,0:T(8,128)(2,1)} %refs_0_.3, ...), custom_call_target="tpu_custom_call" | custom-call | flops 4831838208 | bytes 14680064 | tf_op jit(solution)/shard_map/expert_back/pallas_call | solution.py:465
  148.0 10.5 %all-to-all-start.2 = ((bf16[128,8,1536]{2,1,0:T(8,128)(2,1)}), bf16[128,8,1536]{2,1,0:T(8,128)(2,1)}, u32[]{:S(2)}, u32[]{:S(2)}) async-start(bf16[128,8,1536]{2,1,0:T(8,128)(2,1)} %bitcast.16), calls=%async_computation.2 | async-start | bytes 6291456 | tf_op jit(solution)/shard_map/all_to_all | solution.py:414
  159.6 2.2 collective-permute-start.17
  161.8 46.0 %collective-permute-done.15.refs_8_ = bf16[192,1536]{1,0:T(8,128)(2,1)S(1)} collective-permute-done((bf16[192,1536]{1,0:T(8,128)(2,1)}, bf16[192,1536]{1,0:T(8,128)(2,1)S(1)}, u32[]{:S(2)}, u32[]{:S(2)}) %collective-permute-start.15) | collective-permute-done | bytes 589856 | tf_op jit(solution)/shard_map/ppermute | solution.py:421
  209.5 3.9 %combine_rows.1 = (bf16[128,1536]{1,0:T(8,128)(2,1)}, bf16[64,1536]{1,0:T(8,128)(2,1)}, bf16[64,1536]{1,0:T(8,128)(2,1)}) custom-call(bf16[128,1024]{1,0:T(8,128)(2,1)} %get-tuple-element.39.hi_ref, bf16[128,1024]{1,0:T(8,128)(2,1)} %get-tuple-element.40.lo_ref, bf16[1024,1536]{1,0:T(8,128)(2,1)} %bitcast.8.rows_ref, bf16[128,1536]{1,0:T(8,128)(2,1)} %grad_ref.1), custom_call_target="tpu_custom_call" | custom-call | flops 805306368 | bytes 4194304 | tf_op jit(solution)/shard_map/combine_rows/pallas_call | solution.py:483
  217.6 3.3 %collective-permute-start.18 = (bf16[96,1536]{1,0:T(8,128)(2,1)S(1)}, bf16[96,1536]{1,0:T(8,128)(2,1)S(1)}, u32[]{:S(2)}, u32[]{:S(2)}) collective-permute-start(bf16[96,1536]{1,0:T(8,128)(2,1)S(1)} %slice.9), channel_id=1, source_target_pairs={{0,12},{1,13},{2,14},{3,15},{4,0},{5,1},{6,2},{7,3},{8,4},{9,5},{1... | collective-permute-start | bytes 884744 | tf_op jit(solution)/shard_map/ppermute | solution.py:421
  221.2 2.9 collective-permute-start.11
  224.2 3.2 %collective-permute-start.14 = (bf16[64,1536]{1,0:T(8,128)(2,1)S(1)}, bf16[64,1536]{1,0:T(8,128)(2,1)S(1)}, u32[]{:S(2)}, u32[]{:S(2)}) collective-permute-start(bf16[64,1536]{1,0:T(8,128)(2,1)S(1)} %collective-permute-done.12.refs_4_), channel_id=1, source_target_pairs={{0,3},{1,0},{2,1},{3,2},{4,7},{5,4},{6,5},{7,6},{8,11},{9,8},{10,9... | collective-permute-start | bytes 589832 | tf_op jit(solution)/shard_map/ppermute | solution.py:421
  227.4 2.6 collective-permute-done.10.refs_2_
  232.2 4.6 %project_rows.1 = (bf16[4,192,128]{2,1,0:T(8,128)(2,1)S(1)}, bf16[4,192,128]{2,1,0:T(8,128)(2,1)}, bf16[4,192,128]{2,1,0:T(8,128)(2,1)}, bf16[4,192,128]{2,1,0:T(8,128)(2,1)}) custom-call(s32[1]{0:T(128)} %bitcast.11.y_ref, bf16[128,1536]{1,0:T(8,128)(2,1)} %get-tuple-element.35.refs_0_, bf16[64,1536]{1,0:T(8,128)(2,1)S(1)} %collective-permute-done.9.refs_1_, ...), custom_call_target="tpu_custom_call" | custom-call | flops 1207959552 | bytes 7340032 | tf_op jit(solution)/shard_map/project_rows/pallas_call | solution.py:504
  239.5 13.1 %scan_prepare.1 = (bf16[8,3,256,256]{3,2,1,0:T(8,128)(2,1)}, bf16[8,3,256,256]{3,2,1,0:T(8,128)(2,1)}, f32[8,2048]{1,0:T(8,128)}, f32[8,2048]{1,0:T(8,128)}, f32...) custom-call(f32[3,2048]{1,0:T(4,128)} %d_ref.1, ...), custom_call_target="tpu_custom_call" | custom-call | flops 4000000000 | bytes 20971520 | tf_op jit(solution)/shard_map/scan_prepare/pallas_call | solution.py:438
  255.9 3.6 %scan_state.1 = (f32[8,192,128]{2,1,0:T(8,128)}, bf16[8,224,128]{2,1,0:T(8,128)(2,1)}, bf16[16,192,128]{2,1,0:T(8,128)(2,1)}) custom-call(s32[1]{0:T(128)} %bitcast.10.z_ref, bf16[4,192,128]{2,1,0:T(8,128)(2,1)S(1)} %copy-done.1, bf16[4,192,128]{2,1,0:T(8,128)(2,1)} %collective-permute-done.19.g1_ref, bf16[4,192,128]{2,1,0:T(8,128)(2,1)} %collective-permute-done.20.g2_ref, ...), custom_call_target="tpu_custom_call" | custom-call | flops 1000000000 | bytes 4194304 | tf_op jit(solution)/shard_map/scan_state/pallas_call | solution.py:538
  259.5 4.3 %all-to-all-start.3 = ((bf16[8,224,128]{2,1,0:T(8,128)(2,1)}), bf16[8,224,128]{2,1,0:T(8,128)(2,1)}, u32[]{:S(2)}, u32[]{:S(2)}) async-start(bf16[8,224,128]{2,1,0:T(8,128)(2,1)} %get-tuple-element.55), calls=%async_computation.3 | async-start | bytes 917504 | tf_op jit(solution)/shard_map/all_to_all | solution.py:563
  263.8 9.5 %scan_intra.1 = (f32[192,2048]{1,0:T(8,128)}, f32[2048,128]{1,0:T(8,128)}) custom-call(f32[3]{0:T(128)} %skip_ref.1, bf16[8,3,256,256]{3,2,1,0:T(8,128)(2,1)} %get-tuple-element.58.wh_ref, bf16[8,3,256,256]{3,2,1,0:T(8,128)(2,1)} %get-tuple-element.59.wl_ref, bf16[16,192,128]{2,1,0:T(8,128)(2,1)} %get-tuple-element.60.g_ref, ...), custom_call_target="tpu_custom_call" | custom-call | flops 4000000000 | bytes 16777216 | tf_op jit(solution)/shard_map/scan_intra/pallas_call | solution.py:570
  273.5 3.4 %scan_finish_b.1 = (bf16[2048,128]{1,0:T(8,128)(2,1)}, bf16[192,128]{1,0:T(8,128)(2,1)}, bf16[192,128]{1,0:T(8,128)(2,1)}) custom-call(s32[1]{0:T(128)} %bitcast.9.seq_ref, bf16[8,224,128]{2,1,0:T(8,128)(2,1)} %all-to-all-done.3.pay_ref, bf16[2048,192]{1,0:T(8,128)(2,1)} %get-tuple-element.56.th_ref, bf16[2048,192]{1,0:T(8,128)(2,1)} %get-tuple-element.57.tl_ref, ...), custom_call_target="tpu_custom_call" | custom-call | flops 400000000 | bytes 6291456 | tf_op jit(solution)/shard_map/scan_finish_b/pallas_call | solution.py:582
  276.9 8.2 %all-to-all-start.4 = ((bf16[16,128,128]{2,1,0:T(8,128)(2,1)}), bf16[16,128,128]{2,1,0:T(8,128)(2,1)}, u32[]{:S(2)}, u32[]{:S(2)}) async-start(bf16[16,128,128]{2,1,0:T(8,128)(2,1)} %bitcast.19), calls=%async_computation.4 | async-start | bytes 1048576 | tf_op jit(solution)/shard_map/all_to_all | solution.py:598
  285.1 4.4 %scan_finish_x.1 = f32[192,2048]{1,0:T(8,128)} custom-call(bf16[192,128]{1,0:T(8,128)(2,1)} %get-tuple-element.68.hi_ref, bf16[192,128]{1,0:T(8,128)(2,1)} %get-tuple-element.69.lo_ref, f32[8,2048]{1,0:T(8,128)} %get-tuple-element.70.tt_ref, f32[2048,128]{1,0:T(8,128)} %b_ref.5, f32[192,2048]{1,0:T(8,128)} %get-tuple-element.71.gx_ref), custom_call_target="tpu_custom_call" | custom-call | flops 400000000 | bytes 6291456 | tf_op jit(solution)/shard_map/scan_finish_x/pallas_call | solution.py:601
  289.5 7.6 %all-to-all-done.4 = bf16[16,128,128]{2,1,0:T(8,128)(2,1)} async-done(((bf16[16,128,128]{2,1,0:T(8,128)(2,1)}), bf16[16,128,128]{2,1,0:T(8,128)(2,1)}, u32[]{:S(2)}, u32[]{:S(2)}) %all-to-all-start.4) | async-done | bytes 524320 | tf_op jit(solution)/shard_map/all_to_all | solution.py:598
  (61 shorter events, 26.5 us)
Async XLA Ops:
  4.7 51.7 %all-to-all-start.1 = ((bf16[128,8,1536]{2,1,0:T(8,128)(2,1)}), bf16[128,8,1536]{2,1,0:T(8,128)(2,1)}, u32[]{:S(2)}, u32[]{:S(2)}) async-start(bf16[128,8,1536]{2,1,0:T(8,128)(2,1)} %bitcast.17), calls=%async_computation.1 | async-start | bytes 6291456 | tf_op jit(solution)/shard_map/all_to_all | solution.py:414
  56.3 5.9 %copy-start.5 = (bf16[1,1536,256]{2,1,0:T(8,128)(2,1)S(1)}, bf16[1,1536,256]{2,1,0:T(8,128)(2,1)}, u32[]{:S(2)}) copy-start(bf16[1,1536,256]{2,1,0:T(8,128)(2,1)} %refs_0_.2) | copy-start | bytes 2359300
  56.3 7.2 %copy-start.6 = (bf16[1,1536,256]{2,1,0:T(8,128)(2,1)S(1)}, bf16[1,1536,256]{2,1,0:T(8,128)(2,1)}, u32[]{:S(2)}) copy-start(bf16[1,1536,256]{2,1,0:T(8,128)(2,1)} %refs_2_.1) | copy-start | bytes 2359300
  56.3 80.2 %all-to-all-start = ((bf16[128,8,1536]{2,1,0:T(8,128)(2,1)}), bf16[128,8,1536]{2,1,0:T(8,128)(2,1)}, u32[]{:S(2)}, u32[]{:S(2)}) async-start(bf16[128,8,1536]{2,1,0:T(8,128)(2,1)} %bitcast.15), calls=%async_computation | async-start | bytes 6291456 | tf_op jit(solution)/shard_map/all_to_all | solution.py:414
  62.2 42.9 %collective-permute-start = (bf16[1,1536,256]{2,1,0:T(8,128)(2,1)S(1)}, bf16[1,1536,256]{2,1,0:T(8,128)(2,1)S(1)}, u32[]{:S(2)}, u32[]{:S(2)}) collective-permute-start(bf16[1,1536,256]{2,1,0:T(8,128)(2,1)S(1)} %copy-done.5), channel_id=1, source_target_pairs={{1,0},{3,2},{5,4},{7,6},{9,8},{11,10},{13,12},{15,14},{16,17},{18,... | collective-permute-start | bytes 2359304 | tf_op jit(solution)/shard_map/ppermute | solution.py:376
  63.5 50.0 %collective-permute-start.1 = (bf16[1,1536,256]{2,1,0:T(8,128)(2,1)S(1)}, bf16[1,1536,256]{2,1,0:T(8,128)(2,1)S(1)}, u32[]{:S(2)}, u32[]{:S(2)}) collective-permute-start(bf16[1,1536,256]{2,1,0:T(8,128)(2,1)S(1)} %copy-done.6), channel_id=1, source_target_pairs={{1,0},{3,2},{5,4},{7,6},{9,8},{11,10},{13,12},{15,14},{16,17},{18,... | collective-permute-start | bytes 2359304 | tf_op jit(solution)/shard_map/ppermute | solution.py:376
  64.8 50.9 %collective-permute-start.2 = (bf16[1,1536,256]{2,1,0:T(8,128)(2,1)S(1)}, bf16[1,1536,256]{2,1,0:T(8,128)(2,1)S(1)}, u32[]{:S(2)}, u32[]{:S(2)}) collective-permute-start(bf16[1,1536,256]{2,1,0:T(8,128)(2,1)S(1)} %copy-done.5), channel_id=1, source_target_pairs={{0,16},{2,18},{4,20},{6,22},{8,24},{10,26},{12,28},{14,30},{17,1},... | collective-permute-start | bytes 2359304 | tf_op jit(solution)/shard_map/ppermute | solution.py:378
  68.2 53.9 %collective-permute-start.6 = (bf16[1,256,1536]{2,1,0:T(8,128)(2,1)}, bf16[1,256,1536]{2,1,0:T(8,128)(2,1)}, u32[]{:S(2)}, u32[]{:S(2)}) collective-permute-start(bf16[1,256,1536]{2,1,0:T(8,128)(2,1)} %refs_0_.3), channel_id=1, source_target_pairs={{1,0},{3,2},{5,4},{7,6},{9,8},{11,10},{13,12},{15,14},{16,17},{18,... | collective-permute-start | bytes 2359304 | tf_op jit(solution)/shard_map/ppermute | solution.py:376
  69.5 54.8 %collective-permute-start.4 = (bf16[1,1536,256]{2,1,0:T(8,128)(2,1)S(1)}, bf16[1,1536,256]{2,1,0:T(8,128)(2,1)}, u32[]{:S(2)}, u32[]{:S(2)}) collective-permute-start(bf16[1,1536,256]{2,1,0:T(8,128)(2,1)S(1)} %copy-done.6), channel_id=1, source_target_pairs={{0,16},{2,18},{4,20},{6,22},{8,24},{10,26},{12,28},{14,30},{17,1},... | collective-permute-start | bytes 2359304 | tf_op jit(solution)/shard_map/ppermute | solution.py:378
  105.1 19.2 %copy-start.7 = (bf16[1,1536,256]{2,1,0:T(8,128)(2,1)}, bf16[1,1536,256]{2,1,0:T(8,128)(2,1)S(1)}, u32[]{:S(2)}) copy-start(bf16[1,1536,256]{2,1,0:T(8,128)(2,1)S(1)} %collective-permute-done.refs_1_) | copy-start | bytes 2359300
  105.1 19.2 %collective-permute-start.3 = (bf16[1,1536,256]{2,1,0:T(8,128)(2,1)S(1)}, bf16[1,1536,256]{2,1,0:T(8,128)(2,1)}, u32[]{:S(2)}, u32[]{:S(2)}) collective-permute-start(bf16[1,1536,256]{2,1,0:T(8,128)(2,1)S(1)} %collective-permute-done.refs_1_), channel_id=1, source_target_pairs={{0,16},{2,18},{4,20},{6,22},{8,24},{10,26},{12,28},{14,30},{17,1},... | collective-permute-start | bytes 2359304 | tf_op jit(solution)/shard_map/ppermute | solution.py:381
  113.5 10.8 %copy-start.8 = (bf16[1,1536,256]{2,1,0:T(8,128)(2,1)}, bf16[1,1536,256]{2,1,0:T(8,128)(2,1)S(1)}, u32[]{:S(2)}) copy-start(bf16[1,1536,256]{2,1,0:T(8,128)(2,1)S(1)} %collective-permute-done.1.refs_3_) | copy-start | bytes 2359300
  113.5 10.8 %collective-permute-start.5 = (bf16[1,1536,256]{2,1,0:T(8,128)(2,1)S(1)}, bf16[1,1536,256]{2,1,0:T(8,128)(2,1)}, u32[]{:S(2)}, u32[]{:S(2)}) collective-permute-start(bf16[1,1536,256]{2,1,0:T(8,128)(2,1)S(1)} %collective-permute-done.1.refs_3_), channel_id=1, source_target_pairs={{0,16},{2,18},{4,20},{6,22},{8,24},{10,26},{12,28},{14,30},{17,1},... | collective-permute-start | bytes 2359304 | tf_op jit(solution)/shard_map/ppermute | solution.py:381
  116.6 19.9 %collective-permute-start.7 = (bf16[1,256,1536]{2,1,0:T(8,128)(2,1)}, bf16[1,256,1536]{2,1,0:T(8,128)(2,1)}, u32[]{:S(2)}, u32[]{:S(2)}) collective-permute-start(bf16[1,256,1536]{2,1,0:T(8,128)(2,1)} %refs_0_.3), channel_id=1, source_target_pairs={{0,16},{2,18},{4,20},{6,22},{8,24},{10,26},{12,28},{14,30},{17,1},... | collective-permute-start | bytes 2359304 | tf_op jit(solution)/shard_map/ppermute | solution.py:378
  122.1 14.4 %collective-permute-start.8 = (bf16[1,256,1536]{2,1,0:T(8,128)(2,1)}, bf16[1,256,1536]{2,1,0:T(8,128)(2,1)}, u32[]{:S(2)}, u32[]{:S(2)}) collective-permute-start(bf16[1,256,1536]{2,1,0:T(8,128)(2,1)} %collective-permute-done.6.refs_1_), channel_id=1, source_target_pairs={{0,16},{2,18},{4,20},{6,22},{8,24},{10,26},{12,28},{14,30},{17,1},... | collective-permute-start | bytes 2359304 | tf_op jit(solution)/shard_map/ppermute | solution.py:381
  148.0 61.5 %all-to-all-start.2 = ((bf16[128,8,1536]{2,1,0:T(8,128)(2,1)}), bf16[128,8,1536]{2,1,0:T(8,128)(2,1)}, u32[]{:S(2)}, u32[]{:S(2)}) async-start(bf16[128,8,1536]{2,1,0:T(8,128)(2,1)} %bitcast.16), calls=%async_computation.2 | async-start | bytes 6291456 | tf_op jit(solution)/shard_map/all_to_all | solution.py:414
  158.5 49.4 %collective-permute-start.15 = (bf16[192,1536]{1,0:T(8,128)(2,1)}, bf16[192,1536]{1,0:T(8,128)(2,1)S(1)}, u32[]{:S(2)}, u32[]{:S(2)}) collective-permute-start(bf16[192,1536]{1,0:T(8,128)(2,1)} %refs_7_.1), channel_id=1, source_target_pairs={{0,4},{1,5},{2,6},{3,7},{4,8},{5,9},{6,10},{7,11},{8,12},{9,13},{1... | collective-permute-start | bytes 1769480 | tf_op jit(solution)/shard_map/ppermute | solution.py:421
  159.6 57.0 %collective-permute-start.17 = (bf16[192,1536]{1,0:T(8,128)(2,1)}, bf16[192,1536]{1,0:T(8,128)(2,1)}, u32[]{:S(2)}, u32[]{:S(2)}) collective-permute-start(bf16[192,1536]{1,0:T(8,128)(2,1)} %refs_7_.1), channel_id=1, source_target_pairs={{0,12},{1,13},{2,14},{3,15},{4,0},{5,1},{6,2},{7,3},{8,4},{9,5},{1... | collective-permute-start | bytes 1769480 | tf_op jit(solution)/shard_map/ppermute | solution.py:421
  209.5 11.8 %collective-permute-start.16 = (bf16[96,1536]{1,0:T(8,128)(2,1)}, bf16[96,1536]{1,0:T(8,128)(2,1)}, u32[]{:S(2)}, u32[]{:S(2)}) collective-permute-start(bf16[96,1536]{1,0:T(8,128)(2,1)} %slice.8), channel_id=1, source_target_pairs={{0,4},{1,5},{2,6},{3,7},{4,8},{5,9},{6,10},{7,11},{8,12},{9,13},{1... | collective-permute-start | bytes 884744 | tf_op jit(solution)/shard_map/ppermute | solution.py:421
  213.4 10.8 %collective-permute-start.9 = (bf16[64,1536]{1,0:T(8,128)(2,1)}, bf16[64,1536]{1,0:T(8,128)(2,1)S(1)}, u32[]{:S(2)}, u32[]{:S(2)}) collective-permute-start(bf16[64,1536]{1,0:T(8,128)(2,1)} %get-tuple-element.46), channel_id=1, source_target_pairs={{0,1},{1,2},{2,3},{3,0},{4,5},{5,6},{6,7},{7,4},{8,9},{9,10},{10,1... | collective-permute-start | bytes 589832 | tf_op jit(solution)/shard_map/ppermute | solution.py:421
  214.9 9.2 %collective-permute-start.12 = (bf16[64,1536]{1,0:T(8,128)(2,1)}, bf16[64,1536]{1,0:T(8,128)(2,1)S(1)}, u32[]{:S(2)}, u32[]{:S(2)}) collective-permute-start(bf16[64,1536]{1,0:T(8,128)(2,1)} %get-tuple-element.47), channel_id=1, source_target_pairs={{0,3},{1,0},{2,1},{3,2},{4,7},{5,4},{6,5},{7,6},{8,11},{9,8},{10,9... | collective-permute-start | bytes 589832 | tf_op jit(solution)/shard_map/ppermute | solution.py:421
  217.6 9.8 %collective-permute-start.18 = (bf16[96,1536]{1,0:T(8,128)(2,1)S(1)}, bf16[96,1536]{1,0:T(8,128)(2,1)S(1)}, u32[]{:S(2)}, u32[]{:S(2)}) collective-permute-start(bf16[96,1536]{1,0:T(8,128)(2,1)S(1)} %slice.9), channel_id=1, source_target_pairs={{0,12},{1,13},{2,14},{3,15},{4,0},{5,1},{6,2},{7,3},{8,4},{9,5},{1... | collective-permute-start | bytes 884744 | tf_op jit(solution)/shard_map/ppermute | solution.py:421
  220.9 9.1 %collective-permute-start.10 = (bf16[64,1536]{1,0:T(8,128)(2,1)}, bf16[64,1536]{1,0:T(8,128)(2,1)S(1)}, u32[]{:S(2)}, u32[]{:S(2)}) collective-permute-start(bf16[64,1536]{1,0:T(8,128)(2,1)} %get-tuple-element.47), channel_id=1, source_target_pairs={{0,1},{1,2},{2,3},{3,0},{4,5},{5,6},{6,7},{7,4},{8,9},{9,10},{10,1... | collective-permute-start | bytes 589832 | tf_op jit(solution)/shard_map/ppermute | solution.py:421
  221.2 8.8 %collective-permute-start.11 = (bf16[64,1536]{1,0:T(8,128)(2,1)}, bf16[64,1536]{1,0:T(8,128)(2,1)S(1)}, u32[]{:S(2)}, u32[]{:S(2)}) collective-permute-start(bf16[64,1536]{1,0:T(8,128)(2,1)} %get-tuple-element.46), channel_id=1, source_target_pairs={{0,3},{1,0},{2,1},{3,2},{4,7},{5,4},{6,5},{7,6},{8,11},{9,8},{10,9... | collective-permute-start | bytes 589832 | tf_op jit(solution)/shard_map/ppermute | solution.py:421
  224.2 8.1 %collective-permute-start.13 = (bf16[64,1536]{1,0:T(8,128)(2,1)S(1)}, bf16[64,1536]{1,0:T(8,128)(2,1)S(1)}, u32[]{:S(2)}, u32[]{:S(2)}) collective-permute-start(bf16[64,1536]{1,0:T(8,128)(2,1)S(1)} %collective-permute-done.9.refs_1_), channel_id=1, source_target_pairs={{0,1},{1,2},{2,3},{3,0},{4,5},{5,6},{6,7},{7,4},{8,9},{9,10},{10,1... | collective-permute-start | bytes 589832 | tf_op jit(solution)/shard_map/ppermute | solution.py:421
  224.2 8.1 %collective-permute-start.14 = (bf16[64,1536]{1,0:T(8,128)(2,1)S(1)}, bf16[64,1536]{1,0:T(8,128)(2,1)S(1)}, u32[]{:S(2)}, u32[]{:S(2)}) collective-permute-start(bf16[64,1536]{1,0:T(8,128)(2,1)S(1)} %collective-permute-done.12.refs_4_), channel_id=1, source_target_pairs={{0,3},{1,0},{2,1},{3,2},{4,7},{5,4},{6,5},{7,6},{8,11},{9,8},{10,9... | collective-permute-start | bytes 589832 | tf_op jit(solution)/shard_map/ppermute | solution.py:421
  227.4 4.8 %copy-start.11 = (bf16[96,1536]{1,0:T(8,128)(2,1)}, bf16[96,1536]{1,0:T(8,128)(2,1)S(1)}, u32[]{:S(2)}) copy-start(bf16[96,1536]{1,0:T(8,128)(2,1)S(1)} %collective-permute-done.18.refs_10_) | copy-start | bytes 884740
  237.5 15.2 %collective-permute-start.19 = (bf16[4,192,128]{2,1,0:T(8,128)(2,1)}, bf16[4,192,128]{2,1,0:T(8,128)(2,1)}, u32[]{:S(2)}, u32[]{:S(2)}) collective-permute-start(bf16[4,192,128]{2,1,0:T(8,128)(2,1)} %get-tuple-element.49), channel_id=1, source_target_pairs={{0,12},{1,13},{2,14},{3,15},{4,0},{5,1},{6,2},{7,3},{8,4},{9,5},{1... | collective-permute-start | bytes 589832 | tf_op jit(solution)/shard_map/ppermute | solution.py:421
  238.3 14.4 %collective-permute-start.20 = (bf16[4,192,128]{2,1,0:T(8,128)(2,1)}, bf16[4,192,128]{2,1,0:T(8,128)(2,1)}, u32[]{:S(2)}, u32[]{:S(2)}) collective-permute-start(bf16[4,192,128]{2,1,0:T(8,128)(2,1)} %get-tuple-element.50), channel_id=1, source_target_pairs={{0,8},{1,9},{2,10},{3,11},{4,12},{5,13},{6,14},{7,15},{8,0},{9,1},... | collective-permute-start | bytes 589832 | tf_op jit(solution)/shard_map/ppermute | solution.py:421
  238.4 14.3 %collective-permute-start.21 = (bf16[4,192,128]{2,1,0:T(8,128)(2,1)}, bf16[4,192,128]{2,1,0:T(8,128)(2,1)}, u32[]{:S(2)}, u32[]{:S(2)}) collective-permute-start(bf16[4,192,128]{2,1,0:T(8,128)(2,1)} %get-tuple-element.51), channel_id=1, source_target_pairs={{0,4},{1,5},{2,6},{3,7},{4,8},{5,9},{6,10},{7,11},{8,12},{9,13},{1... | collective-permute-start | bytes 589832 | tf_op jit(solution)/shard_map/ppermute | solution.py:421
  259.5 14.0 %all-to-all-start.3 = ((bf16[8,224,128]{2,1,0:T(8,128)(2,1)}), bf16[8,224,128]{2,1,0:T(8,128)(2,1)}, u32[]{:S(2)}, u32[]{:S(2)}) async-start(bf16[8,224,128]{2,1,0:T(8,128)(2,1)} %get-tuple-element.55), calls=%async_computation.3 | async-start | bytes 917504 | tf_op jit(solution)/shard_map/all_to_all | solution.py:563
  276.9 20.2 %all-to-all-start.4 = ((bf16[16,128,128]{2,1,0:T(8,128)(2,1)}), bf16[16,128,128]{2,1,0:T(8,128)(2,1)}, u32[]{:S(2)}, u32[]{:S(2)}) async-start(bf16[16,128,128]{2,1,0:T(8,128)(2,1)} %bitcast.19), calls=%async_computation.4 | async-start | bytes 1048576 | tf_op jit(solution)/shard_map/all_to_all | solution.py:598
  (7 other events, 5.6 us)
